TPU v7x, 32 devices: a whole 2x2x4 slice. The times are simulated.
32 devices in a mesh: shard: 8 (over z, x), replica: 4 (over y, core).
Axes of the slice: x: 2, y: 2, z: 4, core: 2. Of those that a mesh axis runs over, the one named last changes fastest.
Arguments:
- inputs: bfloat16 [4, 1024, 1280], P('replica', 'shard'), may hold values from -6 to 6
- segment_ids: int32 [4, 1024], P('replica', 'shard'), may hold values from 0 to 4, as said below
- positions: int32 [4, 1024], P('replica', 'shard'), may hold values from 0 to 799, as said below
- gain_one: bfloat16 [1280], P('shard'), may hold values from 0.5 to 1.5
- w_qkv: bfloat16 [1280, 3840], P('shard'), may hold values from -0.15625 to 0.15625
- b_query: bfloat16 [1280], P('shard'), may hold values from -3 to 3
- b_value: bfloat16 [1280], P('shard'), may hold values from -3 to 3
- query_scale: bfloat16 [80], P('shard'), may hold values from -1 to 1
- w_out: bfloat16 [1280, 1280], P('shard'), may hold values from -0.625 to 0.625
- b_out: bfloat16 [1280], P('shard'), may hold values from -3 to 3
- gain_two: bfloat16 [1280], P('shard'), may hold values from 0.5 to 1.5
- w_up: bfloat16 [1280, 1280], P('shard'), may hold values from -0.15625 to 0.15625
- b_up: bfloat16 [1280], P('shard'), may hold values from -3 to 3
- w_down: bfloat16 [1280, 1280], P('shard'), may hold values from -0.15625 to 0.15625
- b_down: bfloat16 [1280], P('shard'), may hold values from -3 to 3
- cotangent: bfloat16 [4, 1024, 1280], P('replica', 'shard'), may hold values from -6 to 6
Outputs:
- output: bfloat16 [4, 1024, 1280], P('replica', 'shard')
- input_grad: float32 [4, 1024, 1280], P('replica', 'shard')
- grad_gain_one: float32 [1280], P('shard')
- grad_w_qkv: float32 [1280, 3840], P('shard')
- grad_b_query: float32 [1280], P('shard')
- grad_b_value: float32 [1280], P('shard')
- grad_query_scale: float32 [80], P('shard')
- grad_w_out: float32 [1280, 1280], P('shard')
- grad_b_out: float32 [1280], P('shard')
- grad_gain_two: float32 [1280], P('shard')
- grad_w_up: float32 [1280, 1280], P('shard')
- grad_b_up: float32 [1280], P('shard')
- grad_w_down: float32 [1280, 1280], P('shard')
- grad_b_down: float32 [1280], P('shard')
Inputs may be any that keep to these rules, and one draw needn't show every extreme that they name: `segment_ids`: along each sequence every document is one run of consecutive tokens, numbered 1, 2, 3, ... in order; the first document has 127 tokens, the second 800, each later one 60 to 800 except the last, which the padding or the sequence's end may cut short. Each sequence ends in 0 to min(64, 799) padding tokens of segment 0, which form one run. In the first sequence every document after the second has 60 tokens, save a last one cut short by the sequence's end, and there is no padding. `positions`: the place of each token within its run (a document, or the padding), counting from 0 at the run's first token.
All inputs are finite; a program needn't handle non-finite values.
Results may differ from a plain program's by a relative error of at most 0.011.
Values may be sent and summed in bfloat16 or wider, within the bound.
A program may use at most 192 MiB of HBM per device.

v0:
```python
import math

import jax
import jax.numpy as jnp
from jax import lax
from jax.sharding import PartitionSpec as P

HEADS = 16
HEAD = 80
DOC_MAX = 800


EPS = 1e-06
QUERY_BASE = 1.442695041
MASKED = -1000000000.0


def passed_along(shard, axis, by):
    peers = lax.axis_size(axis)
    pairs = [(i, i + by) for i in range(peers) if 0 <= i + by < peers]
    return lax.ppermute(shard, axis, pairs)


def norm_apply(rows_in, gain):
    scale = lax.rsqrt(jnp.mean(rows_in * rows_in, axis=-1, keepdims=True) + EPS)
    return rows_in * scale * gain


def scale_queries(query_rows, scale_raw):
    factor = QUERY_BASE / math.sqrt(HEAD) * jax.nn.softplus(scale_raw)
    count = query_rows.shape[0]
    return (query_rows.reshape(count, HEADS, HEAD) * factor).reshape(count, HEADS * HEAD)


def split_heads(array):
    group_count, length, width = array.shape
    return array.reshape(group_count, length, HEADS, width // HEADS)


def place_of(owner, block):
    return (owner * block + lax.iota(jnp.int32, block)).astype(jnp.float32)


def masked_scores(queries_h, keys_h, query_place, starts, key_place):
    raw = jnp.einsum("gqhe,gkhe->ghqk", queries_h, keys_h, preferred_element_type=jnp.float32)
    allowed = (key_place[None, None, :] >= starts[:, :, None]) & (
        key_place[None, None, :] <= query_place[None, :, None]
    )
    return jnp.where(allowed[:, None], raw, MASKED)


def probs_for(queries_h, starts, query_place, keys_low, key_place, log_total):
    scores = masked_scores(queries_h, split_heads(keys_low), query_place, starts, key_place)
    return jnp.exp(scores - log_total[..., None])


def value_grads(context_h, values_low):
    return jnp.einsum(
        "gqhe,gkhe->ghqk", context_h, split_heads(values_low), preferred_element_type=jnp.float32
    )


def on_device(
    inputs,
    segment_ids,
    positions,
    gain_one,
    w_qkv,
    b_query,
    b_value,
    query_scale,
    w_out,
    b_out,
    gain_two,
    w_up,
    b_up,
    w_down,
    b_down,
    cotangent,
):
    group_count, block, width = inputs.shape
    row_count = group_count * block
    shard_count = lax.axis_size("shard")
    shard_index = lax.axis_index("shard")
    reach = min((DOC_MAX + block - 2) // block, shard_count - 1)
    gathered = (
        lax.all_gather(gain_one, "shard", axis=0, tiled=True),
        lax.all_gather(w_qkv, "shard", axis=0, tiled=True),
        lax.all_gather(b_query, "shard", axis=0, tiled=True),
        lax.all_gather(b_value, "shard", axis=0, tiled=True),
        lax.all_gather(query_scale, "shard", axis=0, tiled=True),
        lax.all_gather(w_out, "shard", axis=0, tiled=True),
        lax.all_gather(b_out, "shard", axis=0, tiled=True),
        lax.all_gather(gain_two, "shard", axis=0, tiled=True),
        lax.all_gather(w_up, "shard", axis=0, tiled=True),
        lax.all_gather(b_up, "shard", axis=0, tiled=True),
        lax.all_gather(w_down, "shard", axis=0, tiled=True),
        lax.all_gather(b_down, "shard", axis=0, tiled=True),
    )
    gain_first = gathered[0].astype(jnp.float32)
    weight_qkv = gathered[1]
    bias_query = gathered[2].astype(jnp.float32)
    bias_value = gathered[3].astype(jnp.float32)
    scale_raw = gathered[4].astype(jnp.float32)
    weight_out = gathered[5]
    bias_out = gathered[6].astype(jnp.float32)
    gain_second = gathered[7].astype(jnp.float32)
    weight_up = gathered[8]
    bias_up = gathered[9].astype(jnp.float32)
    weight_down = gathered[10]
    bias_down = gathered[11].astype(jnp.float32)
    inputs_f = inputs.reshape(row_count, width).astype(jnp.float32)
    normed_low = norm_apply(inputs_f, gain_first).astype(jnp.bfloat16)
    projected = jnp.dot(normed_low, weight_qkv, preferred_element_type=jnp.float32)
    query_rows = projected[:, :width] + bias_query
    queries_low = (
        scale_queries(query_rows, scale_raw).astype(jnp.bfloat16).reshape(group_count, block, width)
    )
    keys_low = (
        projected[:, width : 2 * width].astype(jnp.bfloat16).reshape(group_count, block, width)
    )
    values_low = (
        (projected[:, 2 * width :] + bias_value)
        .astype(jnp.bfloat16)
        .reshape(group_count, block, width)
    )
    query_place = place_of(shard_index, block)
    starts = query_place[None, :] - positions.astype(jnp.float32)
    keep = (segment_ids != 0).astype(jnp.float32)[:, :, None]
    pieces = [(keys_low, values_low, query_place)]
    for distance in range(1, reach + 1):
        moved = passed_along((keys_low, values_low), "shard", distance)
        pieces.append((moved[0], moved[1], place_of(shard_index - distance, block)))
    queries_h = split_heads(queries_low)
    first_scores = masked_scores(queries_h, split_heads(keys_low), query_place, starts, query_place)
    running_top = jnp.max(first_scores, axis=-1)
    running_total = jnp.sum(jnp.exp(first_scores - running_top[..., None]), axis=-1)
    for keys_piece, values_piece, place_piece in pieces[1:]:
        scores = masked_scores(queries_h, split_heads(keys_piece), query_place, starts, place_piece)
        new_top = jnp.maximum(running_top, jnp.max(scores, axis=-1))
        running_total = running_total * jnp.exp(running_top - new_top) + jnp.sum(
            jnp.exp(scores - new_top[..., None]), axis=-1
        )
        running_top = new_top
    log_total = running_top + jnp.log(running_total)
    context = jnp.zeros((group_count, block, HEADS, width // HEADS), jnp.float32)
    for keys_piece, values_piece, place_piece in pieces:
        probs = probs_for(queries_h, starts, query_place, keys_piece, place_piece, log_total)
        context = context + jnp.einsum(
            "ghqk,gkhe->gqhe",
            probs.astype(jnp.bfloat16),
            split_heads(values_piece),
            preferred_element_type=jnp.float32,
        )
    attended_low = (
        (context.reshape(group_count, block, width) * keep)
        .astype(jnp.bfloat16)
        .reshape(row_count, width)
    )
    mixed = (
        inputs_f + jnp.dot(attended_low, weight_out, preferred_element_type=jnp.float32) + bias_out
    )
    normed_two_low = norm_apply(mixed, gain_second).astype(jnp.bfloat16)
    hidden = jnp.dot(normed_two_low, weight_up, preferred_element_type=jnp.float32) + bias_up
    activation_low = jax.nn.silu(hidden).astype(jnp.bfloat16)
    output = (
        mixed + jnp.dot(activation_low, weight_down, preferred_element_type=jnp.float32) + bias_down
    ).astype(jnp.bfloat16)
    regathered = (
        lax.all_gather(w_qkv, "shard", axis=0, tiled=True),
        lax.all_gather(w_out, "shard", axis=0, tiled=True),
        lax.all_gather(w_up, "shard", axis=0, tiled=True),
        lax.all_gather(w_down, "shard", axis=0, tiled=True),
    )
    back_qkv, back_out, back_up, back_down = regathered
    cotangent_low = cotangent.reshape(row_count, width)
    cotangent_f = cotangent_low.astype(jnp.float32)
    grad_down = jnp.einsum(
        "tf,td->fd", activation_low, cotangent_low, preferred_element_type=jnp.float32
    )
    grad_bias_down = jnp.sum(cotangent_f, axis=0)
    grad_activation = jnp.einsum(
        "td,fd->tf", cotangent_low, back_down, preferred_element_type=jnp.float32
    )
    grad_hidden = jax.vjp(jax.nn.silu, hidden)[1](grad_activation)[0]
    grad_bias_up = jnp.sum(grad_hidden, axis=0)
    grad_hidden_low = grad_hidden.astype(jnp.bfloat16)
    grad_up = jnp.einsum(
        "td,tf->df", normed_two_low, grad_hidden_low, preferred_element_type=jnp.float32
    )
    grad_normed_two = jnp.einsum(
        "tf,df->td", grad_hidden_low, back_up, preferred_element_type=jnp.float32
    )
    grad_mixed_part, grad_gain_two = jax.vjp(norm_apply, mixed, gain_second)[1](grad_normed_two)
    grad_mixed = cotangent_f + grad_mixed_part
    grad_bias_out = jnp.sum(grad_mixed, axis=0)
    grad_mixed_low = grad_mixed.astype(jnp.bfloat16)
    grad_out = jnp.einsum(
        "ta,td->ad", attended_low, grad_mixed_low, preferred_element_type=jnp.float32
    )
    grad_attended = jnp.einsum(
        "td,ad->ta", grad_mixed_low, back_out, preferred_element_type=jnp.float32
    )
    grad_context_low = grad_attended.astype(jnp.bfloat16).reshape(
        group_count, block, width
    ) * keep.astype(jnp.bfloat16)
    context_h = split_heads(grad_context_low)
    delta = jnp.zeros((group_count, HEADS, block), jnp.float32)
    for keys_piece, values_piece, place_piece in pieces:
        probs = probs_for(queries_h, starts, query_place, keys_piece, place_piece, log_total)
        delta = delta + jnp.sum(probs * value_grads(context_h, values_piece), axis=-1)
    grad_query_h = jnp.zeros((group_count, block, HEADS, width // HEADS), jnp.float32)
    key_total = None
    value_total = None
    for distance in range(reach + 1):
        keys_piece, values_piece, place_piece = pieces[distance]
        probs = probs_for(queries_h, starts, query_place, keys_piece, place_piece, log_total)
        score_grads = (probs * (value_grads(context_h, values_piece) - delta[..., None])).astype(
            jnp.bfloat16
        )
        grad_query_h = grad_query_h + jnp.einsum(
            "ghqk,gkhe->gqhe",
            score_grads,
            split_heads(keys_piece),
            preferred_element_type=jnp.float32,
        )
        key_term = jnp.einsum(
            "ghqk,gqhe->gkhe", score_grads, queries_h, preferred_element_type=jnp.float32
        )
        value_term = jnp.einsum(
            "ghqk,gqhe->gkhe",
            probs.astype(jnp.bfloat16),
            context_h,
            preferred_element_type=jnp.float32,
        )
        if distance == 0:
            key_total = key_term
            value_total = value_term
        else:
            returned = passed_along((key_term, value_term), "shard", -distance)
            key_total = key_total + returned[0]
            value_total = value_total + returned[1]
    grad_query, grad_scale = jax.vjp(scale_queries, query_rows, scale_raw)[1](
        grad_query_h.reshape(row_count, width)
    )
    grad_key_rows = key_total.reshape(row_count, width)
    grad_value_rows = value_total.reshape(row_count, width)
    grad_bias_query = jnp.sum(grad_query, axis=0)
    grad_bias_value = jnp.sum(grad_value_rows, axis=0)
    grad_projected_low = jnp.concatenate(
        [grad_query, grad_key_rows, grad_value_rows], axis=1
    ).astype(jnp.bfloat16)
    grad_qkv_share = lax.psum_scatter(
        jnp.einsum("td,tc->dc", normed_low, grad_projected_low, preferred_element_type=jnp.float32),
        "shard",
        scatter_dimension=0,
        tiled=True,
    )
    grad_normed = jnp.einsum(
        "tc,dc->td", grad_projected_low, back_qkv, preferred_element_type=jnp.float32
    )
    grad_inputs_part, grad_gain_one = jax.vjp(norm_apply, inputs_f, gain_first)[1](grad_normed)
    input_grad = (grad_mixed + grad_inputs_part).reshape(group_count, block, width)
    shares = (
        lax.psum_scatter(grad_gain_one, "shard", scatter_dimension=0, tiled=True),
        lax.psum_scatter(grad_bias_query, "shard", scatter_dimension=0, tiled=True),
        lax.psum_scatter(grad_bias_value, "shard", scatter_dimension=0, tiled=True),
        lax.psum_scatter(grad_scale, "shard", scatter_dimension=0, tiled=True),
        lax.psum_scatter(grad_out, "shard", scatter_dimension=0, tiled=True),
        lax.psum_scatter(grad_bias_out, "shard", scatter_dimension=0, tiled=True),
        lax.psum_scatter(grad_gain_two, "shard", scatter_dimension=0, tiled=True),
        lax.psum_scatter(grad_up, "shard", scatter_dimension=0, tiled=True),
        lax.psum_scatter(grad_bias_up, "shard", scatter_dimension=0, tiled=True),
        lax.psum_scatter(grad_down, "shard", scatter_dimension=0, tiled=True),
        lax.psum_scatter(grad_bias_down, "shard", scatter_dimension=0, tiled=True),
    )
    totals = lax.psum(
        (
            grad_qkv_share,
            shares[0],
            shares[1],
            shares[2],
            shares[3],
            shares[4],
            shares[5],
            shares[6],
            shares[7],
            shares[8],
            shares[9],
            shares[10],
        ),
        "replica",
    )
    return (
        output.reshape(group_count, block, width),
        input_grad,
        totals[1],
        totals[0],
        totals[2],
        totals[3],
        totals[4],
        totals[5],
        totals[6],
        totals[7],
        totals[8],
        totals[9],
        totals[10],
        totals[11],
    )


def solution(mesh):
    in_specs = (
        P("replica", "shard", None),
        P("replica", "shard"),
        P("replica", "shard"),
        P("shard"),
        P("shard", None),
        P("shard"),
        P("shard"),
        P("shard"),
        P("shard", None),
        P("shard"),
        P("shard"),
        P("shard", None),
        P("shard"),
        P("shard", None),
        P("shard"),
        P("replica", "shard", None),
    )
    out_specs = (
        P("replica", "shard", None),
        P("replica", "shard", None),
        P("shard"),
        P("shard", None),
        P("shard"),
        P("shard"),
        P("shard"),
        P("shard", None),
        P("shard"),
        P("shard"),
        P("shard", None),
        P("shard"),
        P("shard", None),
        P("shard"),
    )
    return jax.shard_map(
        on_device, mesh=mesh, in_specs=in_specs, out_specs=out_specs, check_vma=False
    )
```

profile of v0, /device:TPU:0, one launch (start us, length us, event | category | flops | bytes accessed | tf_op | source)
XLA Modules:
  0.0 1415.7 jit_solution(11817390567811746129)
XLA Ops:
  19.5 40.6 %all-reduce.19 = (bf16[1280]{0:T(1024)(128)(2,1)S(1)}, bf16[1280]{0:T(1024)(128)(2,1)S(1)}, bf16[80]{0:T(256)(128)(2,1)S(1)}, bf16[1280]{0:T(1024)(128)(2,1)S(1)...) all-reduce(bf16[1280]{0:T(1024)(128)(2,1)S(1)} %dynamic-update-slic, ...), channel_id=1, replica_groups=mesh['shard'=8,'replica'=4] {'shard'}, use_global_device_ids=true, to_apply=%add | all-reduce | flops 9040 | bytes 36160
  65.7 90.6 %all-gather.5.cloned.1.call-done = bf16[1280,3840]{1,0:T(8,128)(2,1)} async-done(((bf16[160,3840]{1,0:T(8,128)(2,1)}), bf16[1280,3840]{1,0:T(8,128)(2,1)}) %all-gather.5.cloned.1.call-update) | async-done | bytes 9830416 | tf_op jit(solution)/shard_map/all_gather | solution.py:88
  156.3 5.3 fusion.89
  162.5 3.2 collective-permute-start.6
  176.0 4.9 collective-permute-done.6
  183.1 31.1 %collective-permute-done.13 = bf16[1,128,1280]{2,1,0:T(8,128)(2,1)S(1)} collective-permute-done((bf16[1,128,1280]{2,1,0:T(8,128)(2,1)}, bf16[1,128,1280]{2,1,0:T(8,128)(2,1)S(1)}, u32[]{:S(2)}, u32[]{:S(2)}) %collective-permute-start.13) | collective-permute-done | bytes 327712 | tf_op jit(solution)/shard_map/ppermute | solution.py:21
  219.6 7.5 collective-permute-start.12
  235.2 4.5 collective-permute-start.9
  239.7 59.9 %collective-permute-start.7 = (bf16[1,128,1280]{2,1,0:T(8,128)(2,1)}, bf16[1,128,1280]{2,1,0:T(8,128)(2,1)}, u32[]{:S(2)}, u32[]{:S(2)}) collective-permute-start(bf16[1,128,1280]{2,1,0:T(8,128)(2,1)} %bitcast.16), channel_id=1, source_target_pairs={{0,4},{4,8},{8,12},{12,16},{16,20},{20,24},{24,28},{1,5},{5,9},{9,... | collective-permute-start | bytes 983048 | tf_op jit(solution)/shard_map/ppermute | solution.py:21
  342.6 22.0 %all-gather.9.cloned.1.call-done = bf16[1280,1280]{1,0:T(8,128)(2,1)} async-done(((bf16[160,1280]{1,0:T(8,128)(2,1)}), bf16[1280,1280]{1,0:T(8,128)(2,1)}) %all-gather.9.cloned.1.call-update) | async-done | bytes 3276816 | tf_op jit(solution)/shard_map/all_gather | solution.py:95
  364.6 3.4 convolution_add_fusion.1
  368.0 59.2 %all-gather.11.cloned.1.call-done = bf16[1280,1280]{1,0:T(8,128)(2,1)} async-done(((bf16[160,1280]{1,0:T(8,128)(2,1)}), bf16[1280,1280]{1,0:T(8,128)(2,1)}) %all-gather.11.cloned.1.call-update) | async-done | bytes 3276816 | tf_op jit(solution)/shard_map/all_gather | solution.py:97
  427.2 3.5 fusion.110
  433.2 3.7 fusion.59
  437.9 3.9 fusion.62
  442.8 4.9 fusion.53
  448.3 4.1 fusion.3
  480.9 9.8 collective-permute-done.27
  494.2 71.7 %collective-permute-done.25 = f32[1,128,16,80]{1,3,2,0:T(8,128)S(1)} collective-permute-done((f32[1,128,16,80]{1,3,2,0:T(8,128)S(1)}, f32[1,128,16,80]{1,3,2,0:T(8,128)S(1)}, u32[]{:S(2)}, u32[]{:S(2)}) %collective-permute-start.25) | collective-permute-done | bytes 655392 | tf_op jit(solution)/shard_map/ppermute | solution.py:21
  574.5 24.9 %collective-permute-done.20 = f32[1,128,16,80]{1,3,2,0:T(8,128)S(1)} collective-permute-done((f32[1,128,16,80]{1,3,2,0:T(8,128)S(1)}, f32[1,128,16,80]{1,3,2,0:T(8,128)S(1)}, u32[]{:S(2)}, u32[]{:S(2)}) %collective-permute-start.20) | collective-permute-done | bytes 655392 | tf_op jit(solution)/shard_map/ppermute | solution.py:21
  610.1 116.3 %collective-permute-done.18 = f32[1,128,16,80]{1,3,2,0:T(8,128)} collective-permute-done((f32[1,128,16,80]{1,3,2,0:T(8,128)}, f32[1,128,16,80]{1,3,2,0:T(8,128)}, u32[]{:S(2)}, u32[]{:S(2)}) %collective-permute-start.18) | collective-permute-done | bytes 655392 | tf_op jit(solution)/shard_map/ppermute | solution.py:21
  726.4 10.9 collective-permute-done.16
  740.4 8.3 fusion.51
  748.9 101.5 %reduce-scatter.9.cloned.1.call-done = f32[160,1280]{1,0:T(8,128)} async-done(((f32[1280,1280]{1,0:T(8,128)}), f32[160,1280]{1,0:T(8,128)}) %reduce-scatter.9.cloned.1.call-update) | async-done | bytes 819216 | tf_op jit(solution)/shard_map/reduce_scatter | solution.py:272
  850.4 124.4 %reduce-scatter.11.cloned.1.call-done = f32[160,1280]{1,0:T(8,128)} async-done(((f32[1280,1280]{1,0:T(8,128)}), f32[160,1280]{1,0:T(8,128)}) %reduce-scatter.11.cloned.1.call-update) | async-done | bytes 819216 | tf_op jit(solution)/shard_map/reduce_scatter | solution.py:274
  974.8 328.1 %reduce-scatter.5.cloned.1.call-done = f32[160,3840]{1,0:T(8,128)} async-done(((f32[1280,3840]{1,0:T(8,128)}), f32[160,3840]{1,0:T(8,128)}) %reduce-scatter.5.cloned.1.call-update) | async-done | bytes 2457616 | tf_op jit(solution)/shard_map/reduce_scatter | solution.py:253
  1304.5 3.3 fusion.4
  1307.9 8.2 fusion.41
  1316.1 34.8 %all-reduce.16 = (f32[1280]{0:T(1024)S(1)}, f32[1280]{0:T(1024)S(1)}, f32[1280]{0:T(1024)S(1)}, f32[80]{0:T(128)S(1)}, f32[1280]{0:T(1024)S(1)}, /*index=5*/f32[...) all-reduce(f32[1280]{0:T(1024)S(1)} %get-tuple-element.16, ...), channel_id=2, replica_groups=mesh['shard'=8,'replica'=4] {'shard'}, use_global_device_ids=true, to_apply=%region_29.30.clone | all-reduce | flops 9040 | bytes 72320
  1351.5 6.3 all-reduce.17
  1358.9 43.7 %all-reduce.22.cloned.1.call-done = (f32[160,3840]{1,0:T(8,128)}, f32[160,1280]{1,0:T(8,128)}, f32[160,1280]{1,0:T(8,128)}, f32[160,1280]{1,0:T(8,128)}) async-done(((f32[160,3840]{1,0:T(8,128)}, f32[160,1280]{1,0:T(8,128)}, f32[160,1280]{1,0:T(8,128)}, f32[160,1280]{1,0:T(8,128)}), (f32[160,3840]{1,0:T(8,128)}, f32[160,1280]{1,0:T(8,128)}, f32[160,1280]{1,0:T(8,128)}, ...) | async-done | bytes 4915216 | tf_op jit(solution)/shard_map/psum | solution.py:277
  1402.6 3.4 copy.335
  (384 shorter events, 149.1 us)
Async XLA Ops:
  7.2 149.1 %all-gather.5.cloned.1.call-start = ((), (), s32[]{:S(2)}) async-start(), calls=%async_computation.4 | async-start | bytes 11059200 | tf_op jit(solution)/shard_map/all_gather | solution.py:88
  7.9 331.9 %all-gather.7.cloned.1.call-start = ((), (), s32[]{:S(2)}) async-start(), calls=%async_computation.5 | async-start | bytes 3686400 | tf_op jit(solution)/shard_map/all_gather | solution.py:92
  8.7 355.9 %all-gather.9.cloned.1.call-start = ((), (), s32[]{:S(2)}) async-start(), calls=%async_computation.6 | async-start | bytes 3686400 | tf_op jit(solution)/shard_map/all_gather | solution.py:95
  9.4 417.8 %all-gather.11.cloned.1.call-start = ((), (), s32[]{:S(2)}) async-start(), calls=%async_computation.7 | async-start | bytes 3686400 | tf_op jit(solution)/shard_map/all_gather | solution.py:97
  10.0 738.9 %reduce-scatter.7.cloned.1.call-start = ((), (), s32[]{:S(2)}) async-start(), calls=%async_computation.9 | async-start | bytes 7372800 | tf_op jit(solution)/shard_map/reduce_scatter | solution.py:269
  165.7 50.5 %collective-permute-start.5 = (bf16[1,128,1280]{2,1,0:T(8,128)(2,1)}, bf16[1,128,1280]{2,1,0:T(8,128)(2,1)S(1)}, u32[]{:S(2)}, u32[]{:S(2)}) collective-permute-start(bf16[1,128,1280]{2,1,0:T(8,128)(2,1)} %slice_bitcast_fusion), channel_id=1, source_target_pairs={{0,24},{4,28},{1,25},{5,29},{2,26},{6,30},{3,27},{7,31}} | collective-permute-start | bytes 983048 | tf_op jit(solution)/shard_map/ppermute | solution.py:21
  167.0 52.5 %collective-permute-start.4 = (bf16[1,128,1280]{2,1,0:T(8,128)(2,1)}, bf16[1,128,1280]{2,1,0:T(8,128)(2,1)S(1)}, u32[]{:S(2)}, u32[]{:S(2)}) collective-permute-start(bf16[1,128,1280]{2,1,0:T(8,128)(2,1)} %slice_bitcast_fusion), channel_id=1, source_target_pairs={{0,20},{4,24},{8,28},{1,21},{5,25},{9,29},{2,22},{6,26},{10,30},{3... | collective-permute-start | bytes 983048 | tf_op jit(solution)/shard_map/ppermute | solution.py:21
  168.4 62.8 %collective-permute-start.3 = (bf16[1,128,1280]{2,1,0:T(8,128)(2,1)}, bf16[1,128,1280]{2,1,0:T(8,128)(2,1)}, u32[]{:S(2)}, u32[]{:S(2)}) collective-permute-start(bf16[1,128,1280]{2,1,0:T(8,128)(2,1)} %slice_bitcast_fusion), channel_id=1, source_target_pairs={{0,16},{4,20},{8,24},{12,28},{1,17},{5,21},{9,25},{13,29},{2,18},{... | collective-permute-start | bytes 983048 | tf_op jit(solution)/shard_map/ppermute | solution.py:21
  171.3 43.0 %collective-permute-start.13 = (bf16[1,128,1280]{2,1,0:T(8,128)(2,1)}, bf16[1,128,1280]{2,1,0:T(8,128)(2,1)S(1)}, u32[]{:S(2)}, u32[]{:S(2)}) collective-permute-start(bf16[1,128,1280]{2,1,0:T(8,128)(2,1)} %bitcast.16), channel_id=1, source_target_pairs={{0,28},{1,29},{2,30},{3,31}} | collective-permute-start | bytes 983048 | tf_op jit(solution)/shard_map/ppermute | solution.py:21
  180.9 52.2 %collective-permute-start.2 = (bf16[1,128,1280]{2,1,0:T(8,128)(2,1)}, bf16[1,128,1280]{2,1,0:T(8,128)(2,1)}, u32[]{:S(2)}, u32[]{:S(2)}) collective-permute-start(bf16[1,128,1280]{2,1,0:T(8,128)(2,1)} %slice_bitcast_fusion), channel_id=1, source_target_pairs={{0,12},{4,16},{8,20},{12,24},{16,28},{1,13},{5,17},{9,21},{13,25},... | collective-permute-start | bytes 983048 | tf_op jit(solution)/shard_map/ppermute | solution.py:21
  219.6 84.9 %collective-permute-start.12 = (bf16[1,128,1280]{2,1,0:T(8,128)(2,1)}, bf16[1,128,1280]{2,1,0:T(8,128)(2,1)}, u32[]{:S(2)}, u32[]{:S(2)}) collective-permute-start(bf16[1,128,1280]{2,1,0:T(8,128)(2,1)} %bitcast.16), channel_id=1, source_target_pairs={{0,24},{4,28},{1,25},{5,29},{2,26},{6,30},{3,27},{7,31}} | collective-permute-start | bytes 983048 | tf_op jit(solution)/shard_map/ppermute | solution.py:21
  231.1 87.8 %collective-permute-start.11 = (bf16[1,128,1280]{2,1,0:T(8,128)(2,1)}, bf16[1,128,1280]{2,1,0:T(8,128)(2,1)}, u32[]{:S(2)}, u32[]{:S(2)}) collective-permute-start(bf16[1,128,1280]{2,1,0:T(8,128)(2,1)} %bitcast.16), channel_id=1, source_target_pairs={{0,20},{4,24},{8,28},{1,21},{5,25},{9,29},{2,22},{6,26},{10,30},{3... | collective-permute-start | bytes 983048 | tf_op jit(solution)/shard_map/ppermute | solution.py:21
  233.2 87.6 %collective-permute-start.10 = (bf16[1,128,1280]{2,1,0:T(8,128)(2,1)}, bf16[1,128,1280]{2,1,0:T(8,128)(2,1)}, u32[]{:S(2)}, u32[]{:S(2)}) collective-permute-start(bf16[1,128,1280]{2,1,0:T(8,128)(2,1)} %bitcast.16), channel_id=1, source_target_pairs={{0,16},{4,20},{8,24},{12,28},{1,17},{5,21},{9,25},{13,29},{2,18},{... | collective-permute-start | bytes 983048 | tf_op jit(solution)/shard_map/ppermute | solution.py:21
  235.2 87.5 %collective-permute-start.9 = (bf16[1,128,1280]{2,1,0:T(8,128)(2,1)}, bf16[1,128,1280]{2,1,0:T(8,128)(2,1)}, u32[]{:S(2)}, u32[]{:S(2)}) collective-permute-start(bf16[1,128,1280]{2,1,0:T(8,128)(2,1)} %bitcast.16), channel_id=1, source_target_pairs={{0,12},{4,16},{8,20},{12,24},{16,28},{1,13},{5,17},{9,21},{13,25},... | collective-permute-start | bytes 983048 | tf_op jit(solution)/shard_map/ppermute | solution.py:21
  239.7 84.8 %collective-permute-start.7 = (bf16[1,128,1280]{2,1,0:T(8,128)(2,1)}, bf16[1,128,1280]{2,1,0:T(8,128)(2,1)}, u32[]{:S(2)}, u32[]{:S(2)}) collective-permute-start(bf16[1,128,1280]{2,1,0:T(8,128)(2,1)} %bitcast.16), channel_id=1, source_target_pairs={{0,4},{4,8},{8,12},{12,16},{16,20},{20,24},{24,28},{1,5},{5,9},{9,... | collective-permute-start | bytes 983048 | tf_op jit(solution)/shard_map/ppermute | solution.py:21
  437.0 413.4 %reduce-scatter.9.cloned.1.call-start = ((), (), s32[]{:S(2)}) async-start(), calls=%async_computation.10 | async-start | bytes 7372800 | tf_op jit(solution)/shard_map/reduce_scatter | solution.py:272
  441.8 533.0 %reduce-scatter.11.cloned.1.call-start = ((), (), s32[]{:S(2)}) async-start(), calls=%async_computation.11 | async-start | bytes 7372800 | tf_op jit(solution)/shard_map/reduce_scatter | solution.py:274
  447.7 855.3 %reduce-scatter.5.cloned.1.call-start = ((), (), s32[]{:S(2)}) async-start(), calls=%async_computation.8 | async-start | bytes 22118400 | tf_op jit(solution)/shard_map/reduce_scatter | solution.py:253
  454.1 36.6 %collective-permute-start.27 = (f32[1,128,16,80]{1,3,2,0:T(8,128)S(1)}, f32[1,128,16,80]{1,3,2,0:T(8,128)S(1)}, u32[]{:S(2)}, u32[]{:S(2)}) collective-permute-start(f32[1,128,16,80]{1,3,2,0:T(8,128)S(1)} %convolution_bitcast_fusion), channel_id=1, source_target_pairs={{28,0},{29,1},{30,2},{31,3}} | collective-permute-start | bytes 1966088 | tf_op jit(solution)/shard_map/ppermute | solution.py:21
  457.3 35.7 %collective-permute-start.26 = (f32[1,128,16,80]{1,3,2,0:T(8,128)S(1)}, f32[1,128,16,80]{1,3,2,0:T(8,128)S(1)}, u32[]{:S(2)}, u32[]{:S(2)}) collective-permute-start(f32[1,128,16,80]{1,3,2,0:T(8,128)S(1)} %convolution_bitcast_fusion.1), channel_id=1, source_target_pairs={{24,0},{28,4},{25,1},{29,5},{26,2},{30,6},{27,3},{31,7}} | collective-permute-start | bytes 1966088 | tf_op jit(solution)/shard_map/ppermute | solution.py:21
  459.2 106.7 %collective-permute-start.25 = (f32[1,128,16,80]{1,3,2,0:T(8,128)S(1)}, f32[1,128,16,80]{1,3,2,0:T(8,128)S(1)}, u32[]{:S(2)}, u32[]{:S(2)}) collective-permute-start(f32[1,128,16,80]{1,3,2,0:T(8,128)S(1)} %convolution_bitcast_fusion.2), channel_id=1, source_target_pairs={{20,0},{24,4},{28,8},{21,1},{25,5},{29,9},{22,2},{26,6},{30,10},{2... | collective-permute-start | bytes 1966088 | tf_op jit(solution)/shard_map/ppermute | solution.py:21
  461.2 106.0 %collective-permute-start.24 = (f32[1,128,16,80]{1,3,2,0:T(8,128)S(1)}, f32[1,128,16,80]{1,3,2,0:T(8,128)S(1)}, u32[]{:S(2)}, u32[]{:S(2)}) collective-permute-start(f32[1,128,16,80]{1,3,2,0:T(8,128)S(1)} %convolution_bitcast_fusion.3), channel_id=1, source_target_pairs={{16,0},{20,4},{24,8},{28,12},{17,1},{21,5},{25,9},{29,13},{18,2},{... | collective-permute-start | bytes 1966088 | tf_op jit(solution)/shard_map/ppermute | solution.py:21
  463.1 107.4 %collective-permute-start.23 = (f32[1,128,16,80]{1,3,2,0:T(8,128)S(1)}, f32[1,128,16,80]{1,3,2,0:T(8,128)S(1)}, u32[]{:S(2)}, u32[]{:S(2)}) collective-permute-start(f32[1,128,16,80]{1,3,2,0:T(8,128)S(1)} %convolution_bitcast_fusion.4), channel_id=1, source_target_pairs={{12,0},{16,4},{20,8},{24,12},{28,16},{13,1},{17,5},{21,9},{25,13},... | collective-permute-start | bytes 1966088 | tf_op jit(solution)/shard_map/ppermute | solution.py:21
  490.7 81.2 %collective-permute-start.22 = (f32[1,128,16,80]{1,3,2,0:T(8,128)S(1)}, f32[1,128,16,80]{1,3,2,0:T(8,128)S(1)}, u32[]{:S(2)}, u32[]{:S(2)}) collective-permute-start(f32[1,128,16,80]{1,3,2,0:T(8,128)S(1)} %convolution_bitcast_fusion.5), channel_id=1, source_target_pairs={{8,0},{12,4},{16,8},{20,12},{24,16},{28,20},{9,1},{13,5},{17,9},{2... | collective-permute-start | bytes 1966088 | tf_op jit(solution)/shard_map/ppermute | solution.py:21
  492.9 80.3 %collective-permute-start.21 = (f32[1,128,16,80]{1,3,2,0:T(8,128)S(1)}, f32[1,128,16,80]{1,3,2,0:T(8,128)S(1)}, u32[]{:S(2)}, u32[]{:S(2)}) collective-permute-start(f32[1,128,16,80]{1,3,2,0:T(8,128)S(1)} %convolution_bitcast_fusion.6), channel_id=1, source_target_pairs={{4,0},{8,4},{12,8},{16,12},{20,16},{24,20},{28,24},{5,1},{9,5},{13... | collective-permute-start | bytes 1966088 | tf_op jit(solution)/shard_map/ppermute | solution.py:21
  565.9 33.6 %collective-permute-start.20 = (f32[1,128,16,80]{1,3,2,0:T(8,128)S(1)}, f32[1,128,16,80]{1,3,2,0:T(8,128)S(1)}, u32[]{:S(2)}, u32[]{:S(2)}) collective-permute-start(f32[1,128,16,80]{1,3,2,0:T(8,128)S(1)} %convolution_bitcast_fusion.8), channel_id=1, source_target_pairs={{28,0},{29,1},{30,2},{31,3}} | collective-permute-start | bytes 1966088 | tf_op jit(solution)/shard_map/ppermute | solution.py:21
  570.6 155.8 %collective-permute-start.18 = (f32[1,128,16,80]{1,3,2,0:T(8,128)}, f32[1,128,16,80]{1,3,2,0:T(8,128)}, u32[]{:S(2)}, u32[]{:S(2)}) collective-permute-start(f32[1,128,16,80]{1,3,2,0:T(8,128)} %convolution_bitcast_fusion.10), channel_id=1, source_target_pairs={{20,0},{24,4},{28,8},{21,1},{25,5},{29,9},{22,2},{26,6},{30,10},{2... | collective-permute-start | bytes 1966088 | tf_op jit(solution)/shard_map/ppermute | solution.py:21
  571.9 154.5 %collective-permute-start.17 = (f32[1,128,16,80]{1,3,2,0:T(8,128)}, f32[1,128,16,80]{1,3,2,0:T(8,128)}, u32[]{:S(2)}, u32[]{:S(2)}) collective-permute-start(f32[1,128,16,80]{1,3,2,0:T(8,128)} %convolution_bitcast_fusion.11), channel_id=1, source_target_pairs={{16,0},{20,4},{24,8},{28,12},{17,1},{21,5},{25,9},{29,13},{18,2},{... | collective-permute-start | bytes 1966088 | tf_op jit(solution)/shard_map/ppermute | solution.py:21
  573.2 164.1 %collective-permute-start.16 = (f32[1,128,16,80]{1,3,2,0:T(8,128)}, f32[1,128,16,80]{1,3,2,0:T(8,128)}, u32[]{:S(2)}, u32[]{:S(2)}) collective-permute-start(f32[1,128,16,80]{1,3,2,0:T(8,128)} %convolution_bitcast_fusion.12), channel_id=1, source_target_pairs={{12,0},{16,4},{20,8},{24,12},{28,16},{13,1},{17,5},{21,9},{25,13},... | collective-permute-start | bytes 1966088 | tf_op jit(solution)/shard_map/ppermute | solution.py:21
  599.5 137.8 %collective-permute-start.15 = (f32[1,128,16,80]{1,3,2,0:T(8,128)}, f32[1,128,16,80]{1,3,2,0:T(8,128)}, u32[]{:S(2)}, u32[]{:S(2)}) collective-permute-start(f32[1,128,16,80]{1,3,2,0:T(8,128)} %convolution_bitcast_fusion.13), channel_id=1, source_target_pairs={{8,0},{12,4},{16,8},{20,12},{24,16},{28,20},{9,1},{13,5},{17,9},{2... | collective-permute-start | bytes 1966088 | tf_op jit(solution)/shard_map/ppermute | solution.py:21
  600.8 136.5 %collective-permute-start.14 = (f32[1,128,16,80]{1,3,2,0:T(8,128)}, f32[1,128,16,80]{1,3,2,0:T(8,128)}, u32[]{:S(2)}, u32[]{:S(2)}) collective-permute-start(f32[1,128,16,80]{1,3,2,0:T(8,128)} %convolution_bitcast_fusion.14), channel_id=1, source_target_pairs={{4,0},{8,4},{12,8},{16,12},{20,16},{24,20},{28,24},{5,1},{9,5},{13... | collective-permute-start | bytes 1966088 | tf_op jit(solution)/shard_map/ppermute | solution.py:21
  748.8 653.8 %all-reduce.22.cloned.1.call-start = ((), (), s32[]{:S(2)}) async-start(), calls=%async_computation.12 | async-start | bytes 9830400 | tf_op jit(solution)/shard_map/psum | solution.py:277
  (92 other events, 4152.8 us)
Sparse Core Ops, SparseCore 0:
  10.2 146.0 all-gather.4
  158.5 121.0 all-gather.6
  281.8 82.7 all-gather.8
  366.7 60.5 all-gather.10
  437.1 235.9 reduce-scatter.6
  677.0 173.3 reduce-scatter.8
  854.0 120.7 reduce-scatter.10
  979.2 323.6 reduce-scatter.4
  1305.7 96.8 all-reduce.21
where the time goes:
time: 1420 us
  waiting for transfers between devices  1040 us (73%)
  starting transfers between devices  113 us (8%)
  matrix products  96.2 us (7%)
  blocking collectives  81.7 us (6%)
  local copies, waits for them, and re-layouts  49.4 us (3%)
  between operations  18.4 us (1%)
    reduce_scatter x1, waiting for transfers between devices, on_device(): lax.psum_scatter(jnp.einsum('td,tc->dc', normed_low, grad_projected_low,...  328 us
    ppermute x28, waiting for transfers between devices, passed_along(): return lax.ppermute(shard, axis, pairs)  271 us
    reduce_scatter x1, waiting for transfers between devices, on_device(): lax.psum_scatter(grad_down, 'shard', scatter_dimension=0, tiled=True)  124 us
    ppermute x28, starting transfers between devices, passed_along(): return lax.ppermute(shard, axis, pairs)  112 us
    reduce_scatter x1, waiting for transfers between devices, on_device(): lax.psum_scatter(grad_up, 'shard', scatter_dimension=0, tiled=True)  102 us
    all_gather x1, waiting for transfers between devices, on_device(): lax.all_gather(w_qkv, 'shard', axis=0, tiled=True)  90.6 us
    unnamed x2, blocking collectives  75.4 us
    all_gather x1, waiting for transfers between devices, on_device(): lax.all_gather(w_down, 'shard', axis=0, tiled=True)  59.2 us
  transfers between devices with their start and end apart: 37, of which 15 were waited for; matrix products, arithmetic and copies ran while one was open for 10% of the time, Pallas kernels for 0%

commit v1 on v0

v1 whole, which is shorter than its diff:
```python
import functools
import math

import jax
import jax.numpy as jnp
from jax import lax
from jax.experimental import pallas as pl
from jax.experimental.pallas import tpu as pltpu
from jax.sharding import PartitionSpec as P

HEADS = 16
HEAD = 80
DOC_MAX = 800
EPS = 1e-06
QUERY_BASE = 1.442695041
MASKED = -1000000000.0
MESH = pl.DeviceIdType.MESH
MAJOR = 4
VMEM = pl.BlockSpec(memory_space=pltpu.VMEM)
ANY = pl.BlockSpec(memory_space=pl.ANY)
F32 = jnp.float32
BF16 = jnp.bfloat16


class Place:
    def __init__(self, shards):
        self.shards = shards
        self.minor = shards // MAJOR
        self.me = lax.axis_index("shard")
        self.rep = lax.axis_index("replica")
        self.a = self.me // self.minor
        self.b = lax.rem(self.me, self.minor)
        self.started = []

    def at(self, da, db):
        a = lax.rem(self.a + da + MAJOR, MAJOR)
        b = lax.rem(self.b + db + self.minor, self.minor)
        return a * self.minor + b

    def flip(self, mask):
        bit = lax.rem(self.rep // mask, 2)
        return self.rep + mask - 2 * mask * bit

    def greet(self, masks):
        barrier = pltpu.get_barrier_semaphore()
        count = 0
        for da in range(MAJOR):
            for db in range(self.minor):
                if da or db:
                    pl.semaphore_signal(
                        barrier, inc=1, device_id=(self.at(da, db), self.rep), device_id_type=MESH
                    )
                    count += 1
        for mask in masks:
            pl.semaphore_signal(
                barrier, inc=1, device_id=(self.me, self.flip(mask)), device_id_type=MESH
            )
            count += 1
        pl.semaphore_wait(barrier, count)

    def send(self, src, dst, ssem, rsem, shard=None, rep=None):
        copy = pltpu.make_async_remote_copy(
            src_ref=src,
            dst_ref=dst,
            send_sem=ssem,
            recv_sem=rsem,
            device_id=(self.me if shard is None else shard, self.rep if rep is None else rep),
            device_id_type=MESH,
        )
        copy.start()
        self.started.append(copy)
        return copy

    def arrived(self, dst, ssem, rsem):
        pltpu.make_async_remote_copy(
            src_ref=dst,
            dst_ref=dst,
            send_sem=ssem,
            recv_sem=rsem,
            device_id=(self.me, self.rep),
            device_id_type=MESH,
        ).wait_recv()

    def settle(self):
        for copy in self.started:
            copy.wait_send()
        self.started = []


def masks_of(parts):
    return {4: (2, 1), 2: (1,), 1: ()}[parts]


def others(place):
    return [(da, db) for da in range(MAJOR) for db in range(place.minor) if da or db]


def front_kernel(
    shards, wparts, fparts, qblock,
    x_ref, packet_ref, bias_ref, wq_ref, ffn_ref,
    normed_ref, qkv_ref, query_ref, log_ref, att_ref, vec_ref, start_ref, wcols_ref, ffn_out,
    xg, packets, turned, context,
    x_send, x_recv, p_send, p_recv, w_send, w_recv, f_send, f_recv, f_local, a_send, a_recv,
):
    at = Place(shards)
    me, minor = at.me, at.minor
    block, width = x_ref.shape
    length = shards * block
    slab = width // shards
    local = slab // HEAD
    peers = others(at)
    fmasks = masks_of(fparts)
    wmasks = masks_of(wparts)
    at.greet(tuple(sorted(set(fmasks) | set(wmasks))))
    fpart = lax.rem(at.rep, fparts)
    wpart = lax.rem(at.rep, wparts)

    for i, (da, db) in enumerate(peers):
        at.send(packet_ref, packets.at[me], p_send.at[i], p_recv.at[me], shard=at.at(da, db))
    xg[me] = x_ref[...]
    packets[me] = packet_ref[...]
    k = 0
    for da in range(1, MAJOR):
        at.send(xg.at[me], xg.at[me], x_send.at[k], x_recv.at[me], shard=at.at(da, 0))
        k += 1
    for db in range(1, minor):
        at.send(xg.at[me], xg.at[me], x_send.at[k], x_recv.at[me], shard=at.at(0, db))
        k += 1
    for i, (da, db) in enumerate(peers):
        dest = at.at(da, db)
        at.send(
            wq_ref.at[dest, wpart], wcols_ref.at[me, wpart], w_send.at[i], w_recv.at[me, wpart], shard=dest
        )
    own = pltpu.make_async_copy(wq_ref.at[me], wcols_ref.at[me], f_local.at[0])
    own.start()
    own_ffn = pltpu.make_async_copy(ffn_ref, ffn_out.at[:, me], f_local.at[1])
    own_ffn.start()
    fk = 0
    for db in range(1, minor):
        at.send(
            ffn_ref.at[:, fpart], ffn_out.at[:, me, fpart], f_send.at[fk], f_recv.at[me, fpart],
            shard=at.at(0, db),
        )
        fk += 1

    for da in range(1, MAJOR):
        origin = at.at(-da, 0)
        at.arrived(xg.at[origin], x_send.at[0], x_recv.at[origin])
        for db in range(1, minor):
            at.send(xg.at[origin], xg.at[origin], x_send.at[k], x_recv.at[origin], shard=at.at(0, db))
            k += 1
    for da in range(1, MAJOR):
        at.send(
            ffn_ref.at[:, fpart], ffn_out.at[:, me, fpart], f_send.at[fk], f_recv.at[me, fpart],
            shard=at.at(da, 0),
        )
        fk += 1

    wk = len(peers)
    for mask in wmasks:
        for da, db in peers:
            origin = at.at(-da, -db)
            slot = wcols_ref.at[origin, wpart]
            at.arrived(slot, w_send.at[0], w_recv.at[origin, wpart])
            at.send(slot, slot, w_send.at[wk], w_recv.at[origin, wpart], rep=at.flip(mask))
            wk += 1
    for da, db in peers:
        origin = at.at(-da, -db)
        last = wparts - 1 - wpart
        at.arrived(wcols_ref.at[origin, last], w_send.at[0], w_recv.at[origin, last])
    own.wait()
    turned[...] = wcols_ref[...].reshape(width, 3 * slab).T

    for da, db in peers:
        origin = at.at(-da, -db)
        at.arrived(packets.at[origin], p_send.at[0], p_recv.at[origin])
    vectors = jnp.zeros((8, width), F32)
    scales = jnp.zeros((1, 128), F32)
    lanes = lax.broadcasted_iota(jnp.int32, (8, width), 1)
    for j in range(shards):
        piece = packets[j]
        wide = jnp.concatenate([piece, jnp.zeros((8, width - piece.shape[1]), F32)], axis=1)
        wide = jnp.where(lanes < slab, wide, 0.0)
        vectors = vectors + (pltpu.roll(wide, j * slab, 1) if j else wide)
        scales = scales + piece[5:6, :128]
        start_ref[:, j * block : (j + 1) * block] = jnp.broadcast_to(piece[6:7, :block], (8, block))
    rows = lax.broadcasted_iota(jnp.int32, (8, width), 0)
    vec_ref[...] = jnp.where(rows < 5, vectors, 0.0)
    vec_ref[5:6, :128] = scales
    gain = vec_ref[0:1, :]
    column = jnp.broadcast_to(scales, (128, 128)).T[:HEAD, 0:1]
    soft = jnp.maximum(column, 0.0) + jnp.log(1.0 + jnp.exp(-jnp.abs(column)))
    factor = jnp.concatenate([QUERY_BASE / math.sqrt(HEAD) * soft] * local, axis=0)
    bias_query = bias_ref[:, 0:1]
    bias_value = bias_ref[:, 1:2]

    def project(origin):
        rows_in = xg[origin].astype(F32)
        scale = lax.rsqrt(jnp.mean(rows_in * rows_in, axis=-1, keepdims=True) + EPS)
        normed = (rows_in * scale * gain).astype(BF16)
        tokens = pl.ds(pl.multiple_of(origin * block, block), block)
        normed_ref[tokens, :] = normed
        out = lax.dot_general(
            turned[...], normed, (((1,), (1,)), ((), ())), preferred_element_type=F32
        )
        query = out[:slab] + bias_query
        query_ref[:, tokens] = query
        qkv_ref[:slab, tokens] = (query * factor).astype(BF16)
        qkv_ref[slab : 2 * slab, tokens] = out[slab : 2 * slab].astype(BF16)
        qkv_ref[2 * slab :, tokens] = (out[2 * slab :] + bias_value).astype(BF16)

    def project_major(i, carry):
        project(at.at(-i, 0))
        return carry

    def project_minor(i, carry):
        origin = at.at(-lax.rem(i, MAJOR), -(1 + i // MAJOR))
        at.arrived(xg.at[origin], x_send.at[0], x_recv.at[origin])
        project(origin)
        return carry

    lax.fori_loop(0, MAJOR, project_major, 0)
    lax.fori_loop(0, shards - MAJOR, project_minor, 0)

    log_ref[...] = jnp.zeros_like(log_ref)
    for i in range(length // qblock):
        reach = (i + 1) * qblock
        span = slice(i * qblock, reach)
        starts = start_ref[0:1, span]
        key_place = lax.broadcasted_iota(jnp.int32, (reach, qblock), 0).astype(F32)
        query_place = (i * qblock + lax.broadcasted_iota(jnp.int32, (1, qblock), 1)).astype(F32)
        allowed = (key_place >= starts) & (key_place <= query_place)
        for h in range(local):
            head = slice(h * HEAD, (h + 1) * HEAD)
            queries = qkv_ref[h * HEAD : (h + 1) * HEAD, span]
            keys = qkv_ref[slab + h * HEAD : slab + (h + 1) * HEAD, :reach]
            values = qkv_ref[2 * slab + h * HEAD : 2 * slab + (h + 1) * HEAD, :reach]
            scores = lax.dot_general(
                keys, queries, (((0,), (0,)), ((), ())), preferred_element_type=F32
            )
            scores = jnp.where(allowed, scores, MASKED)
            top = jnp.max(scores, axis=0, keepdims=True)
            powers = jnp.exp(scores - top)
            total = jnp.sum(powers, axis=0, keepdims=True)
            probs = (powers * (1.0 / total)).astype(BF16)
            log_ref[h : h + 1, span] = top + jnp.log(total)
            context[head, span] = jnp.dot(values, probs, preferred_element_type=F32).astype(BF16)
        for j in range(i * qblock // block, reach // block):
            @pl.when(me != j)
            def _():
                pltpu.make_async_remote_copy(
                    src_ref=context.at[:, j * block : (j + 1) * block],
                    dst_ref=att_ref.at[pl.ds(pl.multiple_of(me * slab, slab), slab), :],
                    send_sem=a_send.at[j],
                    recv_sem=a_recv.at[me],
                    device_id=(j, at.rep),
                    device_id_type=MESH,
                ).start()

            @pl.when(me == j)
            def _():
                att_ref[pl.ds(pl.multiple_of(me * slab, slab), slab), :] = context[
                    :, j * block : (j + 1) * block
                ]

    def share(origin, have, mask, fk):
        for part in have:
            slot = ffn_out.at[:, origin, part]
            at.send(slot, slot, f_send.at[fk], f_recv.at[origin, part], rep=at.flip(mask))
            fk += 1
        return fk

    def flipped(part, mask):
        bit = lax.rem(part // mask, 2)
        return part + mask - 2 * mask * bit

    own_parts = [fpart]
    for da in range(1, MAJOR):
        origin = at.at(-da, 0)
        slot = ffn_out.at[:, origin, fpart]
        at.arrived(slot, f_send.at[0], f_recv.at[origin, fpart])
        for db in range(1, minor):
            at.send(slot, slot, f_send.at[fk], f_recv.at[origin, fpart], shard=at.at(0, db))
            fk += 1
        for mask in fmasks:
            fk = share(origin, own_parts, mask, fk)
    for db in range(1, minor):
        for da in range(MAJOR):
            origin = at.at(-da, -db)
            slot = ffn_out.at[:, origin, fpart]
            at.arrived(slot, f_send.at[0], f_recv.at[origin, fpart])
            for mask in fmasks:
                fk = share(origin, own_parts, mask, fk)
    order = [(da, 0) for da in range(1, MAJOR)]
    order += [(da, db) for db in range(1, minor) for da in range(MAJOR)]
    got = []
    for n, mask in enumerate(fmasks):
        fresh = [flipped(part, mask) for part in own_parts + got]
        for da, db in order:
            origin = at.at(-da, -db)
            for part in fresh:
                at.arrived(ffn_out.at[:, origin, part], f_send.at[0], f_recv.at[origin, part])
            for later in fmasks[n + 1 :]:
                fk = share(origin, fresh, later, fk)
        got = got + fresh
    for da, db in peers:
        origin = at.at(-da, -db)
        at.arrived(
            att_ref.at[pl.ds(pl.multiple_of(origin * slab, slab), slab), :],
            a_send.at[0],
            a_recv.at[origin],
        )
    own_ffn.wait()
    for j in range(shards):
        @pl.when(me != j)
        def _():
            pltpu.make_async_remote_copy(
                src_ref=context.at[:, j * block : (j + 1) * block],
                dst_ref=context.at[:, j * block : (j + 1) * block],
                send_sem=a_send.at[j],
                recv_sem=a_recv.at[0],
                device_id=(j, at.rep),
                device_id_type=MESH,
            ).wait_send()
    at.settle()


def parts_of(rows, unit, most):
    parts = most
    while parts > 1 and rows % (parts * unit):
        parts //= 2
    return parts


def front(shards, inputs, packet, biases, wq, ffn):
    block, width = inputs.shape
    slab = width // shards
    length = shards * block
    local = slab // HEAD
    wparts = wq.shape[1]
    fparts = ffn.shape[1]
    minor = shards // MAJOR
    qblock = 2 * block
    peers = shards - 1
    shapes = (
        jax.ShapeDtypeStruct((length, width), BF16),
        jax.ShapeDtypeStruct((3 * slab, length), BF16),
        jax.ShapeDtypeStruct((slab, length), F32),
        jax.ShapeDtypeStruct((8, length), F32),
        jax.ShapeDtypeStruct((width, block), BF16),
        jax.ShapeDtypeStruct((8, width), F32),
        jax.ShapeDtypeStruct((8, length), F32),
        jax.ShapeDtypeStruct((shards,) + wq.shape[1:], BF16),
        jax.ShapeDtypeStruct((3, shards) + ffn.shape[1:], BF16),
    )
    dma = pltpu.SemaphoreType.DMA
    plane = MAJOR * minor - 1
    f_sends = plane + plane * (fparts - 1)
    return pl.pallas_call(
        functools.partial(front_kernel, shards, wparts, fparts, qblock),
        out_shape=shapes,
        in_specs=[VMEM, VMEM, VMEM, VMEM, ANY],
        out_specs=[VMEM] * 8 + [ANY],
        scratch_shapes=[
            pltpu.VMEM((shards, block, width), BF16),
            pltpu.VMEM((shards, 8, packet.shape[1]), F32),
            pltpu.VMEM((3 * slab, width), BF16),
            pltpu.VMEM((slab, length), BF16),
            dma((plane,)),
            dma((shards,)),
            dma((peers,)),
            dma((shards,)),
            dma((peers * wparts,)),
            dma((shards, wparts)),
            dma((f_sends + 8,)),
            dma((shards, fparts)),
            dma((2,)),
            dma((shards,)),
            dma((shards,)),
        ],
        compiler_params=pltpu.CompilerParams(
            collective_id=0, has_side_effects=True, vmem_limit_bytes=56 << 20
        ),
        name="front",
    )(inputs, packet, biases, wq, ffn)


def prepare(inputs, segment_ids, positions, gain_one, w_qkv, b_query, b_value, query_scale, w_out, b_out, gain_two, w_up, b_up, w_down, b_down):
    shards = lax.axis_size("shard")
    me = lax.axis_index("shard")
    block, width = inputs.shape
    slab = width // shards
    starts = (me * block + lax.iota(jnp.int32, block) - positions.reshape(block)).astype(F32)
    rows = jnp.stack(
        [jnp.pad(v.astype(F32), (0, 256 - slab)) for v in (gain_one, b_out, gain_two, b_up, b_down)]
    )
    scale_row = lax.dynamic_update_slice(
        jnp.zeros((1, 256), F32), query_scale.astype(F32)[None], (0, me * query_scale.shape[0])
    )
    start_row = jnp.pad(starts, (0, 256 - block))[None]
    packet = jnp.concatenate([rows, scale_row, start_row, jnp.zeros((1, 256), F32)], axis=0)
    biases = jnp.stack([b_query, b_value], axis=1).astype(F32)
    wparts = parts_of(slab, 16, 2)
    fparts = parts_of(slab, 8, 4)
    wq = (
        w_qkv.reshape(slab, 3, shards, slab)
        .transpose(2, 0, 1, 3)
        .reshape(shards, wparts, slab // wparts, 3 * slab)
    )
    ffn = jnp.stack([w_out, w_up, w_down]).reshape(3, fparts, slab // fparts, width)
    return packet, biases, wq, ffn


def flipped(part, mask):
    bit = lax.rem(part // mask, 2)
    return part + mask - 2 * mask * bit


def back_kernel(
    shards, replicas, parts, qblock,
    g_ref, dctx_ref, qkv_ref, query_ref, log_ref, start_ref, normed_ref, wcols_ref, vec_ref, row_ref,
    fin_ref, gw_ref, gn_ref, small_ref,
    dctx, grads, turned, proj,
    own, from_core, from_y, from_x, from_z, extra,
    part_gn, gn_x, gn_z,
    gw, gw_core, gw_y, gw_sum, gw_land, gw_extra,
    windows, small_land, small_got,
    d_send, d_recv, o_sem, c_send, c_recv, y_send, y_recv, x_send, x_recv, z_send, z_recv,
    r_send, r_recv, e_send, e_recv,
    nx_send, nx_recv, nz_send, nz_recv,
    wc_send, wc_recv, wy_send, wy_recv, wa_send, wa_recv, wr_send, wr_recv, we_send, we_recv,
    v_send, v_recv, b_send, b_recv,
):
    at = Place(shards)
    me, minor = at.me, at.minor
    slab3, length = qkv_ref.shape
    slab = slab3 // 3
    local = slab // HEAD
    block = length // shards
    width = normed_ref.shape[1]
    peers = others(at)
    halves = max(parts // 2, 1)
    core = lax.rem(at.rep, 2)
    mine = lax.rem(at.rep, parts)
    km = mine // 2 if parts > 1 else 0
    every = []
    mask = 1
    while mask < replicas:
        every.append(mask)
        mask *= 2
    extras = [m for m in every if m >= parts]
    at.greet(tuple(every))
    mats = (2, 1, 0)

    for i, (da, db) in enumerate(peers):
        dest = at.at(da, db)
        at.send(
            dctx_ref.at[pl.ds(pl.multiple_of(dest * slab, slab), slab), :],
            dctx.at[:, pl.ds(pl.multiple_of(me * block, block), block)],
            d_send.at[i], d_recv.at[me], shard=dest,
        )
    locals_ = {}
    for m in mats:
        for k in range(halves):
            if parts > 1:
                at.send(
                    g_ref.at[m, :, (1 - core) + 2 * k], from_core.at[m, k],
                    c_send.at[m, k], c_recv.at[m, k], rep=at.flip(1),
                )
            copy = pltpu.make_async_copy(
                g_ref.at[m, :, core + 2 * k if parts > 1 else 0], own.at[m, k], o_sem.at[m, k]
            )
            copy.start()
            locals_[m, k] = copy
    dctx[:, pl.ds(pl.multiple_of(me * block, block), block)] = dctx_ref[
        pl.ds(pl.multiple_of(me * slab, slab), slab), :
    ]

    def after_core(m):
        for k in range(halves):
            locals_[m, k].wait()
            if parts > 1:
                at.arrived(from_core.at[m, k], c_send.at[m, k], c_recv.at[m, k])
        if parts > 1:
            def add(j, carry):
                for k in range(halves):
                    own[m, k, j] = own[m, k, j] + from_core[m, k, j]
                return carry
            lax.fori_loop(0, shards, add, 0)
        if parts == 4:
            at.send(own.at[m, 1 - km], from_y.at[m], y_send.at[m], y_recv.at[m], rep=at.flip(2))

    def after_y(m):
        if parts == 4:
            at.arrived(from_y.at[m], y_send.at[m], y_recv.at[m])
            def add(j, carry):
                own[m, km, j] = own[m, km, j] + from_y[m, j]
                return carry
            lax.fori_loop(0, shards, add, 0)
        for db in range(1, minor):
            for da in range(MAJOR):
                at.send(
                    own.at[m, km, at.at(da, db)], from_x.at[m, db - 1, at.at(da, db) // minor],
                    x_send.at[m, db - 1, da], x_recv.at[m, db - 1, at.at(da, db) // minor],
                    shard=at.at(0, db),
                )

    def after_x(m):
        for da in range(1, MAJOR + 1):
            to = at.at(da, 0)
            ta = to // minor
            total = own[m, km, to].astype(F32)
            for db in range(1, minor):
                at.arrived(from_x.at[m, db - 1, ta], x_send.at[m, db - 1, 0], x_recv.at[m, db - 1, ta])
                total = total + from_x[m, db - 1, ta].astype(F32)
            own[m, km, to] = total.astype(BF16)
            if da < MAJOR:
                at.send(
                    own.at[m, km, to], from_z.at[m, da - 1], z_send.at[m, da - 1], z_recv.at[m, da - 1],
                    shard=to,
                )

    def after_z(m):
        total = own[m, km, me].astype(F32)
        for da in range(1, MAJOR):
            at.arrived(from_z.at[m, da - 1], z_send.at[m, da - 1], z_recv.at[m, da - 1])
            total = total + from_z[m, da - 1].astype(F32)
        fin_ref[mine, m] = total.astype(BF16)

    for m in mats:
        after_core(m)

    for da, db in peers:
        origin = at.at(-da, -db)
        at.arrived(
            dctx.at[:, pl.ds(pl.multiple_of(origin * block, block), block)], d_send.at[0], d_recv.at[origin]
        )

    scales = vec_ref[5:6, :128]
    column = jnp.broadcast_to(scales, (128, 128)).T[:HEAD, 0:1]
    base = QUERY_BASE / math.sqrt(HEAD)
    soft = jnp.maximum(column, 0.0) + jnp.log(1.0 + jnp.exp(-jnp.abs(column)))
    factor = base * soft
    grads[...] = jnp.zeros_like(grads)

    def attend(i):
        reach = (i + 1) * qblock
        span = slice(i * qblock, reach)
        starts = start_ref[0:1, span]
        key_place = lax.broadcasted_iota(jnp.int32, (reach, qblock), 0).astype(F32)
        query_place = (i * qblock + lax.broadcasted_iota(jnp.int32, (1, qblock), 1)).astype(F32)
        allowed = (key_place >= starts) & (key_place <= query_place)
        for h in range(local):
            queries = qkv_ref[h * HEAD : (h + 1) * HEAD, span]
            keys = qkv_ref[slab + h * HEAD : slab + (h + 1) * HEAD, :reach]
            values = qkv_ref[2 * slab + h * HEAD : 2 * slab + (h + 1) * HEAD, :reach]
            gctx = dctx[h * HEAD : (h + 1) * HEAD, span]
            turn = (((0,), (0,)), ((), ()))
            both = (((1,), (1,)), ((), ()))
            scores = lax.dot_general(keys, queries, turn, preferred_element_type=F32)
            probs = jnp.where(allowed, jnp.exp(scores - log_ref[h : h + 1, span]), 0.0)
            gprobs = lax.dot_general(values, gctx, turn, preferred_element_type=F32)
            delta = jnp.sum(probs * gprobs, axis=0, keepdims=True)
            gscores = (probs * (gprobs - delta)).astype(BF16)
            low = probs.astype(BF16)
            grads[h * HEAD : (h + 1) * HEAD, span] = jnp.dot(
                keys, gscores, preferred_element_type=F32
            )
            kv = slice(slab + h * HEAD, slab + (h + 1) * HEAD)
            grads[kv, :reach] += lax.dot_general(queries, gscores, both, preferred_element_type=F32)
            kv = slice(2 * slab + h * HEAD, 2 * slab + (h + 1) * HEAD)
            grads[kv, :reach] += lax.dot_general(gctx, low, both, preferred_element_type=F32)

    steps = length // qblock
    for i in range(steps):
        attend(i)
        if i == steps - 2:
            after_y(mats[0])

    gscale = jnp.zeros((HEAD, 1), F32)
    for h in range(local):
        rows = slice(h * HEAD, (h + 1) * HEAD)
        scaled = grads[rows, :]
        gscale = gscale + jnp.sum(scaled * query_ref[rows, :], axis=1, keepdims=True)
        grads[rows, :] = scaled * factor
    gscale = gscale * (base / (1.0 + jnp.exp(-column)))
    bias_q = jnp.sum(grads[:slab, :], axis=1, keepdims=True)
    bias_v = jnp.sum(grads[2 * slab :, :], axis=1, keepdims=True)
    turned[:slab3, :] = grads[...].astype(BF16)
    proj[...] = turned[...].T[:, :slab3]

    wcols = wcols_ref[...].reshape(width, slab3)
    gain_rows = jnp.zeros((8, width), F32)

    def partial(origin, acc):
        tokens = pl.ds(pl.multiple_of(origin * block, block), block)
        out = lax.dot_general(
            proj[tokens, :], wcols, (((1,), (1,)), ((), ())), preferred_element_type=F32
        )
        part_gn[origin] = out.astype(BF16)
        weighted = out * normed_ref[tokens, :].astype(F32)
        return acc + jnp.sum(weighted.reshape(block // 8, 8, width), axis=0)

    def away(i, acc):
        db = 1 + i // MAJOR
        to = at.at(lax.rem(i + 1, MAJOR), db)
        acc = partial(to, acc)
        pltpu.make_async_remote_copy(
            src_ref=part_gn.at[to], dst_ref=gn_x.at[db - 1, to // minor],
            send_sem=nx_send.at[db - 1, to // minor], recv_sem=nx_recv.at[db - 1, to // minor],
            device_id=(at.at(0, db), at.rep), device_id_type=MESH,
        ).start()
        return acc

    gain_rows = lax.fori_loop(0, shards - MAJOR, away, gain_rows)
    gain_rows = lax.fori_loop(0, MAJOR, lambda i, acc: partial(at.at(i, 0), acc), gain_rows)
    gain_row = jnp.sum(gain_rows, axis=0, keepdims=True) / vec_ref[0:1, :]

    rows = row_ref[...]
    place = lax.broadcasted_iota(jnp.int32, (8, width), 0)
    rows = jnp.where(place == 0, jnp.broadcast_to(gain_row, (8, width)), rows)
    turn_in = jnp.concatenate(
        [jnp.broadcast_to(gscale, (HEAD, 128)), jnp.zeros((128 - HEAD, 128), F32)], axis=0
    )
    scale_row = jnp.broadcast_to(turn_in.T[0:1, :], (8, 128))
    scale_tile = jnp.where(lax.broadcasted_iota(jnp.int32, (8, 128), 0) == 5, scale_row, 0.0)
    for j in range(shards):
        first = j * slab // 128 * 128
        window = rows[:, first : min(first + 384, width)]
        if window.shape[1] < 384:
            window = jnp.concatenate([window, jnp.zeros((8, 384 - window.shape[1]), F32)], axis=1)
        windows[j, :, :384] = window
        windows[j, :, 384:] = scale_tile
    for i, (da, db) in enumerate(peers):
        dest = at.at(da, db)
        at.send(windows.at[dest], small_land.at[me], v_send.at[i], v_recv.at[me], shard=dest)
    small_land[me] = windows[me]

    rp = width // (shards * parts)
    whole = lax.dot_general(
        normed_ref[...], proj[...], (((0,), (0,)), ((), ())), preferred_element_type=F32
    )
    gw[...] = whole.reshape(shards, parts, rp, slab3).astype(BF16)
    for k in range(halves):
        if parts > 1:
            at.send(
                gw.at[:, (1 - core) + 2 * k], gw_core.at[k], wc_send.at[k], wc_recv.at[k], rep=at.flip(1)
            )
    for m in mats[1:]:
        after_y(m)
    for k in range(halves):
        if parts > 1:
            at.arrived(gw_core.at[k], wc_send.at[k], wc_recv.at[k])
            part = core + 2 * k
            gw_core[k] = gw[:, part] + gw_core[k]
    if parts == 4:
        at.send(gw_core.at[1 - km], gw_y, wy_send.at[0], wy_recv.at[0], rep=at.flip(2))

    for da in range(1, MAJOR + 1):
        to = at.at(da, 0)
        ta = to // minor
        total = part_gn[to].astype(F32)
        for db in range(1, minor):
            at.arrived(gn_x.at[db - 1, ta], nx_send.at[db - 1, 0], nx_recv.at[db - 1, ta])
            total = total + gn_x[db - 1, ta].astype(F32)
        if da < MAJOR:
            part_gn[to] = total.astype(BF16)
            at.send(part_gn.at[to], gn_z.at[da - 1], nz_send.at[da - 1], nz_recv.at[da - 1], shard=to)
        else:
            gn_ref[...] = total
    for m in mats:
        after_x(m)

    if parts == 4:
        at.arrived(gw_y, wy_send.at[0], wy_recv.at[0])
        gw_sum[...] = gw_core[km] + gw_y[...]
    elif parts > 1:
        gw_sum[...] = gw_core[0]
    else:
        gw_sum[...] = gw[:, 0]
    for i, (da, db) in enumerate(peers):
        dest = at.at(da, db)
        at.send(gw_sum.at[dest], gw_land.at[me], wa_send.at[i], wa_recv.at[me], shard=dest)
    gw_land[me] = gw_sum[me]

    for da, db in peers:
        origin = at.at(-da, -db)
        at.arrived(small_land.at[origin], v_send.at[0], v_recv.at[origin])
    small = jnp.sum(small_land[...], axis=0)
    sides = jnp.concatenate(
        [
            jnp.where(
                lax.broadcasted_iota(jnp.int32, (slab, 128), 1) == 6,
                bias_q,
                jnp.where(lax.broadcasted_iota(jnp.int32, (slab, 128), 1) == 7, bias_v, 0.0),
            ),
            jnp.zeros((256 - slab, 128), F32),
        ],
        axis=0,
    )
    sides = jnp.concatenate([sides[:128].T[:8], sides[128:].T[:8]], axis=1)
    shift = lax.rem(me * slab, 128)
    window = pltpu.roll(small[:, :384], lax.rem(384 - shift, 384), 1)
    tall = lax.broadcasted_iota(jnp.int32, (8, 256), 0)
    small_got[0, :, :256] = jnp.where(tall < 5, window[:, :256], sides)
    unit = HEAD // shards
    small_got[0, :, 256:] = pltpu.roll(small[:, 384:], lax.rem(128 - me * unit, 128), 1)
    for n, mask in enumerate(every):
        at.send(small_got.at[2 * n], small_got.at[2 * n + 1], b_send.at[n], b_recv.at[n], rep=at.flip(mask))
        at.arrived(small_got.at[2 * n + 1], b_send.at[n], b_recv.at[n])
        small_got[2 * n + 2] = small_got[2 * n] + small_got[2 * n + 1]
    small_ref[...] = small_got[2 * len(every)]

    for m in mats:
        after_z(m)
    for n, mask in enumerate(extras):
        at.send(fin_ref.at[mine], extra.at[n], e_send.at[n], e_recv.at[n], rep=at.flip(mask))
        at.arrived(extra.at[n], e_send.at[n], e_recv.at[n])
        at.started[-1].wait_send()
        at.started.pop()
        fin_ref[mine] = fin_ref[mine] + extra[n]
    for da, db in peers:
        origin = at.at(-da, -db)
        at.arrived(gw_land.at[origin], wa_send.at[0], wa_recv.at[origin])
    gw_ref[mine] = gw_land[...]
    for n, mask in enumerate(extras):
        at.send(gw_ref.at[mine], gw_extra.at[n], we_send.at[n], we_recv.at[n], rep=at.flip(mask))
        at.arrived(gw_extra.at[n], we_send.at[n], we_recv.at[n])
        at.started[-1].wait_send()
        at.started.pop()
        gw_ref[mine] = gw_ref[mine] + gw_extra[n]
    have = [mine]
    rk = 0
    for mask in masks_of(parts):
        for part in have:
            at.send(fin_ref.at[part], fin_ref.at[part], r_send.at[rk], r_recv.at[part], rep=at.flip(mask))
            at.send(gw_ref.at[part], gw_ref.at[part], wr_send.at[rk], wr_recv.at[part], rep=at.flip(mask))
            rk += 1
        fresh = [flipped(part, mask) for part in have]
        for part in fresh:
            at.arrived(fin_ref.at[part], r_send.at[0], r_recv.at[part])
            at.arrived(gw_ref.at[part], wr_send.at[0], wr_recv.at[part])
        have = have + fresh

    total = gn_ref[...]
    for da in range(1, MAJOR):
        at.arrived(gn_z.at[da - 1], nz_send.at[da - 1], nz_recv.at[da - 1])
        total = total + gn_z[da - 1].astype(F32)
    gn_ref[...] = total
    for db in range(1, minor):
        for i in range(MAJOR):
            pltpu.make_async_remote_copy(
                src_ref=part_gn.at[me], dst_ref=part_gn.at[me],
                send_sem=nx_send.at[db - 1, i], recv_sem=nx_recv.at[db - 1, i],
                device_id=(at.at(0, db), at.rep), device_id_type=MESH,
            ).wait_send()
    at.settle()


def back(shards, replicas, grads, dctx, qkv, query, log, start, normed, wcols, vec, rows):
    parts, rp, width = grads.shape[2:]
    slab3, length = qkv.shape
    slab = slab3 // 3
    block = length // shards
    minor = shards // MAJOR
    halves = max(parts // 2, 1)
    peers = shards - 1
    dma = pltpu.SemaphoreType.DMA
    bits = (replicas - 1).bit_length()
    more = max(bits - (parts - 1).bit_length(), 1)
    vm = pltpu.VMEM
    turned_rows = -(-slab3 // 128) * 128
    return pl.pallas_call(
        functools.partial(back_kernel, shards, replicas, parts, 2 * block),
        out_shape=(
            jax.ShapeDtypeStruct((parts, 3, rp, width), BF16),
            jax.ShapeDtypeStruct((parts, shards, rp, slab3), BF16),
            jax.ShapeDtypeStruct((block, width), F32),
            jax.ShapeDtypeStruct((8, 384), F32),
        ),
        in_specs=[ANY] + [VMEM] * 9,
        out_specs=[VMEM] * 4,
        scratch_shapes=[
            vm((slab, length), BF16),
            vm((slab3, length), F32),
            vm((turned_rows, length), BF16),
            vm((length, slab3), BF16),
            vm((3, halves, shards, rp, width), BF16),
            vm((3, halves, shards, rp, width), BF16),
            vm((3, shards, rp, width), BF16),
            vm((3, minor - 1, MAJOR, rp, width), BF16),
            vm((3, MAJOR - 1, rp, width), BF16),
            vm((more, 3, rp, width), BF16),
            vm((shards, block, width), BF16),
            vm((minor - 1, MAJOR, block, width), BF16),
            vm((MAJOR - 1, block, width), BF16),
            vm((shards, parts, rp, slab3), BF16),
            vm((halves, shards, rp, slab3), BF16),
            vm((shards, rp, slab3), BF16),
            vm((shards, rp, slab3), BF16),
            vm((shards, rp, slab3), BF16),
            vm((more, shards, rp, slab3), BF16),
            vm((shards, 8, 512), F32),
            vm((shards, 8, 512), F32),
            vm((2 * bits + 1, 8, 384), F32),
            dma((peers,)), dma((shards,)),
            dma((3, halves)), dma((3, halves)), dma((3, halves)),
            dma((3,)), dma((3,)),
            dma((3, minor - 1, MAJOR)), dma((3, minor - 1, MAJOR)),
            dma((3, MAJOR - 1)), dma((3, MAJOR - 1)),
            dma((max(parts - 1, 1),)), dma((parts,)),
            dma((more,)), dma((more,)),
            dma((minor - 1, MAJOR)), dma((minor - 1, MAJOR)),
            dma((MAJOR - 1,)), dma((MAJOR - 1,)),
            dma((halves,)), dma((halves,)),
            dma((1,)), dma((1,)),
            dma((peers,)), dma((shards,)),
            dma((max(parts - 1, 1),)), dma((parts,)),
            dma((more,)), dma((more,)),
            dma((peers,)), dma((shards,)),
            dma((bits,)), dma((bits,)),
        ],
        compiler_params=pltpu.CompilerParams(
            collective_id=1, has_side_effects=True, vmem_limit_bytes=58 << 20
        ),
        name="back",
    )(grads, dctx, qkv, query, log, start, normed, wcols, vec, rows)


def middle(x, att, keep, weights, vec, cotangent):
    width = x.shape[1]
    w_out, w_up, w_down = weights
    b_out, gain_two, b_up, b_down = vec[1], vec[2], vec[3], vec[4]
    x = x.astype(F32)
    att = att * keep.astype(BF16)[None, :]
    mixed = x + lax.dot_general(att, w_out, (((0,), (0,)), ((), ())), preferred_element_type=F32) + b_out
    r = lax.rsqrt(jnp.mean(mixed * mixed, axis=-1, keepdims=True) + EPS)
    normed = (mixed * r * gain_two).astype(BF16)
    hidden = jnp.dot(normed, w_up, preferred_element_type=F32) + b_up
    s = 1.0 / (1.0 + jnp.exp(-hidden))
    act = (hidden * s).astype(BF16)
    output = (mixed + jnp.dot(act, w_down, preferred_element_type=F32) + b_down).astype(BF16)
    cot = cotangent.astype(F32)
    both = (((1,), (1,)), ((), ()))
    tokens = (((0,), (0,)), ((), ()))
    g_down = lax.dot_general(act, cotangent, tokens, preferred_element_type=F32)
    g_act = lax.dot_general(cotangent, w_down, both, preferred_element_type=F32)
    g_hidden = g_act * (s + hidden * s * (1.0 - s))
    low = g_hidden.astype(BF16)
    g_up = lax.dot_general(normed, low, tokens, preferred_element_type=F32)
    g_normed = lax.dot_general(low, w_up, both, preferred_element_type=F32)
    g_mixed = cot + r * gain_two * g_normed - mixed * (r * r * r) * jnp.mean(
        mixed * gain_two * g_normed, axis=-1, keepdims=True
    )
    g_low = g_mixed.astype(BF16)
    g_out = jnp.dot(att, g_low, preferred_element_type=F32)
    dctx = lax.dot_general(w_out, g_low, both, preferred_element_type=F32).astype(BF16) * keep.astype(BF16)[None, :]
    rows = jnp.stack(
        [jnp.zeros(width, F32), g_mixed.sum(0), (g_normed * mixed * r).sum(0), g_hidden.sum(0), cot.sum(0)]
        + [jnp.zeros(width, F32)] * 3
    )
    grads = jnp.stack([g_out.astype(BF16), g_up.astype(BF16), g_down.astype(BF16)])
    return output, g_mixed, grads, dctx, rows


def on_device(
    inputs, segment_ids, positions, gain_one, w_qkv, b_query, b_value, query_scale, w_out, b_out,
    gain_two, w_up, b_up, w_down, b_down, cotangent,
):
    shards = lax.axis_size("shard")
    replicas = lax.axis_size("replica")
    block, width = inputs.shape[1:]
    slab = width // shards
    x = inputs.reshape(block, width)
    packet, biases, wq, ffn = prepare(
        x, segment_ids, positions, gain_one, w_qkv, b_query, b_value, query_scale, w_out, b_out,
        gain_two, w_up, b_up, w_down, b_down,
    )
    normed, qkv, query, log, att, vec, start, wcols, weights = front(shards, x, packet, biases, wq, ffn)
    shape = weights.shape
    keep = segment_ids.reshape(block) != 0
    output, g_mixed, grads, dctx, rows = middle(
        x, att, keep, weights.reshape(3, width, width), vec, cotangent.reshape(block, width)
    )
    fin, gw, gn, small = back(
        shards, replicas, grads.reshape(shape), dctx, qkv, query, log, start, normed, wcols, vec, rows
    )
    parts, rp = fin.shape[0], fin.shape[2]
    fin = fin.transpose(1, 0, 2, 3).reshape(3, slab, width).astype(F32)
    gw = gw.reshape(parts, shards, rp, 3, slab).transpose(0, 2, 3, 1, 4).reshape(slab, 3 * width).astype(F32)
    xf = x.astype(F32)
    r = lax.rsqrt(jnp.mean(xf * xf, axis=-1, keepdims=True) + EPS)
    gain = vec[0]
    input_grad = g_mixed + r * gain * gn - xf * (r * r * r) * jnp.mean(xf * gain * gn, axis=-1, keepdims=True)
    unit = HEAD // shards
    return (
        output[None], input_grad[None], small[0, :slab], gw, small[6, :slab], small[7, :slab],
        small[5, 256 : 256 + unit], fin[0], small[1, :slab], small[2, :slab], fin[1], small[3, :slab],
        fin[2], small[4, :slab],
    )


def solution(mesh):
    rows = P("replica", "shard", None)
    ids = P("replica", "shard")
    vector = P("shard")
    matrix = P("shard", None)
    in_specs = (
        rows, ids, ids, vector, matrix, vector, vector, vector, matrix, vector, vector, matrix, vector,
        matrix, vector, rows,
    )
    out_specs = (
        rows, rows, vector, matrix, vector, vector, vector, matrix, vector, vector, matrix, vector, matrix,
        vector,
    )
    return jax.shard_map(on_device, mesh=mesh, in_specs=in_specs, out_specs=out_specs, check_vma=False)
```

time: 1420 us -> 353 us (0.25)
  waiting for transfers between devices: 1040 us -> 0 us
  Pallas kernels: 0 us -> 280 us
  starting transfers between devices: 113 us -> 0 us
  matrix products: 96.2 us -> 10.4 us
  blocking collectives: 81.7 us -> 0 us
  between operations: 18.4 us -> 0.91 us
    reduce_scatter x4 -> x0, waiting for transfers between devices: 554 us -> none  [the longest x1 328 us: on_device(): lax.psum_scatter(jnp.einsum('td,tc->dc', normed_low, grad_projected_low,...]
    pallas_call x0 -> x2, Pallas kernels: none -> 280 us  [the longest x1 152 us: back(): pl.pallas_call(functools.partial(back_kernel, shards, replicas, parts, 2...]
    ppermute x28 -> x0, waiting for transfers between devices: 271 us -> none  [passed_along(): return lax.ppermute(shard, axis, pairs)]
    all_gather x4 -> x0, waiting for transfers between devices: 172 us -> none  [the longest x1 90.6 us: on_device(): lax.all_gather(w_qkv, 'shard', axis=0, tiled=True)]
    ppermute x28 -> x0, starting transfers between devices: 112 us -> none  [passed_along(): return lax.ppermute(shard, axis, pairs)]
    dot_general x60 -> x9, matrix products: 96.2 us -> 10.4 us  [the longest x1 1.76 us: middle(): lax.dot_general(w_out, g_low, both, preferred_element_type=F32).astype(BF16)]
    unnamed x2 -> x0, blocking collectives: 75.4 us -> none
    psum x1 -> x0, waiting for transfers between devices: 43.7 us -> none  [on_device(): lax.psum((grad_qkv_share, shares[0], shares[1], shares[2], shares[3], sha...]
  transfers between devices with their start and end apart: 37 -> 0, of which waited for: 15 -> 0; matrix products, arithmetic and copies ran while one was open for 10% -> 0% of each run, Pallas kernels for 0% -> 0%
where the time goes in v1:
time: 353 us; the launch traced here: 352 us
  Pallas kernels  280 us (79%)
  local copies, waits for them, and re-layouts  44.4 us (13%)
  other arithmetic  16.3 us (5%)
  matrix products  10.4 us (3%)
    pallas_call x1, Pallas kernels, back(): pl.pallas_call(functools.partial(back_kernel, shards, replicas, parts, 2...  152 us
    pallas_call x1, Pallas kernels, front(): pl.pallas_call(functools.partial(front_kernel, shards, wparts, fparts, qb...  127 us
    convert_element_type x3, local copies, waits for them, and re-layouts, on_device(): gw.reshape(parts, shards, rp, 3, slab).transpose(0, 2, 3, 1, 4)  16.4 us
    reshape x2, local copies, waits for them, and re-layouts, prepare(): wq = w_qkv.reshape(slab, 3, shards, slab).transpose(2, 0, 1, 3).reshape(s...  8.35 us

profile of v1, /device:TPU:0, one launch (start us, length us, event | category | flops | bytes accessed | tf_op | source)
XLA Modules:
  0.0 351.6 jit_solution(978466201141424736)
XLA Ops:
  0.7 0.8 fusion.27
  1.4 0.7 fusion.26
  3.4 0.7 stack.91
  4.7 0.7 pad_convert_fusion.3
  8.1 0.8 copy.46.bias_ref
  8.8 2.4 pad_maximum_fusion.1.ffn_ref
  11.3 3.5 reshape.117
  14.8 3.2 copy.45
  18.0 2.4 reshape.118
  20.4 6.0 %copy.47.wq_ref = bf16[8,2,80,480]{3,2,1,0:T(8,128)(2,1)} copy(bf16[8,2,80,480]{2,1,3,0:T(2,128)(2,1)} %reshape.118) | data formatting | bytes 2457600 | tf_op jit(solution)/shard_map/reshape | solution.py:408
  26.3 127.2 %front.1 = (bf16[1024,1280]{1,0:T(8,128)(2,1)}, bf16[480,1024]{1,0:T(8,128)(2,1)}, f32[160,1024]{1,0:T(8,128)}, f32[8,1024]{1,0:T(8,128)}, bf16[1280,128]{1,0:T(...) custom-call(bf16[128,1280]{1,0:T(8,128)(2,1)} %bitcast.88, ...), custom_call_target="tpu_custom_call" | custom-call | tf_op jit(solution)/shard_map/front/pallas_call | solution.py:359
  153.5 4.4 %fusion.32 = (bf16[1,8,4,40,1280]{4,3,2,1,0:T(8,128)(2,1)S(1)}, bf16[1,8,4,40,1280]{4,3,2,1,0:T(8,128)(2,1)S(1)}, bf16[1,8,4,40,1280]{4,3,2,1,0:T(8,128)(2,1)S(1)}) fusion(bf16[3,8,4,40,1280]{4,3,2,1,0:T(8,128)(2,1)} %get-tuple-element.28), kind=kLoop, calls=%fused_computation.71 | loop fusion | bytes 19660800 | tf_op jit(solution)/shard_map/unstack | solution.py:832
  158.1 0.8 multiply_reduce_fusion.2
  158.9 0.7 convolution_add_fusion.1
  159.6 1.4 fusion.5
  161.0 1.2 fusion.35
  162.3 1.3 multiply_reduce_fusion
  163.9 1.8 fusion.4.dctx_ref
  165.7 0.7 stack.107.row_ref
  166.4 1.1 convolution_convert_fusion.1
  167.5 1.1 convolution_convert_fusion
  168.6 1.0 convolution_convert_fusion.2
  169.6 4.5 %pad_maximum_fusion.g_ref = bf16[3,8,4,40,1280]{4,3,2,1,0:T(8,128)(2,1)} fusion(bf16[1,8,4,40,1280]{4,3,2,1,0:T(8,128)(2,1)S(1)} %bitcast.85, bf16[1,8,4,40,1280]{4,3,2,1,0:T(8,128)(2,1)S(1)} %bitcast.84, bf16[1,8,4,40,1280]{4,3,2,1,0:T(8,128)(2,1)S(1)} %bitcast.86), kind=kLoop, calls=%fused_computation | loop fusion | flops 9830400 | bytes 19660800 | tf_op jit(solution)/shard_map/stack | solution.py:862
  174.1 152.4 %back.1 = (bf16[4,3,40,1280]{3,2,1,0:T(8,128)(2,1)}, bf16[4,8,40,480]{3,2,1,0:T(8,128)(2,1)}, f32[128,1280]{1,0:T(8,128)}, f32[8,384]{1,0:T(8,128)}) custom-call(bf16[3,8,4,40,1280]{4,3,2,1,0:T(8,128)(2,1)} %pad_maximum_fusion.g_ref, bf16[1280,128]{1,0:T(8,128)(2,1)} %fusion.4.dctx_ref, bf16[480,1024]{1,0:T(8,128)(2,1)} %get-tuple-element.30.qkv_ref, ...), custom_call_target="tpu_custom_call" | custom-call | tf_op jit(solution)/shard_map/back/pallas_call | solution.py:773
  326.5 1.3 slice_bitcast_fusion
  327.8 1.5 fusion.34
  329.4 1.3 fusion.7
  330.7 2.2 fusion.10
  333.1 1.5 fusion.33
  335.2 4.7 %reshape.128 = f32[4,8,40,3,160]{4,3,2,1,0:T(4,128)} reshape(bf16[4,8,40,480]{3,2,1,0:T(8,128)(2,1)S(1)} %copy-done.3) | data formatting | bytes 3686400 | tf_op jit(solution)/shard_map/convert_element_type | solution.py:890
  339.9 6.7 %copy.48 = f32[4,40,3,8,160]{4,3,2,1,0:T(8,128)} copy(f32[4,40,3,8,160]{4,2,1,3,0:T(4,128)} %bitcast.83) | data formatting | bytes 4915200 | tf_op jit(solution)/shard_map/convert_element_type | solution.py:890
  346.6 5.0 %reshape.127 = f32[160,3840]{1,0:T(8,128)} reshape(f32[4,40,3,8,160]{4,3,2,1,0:T(8,128)} %copy.48) | data formatting | bytes 4915200 | tf_op jit(solution)/shard_map/convert_element_type | solution.py:890
  (38 shorter events, 5.9 us)
Async XLA Ops:
  0.6 10.6 %copy-start.4 = (bf16[160,3840]{1,0:T(8,128)(2,1)S(1)}, bf16[160,3840]{1,0:T(8,128)(2,1)}, u32[]{:S(2)}) copy-start(bf16[160,3840]{1,0:T(8,128)(2,1)} %param.20) | copy-start | bytes 3686404
  153.5 4.5 %copy-start.6 = (f32[8,1280]{1,0:T(8,128)S(1)}, f32[8,1280]{1,0:T(8,128)}, u32[]{:S(2)}) copy-start(f32[8,1280]{1,0:T(8,128)} %get-tuple-element.29.vec_ref) | copy-start | bytes 122884
  153.5 4.5 %copy-start = (bf16[1,128,1280]{2,1,0:T(8,128)(2,1)S(1)}, bf16[1,128,1280]{2,1,0:T(8,128)(2,1)}, u32[]{:S(2)}) copy-start(bf16[1,128,1280]{2,1,0:T(8,128)(2,1)} %param.16) | copy-start | bytes 983044
  153.5 4.5 %copy-start.1 = (bf16[1280,128]{1,0:T(8,128)(2,1)S(1)}, bf16[1280,128]{1,0:T(8,128)(2,1)}, u32[]{:S(2)}) copy-start(bf16[1280,128]{1,0:T(8,128)(2,1)} %get-tuple-element.27) | copy-start | bytes 983044
  159.6 1.5 copy-start.2
  326.5 6.4 %copy-start.5 = (bf16[4,3,40,1280]{3,2,1,0:T(8,128)(2,1)S(1)}, bf16[4,3,40,1280]{3,2,1,0:T(8,128)(2,1)}, u32[]{:S(2)}) copy-start(bf16[4,3,40,1280]{3,2,1,0:T(8,128)(2,1)} %get-tuple-element.39) | copy-start | bytes 3686404
  333.1 2.1 copy-start.3

commit v2 on v1

--- a/solution.py
+++ b/solution.py
@@ -10,7 +10,6 @@
 
 HEADS = 16
 HEAD = 80
-DOC_MAX = 800
 EPS = 1e-06
 QUERY_BASE = 1.442695041
 MASKED = -1000000000.0
@@ -20,6 +19,13 @@
 ANY = pl.BlockSpec(memory_space=pl.ANY)
 F32 = jnp.float32
 BF16 = jnp.bfloat16
+NN = (((1,), (0,)), ((), ()))
+NT = (((1,), (1,)), ((), ()))
+TN = (((0,), (0,)), ((), ()))
+
+
+def dot(lhs, rhs, dims=NN):
+    return lax.dot_general(lhs, rhs, dims, preferred_element_type=F32)
 
 
 class Place:
@@ -37,28 +43,26 @@
         b = lax.rem(self.b + db + self.minor, self.minor)
         return a * self.minor + b
 
+    def peers(self):
+        return [(da, db) for da in range(MAJOR) for db in range(self.minor) if da or db]
+
     def flip(self, mask):
         bit = lax.rem(self.rep // mask, 2)
         return self.rep + mask - 2 * mask * bit
 
     def greet(self, masks):
         barrier = pltpu.get_barrier_semaphore()
-        count = 0
-        for da in range(MAJOR):
-            for db in range(self.minor):
-                if da or db:
-                    pl.semaphore_signal(
-                        barrier, inc=1, device_id=(self.at(da, db), self.rep), device_id_type=MESH
-                    )
-                    count += 1
+        for da, db in self.peers():
+            pl.semaphore_signal(
+                barrier, inc=1, device_id=(self.at(da, db), self.rep), device_id_type=MESH
+            )
         for mask in masks:
             pl.semaphore_signal(
                 barrier, inc=1, device_id=(self.me, self.flip(mask)), device_id_type=MESH
             )
-            count += 1
-        pl.semaphore_wait(barrier, count)
-
-    def send(self, src, dst, ssem, rsem, shard=None, rep=None):
+        pl.semaphore_wait(barrier, len(self.peers()) + len(masks))
+
+    def send(self, src, dst, ssem, rsem, shard=None, rep=None, when=None):
         copy = pltpu.make_async_remote_copy(
             src_ref=src,
             dst_ref=dst,
@@ -67,122 +71,220 @@
             device_id=(self.me if shard is None else shard, self.rep if rep is None else rep),
             device_id_type=MESH,
         )
-        copy.start()
-        self.started.append(copy)
-        return copy
-
-    def arrived(self, dst, ssem, rsem):
+        if when is None:
+            copy.start()
+        else:
+            @pl.when(when)
+            def _():
+                copy.start()
+        self.started.append((when, copy))
+
+    def arrived(self, dst, rsem):
         pltpu.make_async_remote_copy(
             src_ref=dst,
             dst_ref=dst,
-            send_sem=ssem,
+            send_sem=rsem,
             recv_sem=rsem,
             device_id=(self.me, self.rep),
             device_id_type=MESH,
         ).wait_recv()
 
     def settle(self):
-        for copy in self.started:
-            copy.wait_send()
+        for when, copy in self.started:
+            if when is None:
+                copy.wait_send()
+            else:
+                @pl.when(when)
+                def _():
+                    copy.wait_send()
         self.started = []
 
 
-def masks_of(parts):
-    return {4: (2, 1), 2: (1,), 1: ()}[parts]
-
-
-def others(place):
-    return [(da, db) for da in range(MAJOR) for db in range(place.minor) if da or db]
+class Line:
+    def __init__(self, at, slot, major_send, minor_send, recv):
+        self.at, self.slot = at, slot
+        self.major_send, self.minor_send, self.recv = major_send, minor_send, recv
+
+    def onward(self, origin, up, down, d):
+        at = self.at
+        if up is not None:
+            at.send(
+                self.slot(origin), self.slot(origin), self.major_send.at[0, d], self.recv(origin),
+                shard=lax.min(at.a + 1, MAJOR - 1) * at.minor + at.b, when=up,
+            )
+        if down is not None:
+            at.send(
+                self.slot(origin), self.slot(origin), self.major_send.at[1, d], self.recv(origin),
+                shard=lax.max(at.a - 1, 0) * at.minor + at.b, when=down,
+            )
+
+    def across(self, origin, when=None):
+        at = self.at
+        for db in range(1, at.minor):
+            at.send(
+                self.slot(origin), self.slot(origin), self.minor_send.at[origin // at.minor, db - 1],
+                self.recv(origin), shard=at.at(0, db), when=when,
+            )
+
+    def begin(self):
+        at = self.at
+        self.onward(at.me, at.a + 1 < MAJOR, at.a > 0, 0)
+        self.across(at.me)
+
+    def step(self, d, then=None):
+        at = self.at
+        for side in (-1, 1):
+            ok = (at.a - d >= 0) if side < 0 else (at.a + d < MAJOR)
+            origin = lax.max(at.a - d, 0) if side < 0 else lax.min(at.a + d, MAJOR - 1)
+            origin = origin * at.minor + at.b
+
+            @pl.when(ok)
+            def _():
+                at.arrived(self.slot(origin), self.recv(origin))
+
+            if d + 1 < MAJOR:
+                if side < 0:
+                    self.onward(origin, ok & (at.a + 1 < MAJOR), None, d)
+                else:
+                    self.onward(origin, None, ok & (at.a > 0), d)
+            self.across(origin, when=ok)
+            if then is not None:
+                then(origin, ok)
+
+
+def parts_of(rows):
+    return 4 if rows % 32 == 0 else 2
+
+
+def part_box(part, parts, rows, cols):
+    if parts == 4:
+        i, j, rows = lax.rem(part, 2), part // 2, rows // 2
+    else:
+        i, j = 0, part
+    return i * rows, rows, j * (cols // 2), cols // 2
+
+
+def flipped(part, mask):
+    bit = lax.rem(part // mask, 2)
+    return part + mask - 2 * mask * bit
 
 
 def front_kernel(
     shards, wparts, fparts, qblock,
-    x_ref, packet_ref, bias_ref, wq_ref, ffn_ref,
-    normed_ref, qkv_ref, query_ref, log_ref, att_ref, vec_ref, start_ref, wcols_ref, ffn_out,
-    xg, packets, turned, context,
-    x_send, x_recv, p_send, p_recv, w_send, w_recv, f_send, f_recv, f_local, a_send, a_recv,
+    x_ref, small_ref, w_ref, wout_ref, wup_ref, wdown_ref, cot_ref,
+    normed_ref, qkv_ref, query_ref, log_ref, vec_ref, start_ref, wcols_ref,
+    out_ref, gmixed_ref, xt_ref, dy_ref, dctx_ref, row_ref,
+    xg, packets, pieces, turned, context, att, weights,
+    xm_send, xn_send, x_recv, p_send, p_recv, w_send, w_recv, wc_send,
+    fm_send, fn_send, f_recv, fy_send, fc_send, local_sem, a_send, a_recv,
 ):
     at = Place(shards)
     me, minor = at.me, at.minor
     block, width = x_ref.shape
     length = shards * block
     slab = width // shards
+    slab3 = 3 * slab
     local = slab // HEAD
-    peers = others(at)
-    fmasks = masks_of(fparts)
-    wmasks = masks_of(wparts)
-    at.greet(tuple(sorted(set(fmasks) | set(wmasks))))
+    peers = at.peers()
+    masks = (2, 1) if fparts == 4 else (1,)
     fpart = lax.rem(at.rep, fparts)
     wpart = lax.rem(at.rep, wparts)
 
+    loads = []
+    for m, ref in enumerate((wout_ref, wup_ref, wdown_ref)):
+        copy = pltpu.make_async_copy(
+            ref, weights.at[m, pl.ds(pl.multiple_of(me * slab, 16), slab), :], local_sem.at[m]
+        )
+        copy.start()
+        loads.append(copy)
+    xg[me] = x_ref[...]
+    packets[me] = small_ref[:8]
+    at.greet(masks)
+
+    def wslot(origin, part):
+        row, rows, col, cols = part_box(part, fparts, slab, width)
+        return weights.at[
+            :,
+            pl.ds(pl.multiple_of(origin * slab + row, 16), rows),
+            pl.ds(pl.multiple_of(col, 128), cols),
+        ]
+
+    rows_line = Line(at, lambda o: xg.at[o], xm_send, xn_send, lambda o: x_recv.at[o])
+    ffn_line = Line(
+        at, lambda o: wslot(o, fpart), fm_send, fn_send, lambda o: f_recv.at[o, fpart]
+    )
+
+    def to_replicas(origin, when=None):
+        slot = wslot(origin, fpart)
+        for mask in masks:
+            sem = fy_send.at[origin] if mask == 2 else fc_send.at[origin, 0]
+            at.send(slot, slot, sem, f_recv.at[origin, fpart], rep=at.flip(mask), when=when)
+
+    rows_line.begin()
     for i, (da, db) in enumerate(peers):
-        at.send(packet_ref, packets.at[me], p_send.at[i], p_recv.at[me], shard=at.at(da, db))
-    xg[me] = x_ref[...]
-    packets[me] = packet_ref[...]
-    k = 0
-    for da in range(1, MAJOR):
-        at.send(xg.at[me], xg.at[me], x_send.at[k], x_recv.at[me], shard=at.at(da, 0))
-        k += 1
-    for db in range(1, minor):
-        at.send(xg.at[me], xg.at[me], x_send.at[k], x_recv.at[me], shard=at.at(0, db))
-        k += 1
+        at.send(packets.at[me], packets.at[me], p_send.at[i], p_recv.at[me], shard=at.at(da, db))
+    for copy in loads:
+        copy.wait()
+    ffn_line.begin()
+
+    cut = slab // wparts
+    for j in range(shards):
+        for t in range(3):
+            first = t * width + j * slab
+            pieces[j, :, :, t * slab : (t + 1) * slab] = w_ref[:, first : first + slab].reshape(
+                wparts, cut, slab
+            )
     for i, (da, db) in enumerate(peers):
         dest = at.at(da, db)
         at.send(
-            wq_ref.at[dest, wpart], wcols_ref.at[me, wpart], w_send.at[i], w_recv.at[me, wpart], shard=dest
+            pieces.at[dest, wpart], wcols_ref.at[me, wpart], w_send.at[i], w_recv.at[me, wpart], shard=dest
         )
-    own = pltpu.make_async_copy(wq_ref.at[me], wcols_ref.at[me], f_local.at[0])
-    own.start()
-    own_ffn = pltpu.make_async_copy(ffn_ref, ffn_out.at[:, me], f_local.at[1])
-    own_ffn.start()
-    fk = 0
-    for db in range(1, minor):
-        at.send(
-            ffn_ref.at[:, fpart], ffn_out.at[:, me, fpart], f_send.at[fk], f_recv.at[me, fpart],
-            shard=at.at(0, db),
-        )
-        fk += 1
-
-    for da in range(1, MAJOR):
-        origin = at.at(-da, 0)
-        at.arrived(xg.at[origin], x_send.at[0], x_recv.at[origin])
+    wcols_ref[me] = pieces[me]
+
+    rows_line.step(1)
+    ffn_line.step(1, to_replicas)
+
+    def ffn_minor(distance):
         for db in range(1, minor):
-            at.send(xg.at[origin], xg.at[origin], x_send.at[k], x_recv.at[origin], shard=at.at(0, db))
-            k += 1
-    for da in range(1, MAJOR):
-        at.send(
-            ffn_ref.at[:, fpart], ffn_out.at[:, me, fpart], f_send.at[fk], f_recv.at[me, fpart],
-            shard=at.at(da, 0),
-        )
-        fk += 1
-
-    wk = len(peers)
-    for mask in wmasks:
-        for da, db in peers:
+            sides = ((-1, 1) if distance else (0,))
+            for side in sides:
+                a = at.a + side * distance
+                ok = None
+                if distance:
+                    ok = (a >= 0) & (a < MAJOR)
+                origin = lax.max(lax.min(a, MAJOR - 1), 0) * minor + lax.rem(at.b + db, minor)
+                slot = wslot(origin, fpart)
+                if ok is None:
+                    at.arrived(slot, f_recv.at[origin, fpart])
+                else:
+                    @pl.when(ok)
+                    def _():
+                        at.arrived(slot, f_recv.at[origin, fpart])
+                to_replicas(origin, ok)
+
+    ffn_minor(0)
+
+    if wparts == 2:
+        for i, (da, db) in enumerate(peers):
             origin = at.at(-da, -db)
             slot = wcols_ref.at[origin, wpart]
-            at.arrived(slot, w_send.at[0], w_recv.at[origin, wpart])
-            at.send(slot, slot, w_send.at[wk], w_recv.at[origin, wpart], rep=at.flip(mask))
-            wk += 1
+            at.arrived(slot, w_recv.at[origin, wpart])
+            at.send(slot, slot, wc_send.at[i], w_recv.at[origin, wpart], rep=at.flip(1))
+
     for da, db in peers:
         origin = at.at(-da, -db)
-        last = wparts - 1 - wpart
-        at.arrived(wcols_ref.at[origin, last], w_send.at[0], w_recv.at[origin, last])
-    own.wait()
-    turned[...] = wcols_ref[...].reshape(width, 3 * slab).T
-
-    for da, db in peers:
-        origin = at.at(-da, -db)
-        at.arrived(packets.at[origin], p_send.at[0], p_recv.at[origin])
+        at.arrived(packets.at[origin], p_recv.at[origin])
     vectors = jnp.zeros((8, width), F32)
     scales = jnp.zeros((1, 128), F32)
     lanes = lax.broadcasted_iota(jnp.int32, (8, width), 1)
+    unit = HEAD // shards
     for j in range(shards):
         piece = packets[j]
         wide = jnp.concatenate([piece, jnp.zeros((8, width - piece.shape[1]), F32)], axis=1)
         wide = jnp.where(lanes < slab, wide, 0.0)
         vectors = vectors + (pltpu.roll(wide, j * slab, 1) if j else wide)
-        scales = scales + piece[5:6, :128]
+        scale = jnp.where(lanes[0:1, :128] < unit, piece[5:6, :128], 0.0)
+        scales = scales + (pltpu.roll(scale, j * unit, 1) if j else scale)
         start_ref[:, j * block : (j + 1) * block] = jnp.broadcast_to(piece[6:7, :block], (8, block))
     rows = lax.broadcasted_iota(jnp.int32, (8, width), 0)
     vec_ref[...] = jnp.where(rows < 5, vectors, 0.0)
@@ -191,8 +293,20 @@
     column = jnp.broadcast_to(scales, (128, 128)).T[:HEAD, 0:1]
     soft = jnp.maximum(column, 0.0) + jnp.log(1.0 + jnp.exp(-jnp.abs(column)))
     factor = jnp.concatenate([QUERY_BASE / math.sqrt(HEAD) * soft] * local, axis=0)
-    bias_query = bias_ref[:, 0:1]
-    bias_value = bias_ref[:, 1:2]
+    own = small_ref[8:16, :]
+    tall = jnp.concatenate([own, jnp.zeros((120, 256), F32)], axis=0)
+    tall = jnp.concatenate([tall[:, :128].T, tall[:, 128:].T], axis=0)
+    bias_query = tall[:slab, 0:1]
+    bias_value = tall[:slab, 1:2]
+
+    rows_line.step(2)
+    ffn_line.step(2, to_replicas)
+    ffn_minor(1)
+    for da, db in peers:
+        origin = at.at(-da, -db)
+        last = wparts - 1 - wpart
+        at.arrived(wcols_ref.at[origin, last], w_recv.at[origin, last])
+    turned[...] = wcols_ref[...].reshape(width, slab3).T
 
     def project(origin):
         rows_in = xg[origin].astype(F32)
@@ -200,27 +314,30 @@
         normed = (rows_in * scale * gain).astype(BF16)
         tokens = pl.ds(pl.multiple_of(origin * block, block), block)
         normed_ref[tokens, :] = normed
-        out = lax.dot_general(
-            turned[...], normed, (((1,), (1,)), ((), ())), preferred_element_type=F32
-        )
+        out = dot(turned[...], normed, NT)
         query = out[:slab] + bias_query
         query_ref[:, tokens] = query
         qkv_ref[:slab, tokens] = (query * factor).astype(BF16)
         qkv_ref[slab : 2 * slab, tokens] = out[slab : 2 * slab].astype(BF16)
         qkv_ref[2 * slab :, tokens] = (out[2 * slab :] + bias_value).astype(BF16)
 
+    rows_line.step(3)
+    ffn_line.step(3, to_replicas)
+
     def project_major(i, carry):
-        project(at.at(-i, 0))
+        project(at.at(i, 0))
         return carry
 
     def project_minor(i, carry):
-        origin = at.at(-lax.rem(i, MAJOR), -(1 + i // MAJOR))
-        at.arrived(xg.at[origin], x_send.at[0], x_recv.at[origin])
+        origin = at.at(lax.rem(i, MAJOR), 1 + i // MAJOR)
+        at.arrived(xg.at[origin], x_recv.at[origin])
         project(origin)
         return carry
 
     lax.fori_loop(0, MAJOR, project_major, 0)
+    ffn_minor(2)
     lax.fori_loop(0, shards - MAJOR, project_minor, 0)
+    ffn_minor(3)
 
     log_ref[...] = jnp.zeros_like(log_ref)
     for i in range(length // qblock):
@@ -235,185 +352,149 @@
             queries = qkv_ref[h * HEAD : (h + 1) * HEAD, span]
             keys = qkv_ref[slab + h * HEAD : slab + (h + 1) * HEAD, :reach]
             values = qkv_ref[2 * slab + h * HEAD : 2 * slab + (h + 1) * HEAD, :reach]
-            scores = lax.dot_general(
-                keys, queries, (((0,), (0,)), ((), ())), preferred_element_type=F32
-            )
-            scores = jnp.where(allowed, scores, MASKED)
+            scores = jnp.where(allowed, dot(keys, queries, TN), MASKED)
             top = jnp.max(scores, axis=0, keepdims=True)
             powers = jnp.exp(scores - top)
             total = jnp.sum(powers, axis=0, keepdims=True)
             probs = (powers * (1.0 / total)).astype(BF16)
             log_ref[h : h + 1, span] = top + jnp.log(total)
-            context[head, span] = jnp.dot(values, probs, preferred_element_type=F32).astype(BF16)
+            context[head, span] = dot(values, probs).astype(BF16)
+        mine = pl.ds(pl.multiple_of(me * slab, 16), slab)
         for j in range(i * qblock // block, reach // block):
-            @pl.when(me != j)
-            def _():
-                pltpu.make_async_remote_copy(
-                    src_ref=context.at[:, j * block : (j + 1) * block],
-                    dst_ref=att_ref.at[pl.ds(pl.multiple_of(me * slab, slab), slab), :],
-                    send_sem=a_send.at[j],
-                    recv_sem=a_recv.at[me],
-                    device_id=(j, at.rep),
-                    device_id_type=MESH,
-                ).start()
+            piece = slice(j * block, (j + 1) * block)
+            at.send(context.at[:, piece], att.at[mine, :], a_send.at[j], a_recv.at[me], shard=j, when=me != j)
 
             @pl.when(me == j)
             def _():
-                att_ref[pl.ds(pl.multiple_of(me * slab, slab), slab), :] = context[
-                    :, j * block : (j + 1) * block
-                ]
-
-    def share(origin, have, mask, fk):
-        for part in have:
-            slot = ffn_out.at[:, origin, part]
-            at.send(slot, slot, f_send.at[fk], f_recv.at[origin, part], rep=at.flip(mask))
-            fk += 1
-        return fk
-
-    def flipped(part, mask):
-        bit = lax.rem(part // mask, 2)
-        return part + mask - 2 * mask * bit
-
-    own_parts = [fpart]
-    for da in range(1, MAJOR):
-        origin = at.at(-da, 0)
-        slot = ffn_out.at[:, origin, fpart]
-        at.arrived(slot, f_send.at[0], f_recv.at[origin, fpart])
-        for db in range(1, minor):
-            at.send(slot, slot, f_send.at[fk], f_recv.at[origin, fpart], shard=at.at(0, db))
-            fk += 1
-        for mask in fmasks:
-            fk = share(origin, own_parts, mask, fk)
-    for db in range(1, minor):
-        for da in range(MAJOR):
-            origin = at.at(-da, -db)
-            slot = ffn_out.at[:, origin, fpart]
-            at.arrived(slot, f_send.at[0], f_recv.at[origin, fpart])
-            for mask in fmasks:
-                fk = share(origin, own_parts, mask, fk)
-    order = [(da, 0) for da in range(1, MAJOR)]
-    order += [(da, db) for db in range(1, minor) for da in range(MAJOR)]
-    got = []
-    for n, mask in enumerate(fmasks):
-        fresh = [flipped(part, mask) for part in own_parts + got]
+                att[mine, :] = context[:, piece]
+
+    order = [(0, db) for db in range(1, minor)]
+    order += [(da, db) for da in range(1, MAJOR) for db in range(minor)]
+    if fparts == 4:
         for da, db in order:
-            origin = at.at(-da, -db)
-            for part in fresh:
-                at.arrived(ffn_out.at[:, origin, part], f_send.at[0], f_recv.at[origin, part])
-            for later in fmasks[n + 1 :]:
-                fk = share(origin, fresh, later, fk)
-        got = got + fresh
+            origin = at.at(da, db)
+            part = flipped(fpart, 2)
+            slot = wslot(origin, part)
+            at.arrived(slot, f_recv.at[origin, part])
+            at.send(slot, slot, fc_send.at[origin, 1], f_recv.at[origin, part], rep=at.flip(1))
     for da, db in peers:
         origin = at.at(-da, -db)
-        at.arrived(
-            att_ref.at[pl.ds(pl.multiple_of(origin * slab, slab), slab), :],
-            a_send.at[0],
-            a_recv.at[origin],
-        )
-    own_ffn.wait()
-    for j in range(shards):
-        @pl.when(me != j)
-        def _():
-            pltpu.make_async_remote_copy(
-                src_ref=context.at[:, j * block : (j + 1) * block],
-                dst_ref=context.at[:, j * block : (j + 1) * block],
-                send_sem=a_send.at[j],
-                recv_sem=a_recv.at[0],
-                device_id=(j, at.rep),
-                device_id_type=MESH,
-            ).wait_send()
+        at.arrived(att.at[pl.ds(pl.multiple_of(origin * slab, 16), slab), :], a_recv.at[origin])
+    others = [flipped(fpart, 1)] + ([flipped(flipped(fpart, 1), 2)] if fparts == 4 else [])
+    for da, db in order:
+        origin = at.at(da, db)
+        for part in others:
+            at.arrived(wslot(origin, part), f_recv.at[origin, part])
+
+    keep_row = small_ref[10:11, :block]
+    b_out, gain_two, b_up, b_down = (vec_ref[i : i + 1, :] for i in range(1, 5))
+    att_t = (att[...].astype(F32) * keep_row).astype(BF16)
+    halves = xt_ref.shape[2]
+    xt_ref[0] = att_t.reshape(shards, halves, slab // halves, block)
+    mixed = x_ref[...].astype(F32) + dot(att_t.T, weights[0]) + b_out
+    r = lax.rsqrt(jnp.mean(mixed * mixed, axis=-1, keepdims=True) + EPS)
+    normed_two = (mixed * r * gain_two).astype(BF16)
+    xt_ref[1] = normed_two.T.reshape(shards, halves, slab // halves, block)
+    hidden = dot(normed_two, weights[1]) + b_up
+    s = 1.0 / (1.0 + jnp.exp(-hidden))
+    act = (hidden * s).astype(BF16)
+    xt_ref[2] = act.T.reshape(shards, halves, slab // halves, block)
+    out_ref[...] = (mixed + dot(act, weights[2]) + b_down).astype(BF16)
+    dy_ref[2] = cot_ref[...]
+    cot = cot_ref[...].astype(F32)
+    g_hidden = dot(cot_ref[...], weights[2], NT) * (s + hidden * s * (1.0 - s))
+    low = g_hidden.astype(BF16)
+    dy_ref[1] = low
+    g_normed = dot(low, weights[1], NT)
+    weighted = gain_two * g_normed
+    g_mixed = cot + r * weighted - mixed * (r * r * r) * jnp.mean(mixed * weighted, axis=-1, keepdims=True)
+    gmixed_ref[...] = g_mixed
+    low = g_mixed.astype(BF16)
+    dy_ref[0] = low
+    dctx_ref[...] = (dot(weights[0], low, NT).astype(BF16).astype(F32) * keep_row).astype(BF16)
+    row_ref[...] = jnp.zeros_like(row_ref)
+    row_ref[1:2, :] = jnp.sum(g_mixed, axis=0, keepdims=True)
+    row_ref[2:3, :] = jnp.sum(g_normed * mixed * r, axis=0, keepdims=True)
+    row_ref[3:4, :] = jnp.sum(g_hidden, axis=0, keepdims=True)
+    row_ref[4:5, :] = jnp.sum(cot, axis=0, keepdims=True)
     at.settle()
 
 
-def parts_of(rows, unit, most):
-    parts = most
-    while parts > 1 and rows % (parts * unit):
-        parts //= 2
-    return parts
-
-
-def front(shards, inputs, packet, biases, wq, ffn):
+def front(shards, inputs, small, w_qkv, w_out, w_up, w_down, cotangent):
     block, width = inputs.shape
     slab = width // shards
     length = shards * block
-    local = slab // HEAD
-    wparts = wq.shape[1]
-    fparts = ffn.shape[1]
+    wparts = 2 if slab % 32 == 0 else 1
+    fparts = parts_of(slab)
+    halves = 2 if fparts == 4 else 1
     minor = shards // MAJOR
-    qblock = 2 * block
     peers = shards - 1
+    shape = jax.ShapeDtypeStruct
     shapes = (
-        jax.ShapeDtypeStruct((length, width), BF16),
-        jax.ShapeDtypeStruct((3 * slab, length), BF16),
-        jax.ShapeDtypeStruct((slab, length), F32),
-        jax.ShapeDtypeStruct((8, length), F32),
-        jax.ShapeDtypeStruct((width, block), BF16),
-        jax.ShapeDtypeStruct((8, width), F32),
-        jax.ShapeDtypeStruct((8, length), F32),
-        jax.ShapeDtypeStruct((shards,) + wq.shape[1:], BF16),
-        jax.ShapeDtypeStruct((3, shards) + ffn.shape[1:], BF16),
+        shape((length, width), BF16),
+        shape((3 * slab, length), BF16),
+        shape((slab, length), F32),
+        shape((8, length), F32),
+        shape((8, width), F32),
+        shape((8, length), F32),
+        shape((shards, wparts, slab // wparts, 3 * slab), BF16),
+        shape((block, width), BF16),
+        shape((block, width), F32),
+        shape((3, shards, halves, slab // halves, block), BF16),
+        shape((3, block, width), BF16),
+        shape((width, block), BF16),
+        shape((8, width), F32),
     )
     dma = pltpu.SemaphoreType.DMA
-    plane = MAJOR * minor - 1
-    f_sends = plane + plane * (fparts - 1)
+    vm = pltpu.VMEM
     return pl.pallas_call(
-        functools.partial(front_kernel, shards, wparts, fparts, qblock),
+        functools.partial(front_kernel, shards, wparts, fparts, 2 * block),
         out_shape=shapes,
-        in_specs=[VMEM, VMEM, VMEM, VMEM, ANY],
-        out_specs=[VMEM] * 8 + [ANY],
+        in_specs=[VMEM] * 3 + [ANY] * 3 + [VMEM],
+        out_specs=[VMEM] * len(shapes),
         scratch_shapes=[
-            pltpu.VMEM((shards, block, width), BF16),
-            pltpu.VMEM((shards, 8, packet.shape[1]), F32),
-            pltpu.VMEM((3 * slab, width), BF16),
-            pltpu.VMEM((slab, length), BF16),
-            dma((plane,)),
-            dma((shards,)),
-            dma((peers,)),
-            dma((shards,)),
-            dma((peers * wparts,)),
-            dma((shards, wparts)),
-            dma((f_sends + 8,)),
-            dma((shards, fparts)),
-            dma((2,)),
-            dma((shards,)),
-            dma((shards,)),
+            vm((shards, block, width), BF16),
+            vm((shards, 8, 256), F32),
+            vm((shards, wparts, slab // wparts, 3 * slab), BF16),
+            vm((3 * slab, width), BF16),
+            vm((slab, length), BF16),
+            vm((width, block), BF16),
+            vm((3, width, width), BF16),
+            dma((2, MAJOR)), dma((MAJOR, minor - 1)), dma((shards,)),
+            dma((peers,)), dma((shards,)),
+            dma((peers,)), dma((shards, wparts)), dma((peers,)),
+            dma((2, MAJOR)), dma((MAJOR, minor - 1)), dma((shards, fparts)),
+            dma((shards,)), dma((shards, 2)),
+            dma((3,)), dma((shards,)), dma((shards,)),
         ],
         compiler_params=pltpu.CompilerParams(
-            collective_id=0, has_side_effects=True, vmem_limit_bytes=56 << 20
+            collective_id=0, has_side_effects=True, vmem_limit_bytes=58 << 20
         ),
         name="front",
-    )(inputs, packet, biases, wq, ffn)
-
-
-def prepare(inputs, segment_ids, positions, gain_one, w_qkv, b_query, b_value, query_scale, w_out, b_out, gain_two, w_up, b_up, w_down, b_down):
-    shards = lax.axis_size("shard")
+    )(inputs, small, w_qkv, w_out, w_up, w_down, cotangent)
+
+
+def pack(positions, segment_ids, gain_one, b_query, b_value, query_scale, b_out, gain_two, b_up, b_down):
+    block = positions.shape[-1]
     me = lax.axis_index("shard")
-    block, width = inputs.shape
-    slab = width // shards
     starts = (me * block + lax.iota(jnp.int32, block) - positions.reshape(block)).astype(F32)
-    rows = jnp.stack(
-        [jnp.pad(v.astype(F32), (0, 256 - slab)) for v in (gain_one, b_out, gain_two, b_up, b_down)]
-    )
-    scale_row = lax.dynamic_update_slice(
-        jnp.zeros((1, 256), F32), query_scale.astype(F32)[None], (0, me * query_scale.shape[0])
-    )
-    start_row = jnp.pad(starts, (0, 256 - block))[None]
-    packet = jnp.concatenate([rows, scale_row, start_row, jnp.zeros((1, 256), F32)], axis=0)
-    biases = jnp.stack([b_query, b_value], axis=1).astype(F32)
-    wparts = parts_of(slab, 16, 2)
-    fparts = parts_of(slab, 8, 4)
-    wq = (
-        w_qkv.reshape(slab, 3, shards, slab)
-        .transpose(2, 0, 1, 3)
-        .reshape(shards, wparts, slab // wparts, 3 * slab)
-    )
-    ffn = jnp.stack([w_out, w_up, w_down]).reshape(3, fparts, slab // fparts, width)
-    return packet, biases, wq, ffn
-
-
-def flipped(part, mask):
-    bit = lax.rem(part // mask, 2)
-    return part + mask - 2 * mask * bit
+    keep = (segment_ids.reshape(block) != 0).astype(F32)
+    table = {
+        0: gain_one, 1: b_out, 2: gain_two, 3: b_up, 4: b_down, 5: query_scale, 6: starts,
+        8: b_query, 9: b_value, 10: keep,
+    }
+    total = jnp.zeros((16, 256), F32)
+    for row, vector in table.items():
+        total = total + jnp.pad(vector.astype(F32)[None], ((row, 15 - row), (0, 256 - vector.shape[0])))
+    return total
+
+
+def masks_of(parts):
+    return {4: (2, 1), 2: (1,), 1: ()}[parts]
+
+
+def others(at):
+    return at.peers()
 
 
 def back_kernel(
@@ -480,7 +561,7 @@
         for k in range(halves):
             locals_[m, k].wait()
             if parts > 1:
-                at.arrived(from_core.at[m, k], c_send.at[m, k], c_recv.at[m, k])
+                at.arrived(from_core.at[m, k], c_recv.at[m, k])
         if parts > 1:
             def add(j, carry):
                 for k in range(halves):
@@ -492,7 +573,7 @@
 
     def after_y(m):
         if parts == 4:
-            at.arrived(from_y.at[m], y_send.at[m], y_recv.at[m])
+            at.arrived(from_y.at[m], y_recv.at[m])
             def add(j, carry):
                 own[m, km, j] = own[m, km, j] + from_y[m, j]
                 return carry
@@ -511,7 +592,7 @@
             ta = to // minor
             total = own[m, km, to].astype(F32)
             for db in range(1, minor):
-                at.arrived(from_x.at[m, db - 1, ta], x_send.at[m, db - 1, 0], x_recv.at[m, db - 1, ta])
+                at.arrived(from_x.at[m, db - 1, ta], x_recv.at[m, db - 1, ta])
                 total = total + from_x[m, db - 1, ta].astype(F32)
             own[m, km, to] = total.astype(BF16)
             if da < MAJOR:
@@ -523,7 +604,7 @@
     def after_z(m):
         total = own[m, km, me].astype(F32)
         for da in range(1, MAJOR):
-            at.arrived(from_z.at[m, da - 1], z_send.at[m, da - 1], z_recv.at[m, da - 1])
+            at.arrived(from_z.at[m, da - 1], z_recv.at[m, da - 1])
             total = total + from_z[m, da - 1].astype(F32)
         fin_ref[mine, m] = total.astype(BF16)
 
@@ -533,7 +614,7 @@
     for da, db in peers:
         origin = at.at(-da, -db)
         at.arrived(
-            dctx.at[:, pl.ds(pl.multiple_of(origin * block, block), block)], d_send.at[0], d_recv.at[origin]
+            dctx.at[:, pl.ds(pl.multiple_of(origin * block, block), block)], d_recv.at[origin]
         )
 
     scales = vec_ref[5:6, :128]
@@ -650,7 +731,7 @@
         after_y(m)
     for k in range(halves):
         if parts > 1:
-            at.arrived(gw_core.at[k], wc_send.at[k], wc_recv.at[k])
+            at.arrived(gw_core.at[k], wc_recv.at[k])
             part = core + 2 * k
             gw_core[k] = gw[:, part] + gw_core[k]
     if parts == 4:
@@ -661,7 +742,7 @@
         ta = to // minor
         total = part_gn[to].astype(F32)
         for db in range(1, minor):
-            at.arrived(gn_x.at[db - 1, ta], nx_send.at[db - 1, 0], nx_recv.at[db - 1, ta])
+            at.arrived(gn_x.at[db - 1, ta], nx_recv.at[db - 1, ta])
             total = total + gn_x[db - 1, ta].astype(F32)
         if da < MAJOR:
             part_gn[to] = total.astype(BF16)
@@ -672,7 +753,7 @@
         after_x(m)
 
     if parts == 4:
-        at.arrived(gw_y, wy_send.at[0], wy_recv.at[0])
+        at.arrived(gw_y, wy_recv.at[0])
         gw_sum[...] = gw_core[km] + gw_y[...]
     elif parts > 1:
         gw_sum[...] = gw_core[0]
@@ -685,7 +766,7 @@
 
     for da, db in peers:
         origin = at.at(-da, -db)
-        at.arrived(small_land.at[origin], v_send.at[0], v_recv.at[origin])
+        at.arrived(small_land.at[origin], v_recv.at[origin])
     small = jnp.sum(small_land[...], axis=0)
     sides = jnp.concatenate(
         [
@@ -707,7 +788,7 @@
     small_got[0, :, 256:] = pltpu.roll(small[:, 384:], lax.rem(128 - me * unit, 128), 1)
     for n, mask in enumerate(every):
         at.send(small_got.at[2 * n], small_got.at[2 * n + 1], b_send.at[n], b_recv.at[n], rep=at.flip(mask))
-        at.arrived(small_got.at[2 * n + 1], b_send.at[n], b_recv.at[n])
+        at.arrived(small_got.at[2 * n + 1], b_recv.at[n])
         small_got[2 * n + 2] = small_got[2 * n] + small_got[2 * n + 1]
     small_ref[...] = small_got[2 * len(every)]
 
@@ -715,18 +796,18 @@
         after_z(m)
     for n, mask in enumerate(extras):
         at.send(fin_ref.at[mine], extra.at[n], e_send.at[n], e_recv.at[n], rep=at.flip(mask))
-        at.arrived(extra.at[n], e_send.at[n], e_recv.at[n])
-        at.started[-1].wait_send()
+        at.arrived(extra.at[n], e_recv.at[n])
+        at.started[-1][1].wait_send()
         at.started.pop()
         fin_ref[mine] = fin_ref[mine] + extra[n]
     for da, db in peers:
         origin = at.at(-da, -db)
-        at.arrived(gw_land.at[origin], wa_send.at[0], wa_recv.at[origin])
+        at.arrived(gw_land.at[origin], wa_recv.at[origin])
     gw_ref[mine] = gw_land[...]
     for n, mask in enumerate(extras):
         at.send(gw_ref.at[mine], gw_extra.at[n], we_send.at[n], we_recv.at[n], rep=at.flip(mask))
-        at.arrived(gw_extra.at[n], we_send.at[n], we_recv.at[n])
-        at.started[-1].wait_send()
+        at.arrived(gw_extra.at[n], we_recv.at[n])
+        at.started[-1][1].wait_send()
         at.started.pop()
         gw_ref[mine] = gw_ref[mine] + gw_extra[n]
     have = [mine]
@@ -738,13 +819,13 @@
             rk += 1
         fresh = [flipped(part, mask) for part in have]
         for part in fresh:
-            at.arrived(fin_ref.at[part], r_send.at[0], r_recv.at[part])
-            at.arrived(gw_ref.at[part], wr_send.at[0], wr_recv.at[part])
+            at.arrived(fin_ref.at[part], r_recv.at[part])
+            at.arrived(gw_ref.at[part], wr_recv.at[part])
         have = have + fresh
 
     total = gn_ref[...]
     for da in range(1, MAJOR):
-        at.arrived(gn_z.at[da - 1], nz_send.at[da - 1], nz_recv.at[da - 1])
+        at.arrived(gn_z.at[da - 1], nz_recv.at[da - 1])
         total = total + gn_z[da - 1].astype(F32)
     gn_ref[...] = total
     for db in range(1, minor):
@@ -827,42 +908,6 @@
     )(grads, dctx, qkv, query, log, start, normed, wcols, vec, rows)
 
 
-def middle(x, att, keep, weights, vec, cotangent):
-    width = x.shape[1]
-    w_out, w_up, w_down = weights
-    b_out, gain_two, b_up, b_down = vec[1], vec[2], vec[3], vec[4]
-    x = x.astype(F32)
-    att = att * keep.astype(BF16)[None, :]
-    mixed = x + lax.dot_general(att, w_out, (((0,), (0,)), ((), ())), preferred_element_type=F32) + b_out
-    r = lax.rsqrt(jnp.mean(mixed * mixed, axis=-1, keepdims=True) + EPS)
-    normed = (mixed * r * gain_two).astype(BF16)
-    hidden = jnp.dot(normed, w_up, preferred_element_type=F32) + b_up
-    s = 1.0 / (1.0 + jnp.exp(-hidden))
-    act = (hidden * s).astype(BF16)
-    output = (mixed + jnp.dot(act, w_down, preferred_element_type=F32) + b_down).astype(BF16)
-    cot = cotangent.astype(F32)
-    both = (((1,), (1,)), ((), ()))
-    tokens = (((0,), (0,)), ((), ()))
-    g_down = lax.dot_general(act, cotangent, tokens, preferred_element_type=F32)
-    g_act = lax.dot_general(cotangent, w_down, both, preferred_element_type=F32)
-    g_hidden = g_act * (s + hidden * s * (1.0 - s))
-    low = g_hidden.astype(BF16)
-    g_up = lax.dot_general(normed, low, tokens, preferred_element_type=F32)
-    g_normed = lax.dot_general(low, w_up, both, preferred_element_type=F32)
-    g_mixed = cot + r * gain_two * g_normed - mixed * (r * r * r) * jnp.mean(
-        mixed * gain_two * g_normed, axis=-1, keepdims=True
-    )
-    g_low = g_mixed.astype(BF16)
-    g_out = jnp.dot(att, g_low, preferred_element_type=F32)
-    dctx = lax.dot_general(w_out, g_low, both, preferred_element_type=F32).astype(BF16) * keep.astype(BF16)[None, :]
-    rows = jnp.stack(
-        [jnp.zeros(width, F32), g_mixed.sum(0), (g_normed * mixed * r).sum(0), g_hidden.sum(0), cot.sum(0)]
-        + [jnp.zeros(width, F32)] * 3
-    )
-    grads = jnp.stack([g_out.astype(BF16), g_up.astype(BF16), g_down.astype(BF16)])
-    return output, g_mixed, grads, dctx, rows
-
-
 def on_device(
     inputs, segment_ids, positions, gain_one, w_qkv, b_query, b_value, query_scale, w_out, b_out,
     gain_two, w_up, b_up, w_down, b_down, cotangent,
@@ -872,18 +917,14 @@
     block, width = inputs.shape[1:]
     slab = width // shards
     x = inputs.reshape(block, width)
-    packet, biases, wq, ffn = prepare(
-        x, segment_ids, positions, gain_one, w_qkv, b_query, b_value, query_scale, w_out, b_out,
-        gain_two, w_up, b_up, w_down, b_down,
+    small = pack(positions, segment_ids, gain_one, b_query, b_value, query_scale, b_out, gain_two, b_up, b_down)
+    normed, qkv, query, log, vec, start, wcols, output, g_mixed, xt, dy, dctx, rows = front(
+        shards, x, small, w_qkv, w_out, w_up, w_down, cotangent.reshape(block, width)
     )
-    normed, qkv, query, log, att, vec, start, wcols, weights = front(shards, x, packet, biases, wq, ffn)
-    shape = weights.shape
-    keep = segment_ids.reshape(block) != 0
-    output, g_mixed, grads, dctx, rows = middle(
-        x, att, keep, weights.reshape(3, width, width), vec, cotangent.reshape(block, width)
-    )
+    grads = jnp.einsum("mat,mtd->mad", xt.reshape(3, width, block), dy, preferred_element_type=F32).astype(BF16)
+    parts = 4 if (width // shards) % 32 == 0 else 2
     fin, gw, gn, small = back(
-        shards, replicas, grads.reshape(shape), dctx, qkv, query, log, start, normed, wcols, vec, rows
+        shards, replicas, grads.reshape(3, shards, parts, slab // parts, width), dctx, qkv, query, log, start, normed, wcols, vec, rows
     )
     parts, rp = fin.shape[0], fin.shape[2]
     fin = fin.transpose(1, 0, 2, 3).reshape(3, slab, width).astype(F32)

time: 353 us -> 282 us (0.80)
  Pallas kernels: 280 us -> 240 us
  local copies, waits for them, and re-layouts: 44.4 us -> 25.3 us
  other arithmetic: 16.3 us -> 6.27 us
    pallas_call x1, Pallas kernels: 127 us -> 92.5 us  [front(): pl.pallas_call(functools.partial(front_kernel, shards, wparts, fparts, 2...]
    reshape x4 -> x0, local copies, waits for them, and re-layouts: 15 us -> none  [the longest x2 8.35 us: prepare(): wq = w_qkv.reshape(slab, 3, shards, slab).transpose(2, 0, 1, 3).reshape(s...]
    another operation x7 -> x0, other arithmetic: 10.3 us -> none  [the longest x1 4.55 us: middle(): jnp.stack([g_out.astype(BF16), g_up.astype(BF16), g_down.astype(BF16)])]
    another operation x12 -> x0, local copies, waits for them, and re-layouts: 6.44 us -> none  [the longest x1 4.41 us: middle(): w_out, w_up, w_down = weights]
    pallas_call x1, Pallas kernels: 152 us -> 147 us  [back(): pl.pallas_call(functools.partial(back_kernel, shards, replicas, parts, 2...]
    broadcast_in_dim x0 -> x7, local copies, waits for them, and re-layouts: none -> 4.61 us  [pack(): vector.astype(F32)[None]]
    dot_general x9 -> x1, matrix products: 10.4 us -> 7.99 us  [on_device(): jnp.einsum('mat,mtd->mad', xt.reshape(3, width, block), dy, preferred_ele...]
where the time goes in v2:
time: 282 us; the launch traced here: 280 us
  Pallas kernels  240 us (85%)
  local copies, waits for them, and re-layouts  25.3 us (9%)
  matrix products  7.99 us (3%)
  other arithmetic  6.27 us (2%)
    pallas_call x1, Pallas kernels, back(): pl.pallas_call(functools.partial(back_kernel, shards, replicas, parts, 2...  147 us
    pallas_call x1, Pallas kernels, front(): pl.pallas_call(functools.partial(front_kernel, shards, wparts, fparts, 2...  92.5 us
    convert_element_type x3, local copies, waits for them, and re-layouts, on_device(): gw.reshape(parts, shards, rp, 3, slab).transpose(0, 2, 3, 1, 4)  16.5 us
    dot_general x1, matrix products, on_device(): jnp.einsum('mat,mtd->mad', xt.reshape(3, width, block), dy, preferred_ele...  7.99 us

profile of v2, /device:TPU:0, one launch (start us, length us, event | category | flops | bytes accessed | tf_op | source)
XLA Modules:
  0.0 280.1 jit_solution(5303321311988274047)
XLA Ops:
  0.6 0.7 subtract_convert_fusion
  1.3 0.7 broadcast_compare_fusion
  2.0 0.7 broadcast_in_dim.49
  2.6 0.7 broadcast_in_dim.48
  3.3 0.7 broadcast_in_dim.46
  3.9 0.7 broadcast_in_dim.45
  4.6 0.7 broadcast_in_dim.44
  5.3 0.7 broadcast_in_dim.43
  5.9 0.7 broadcast_in_dim.42
  6.6 1.3 convert_add_fusion.small_ref
  7.9 92.5 %front.1 = (bf16[1024,1280]{1,0:T(8,128)(2,1)}, bf16[480,1024]{1,0:T(8,128)(2,1)}, f32[160,1024]{1,0:T(8,128)}, f32[8,1024]{1,0:T(8,128)}, f32[8,1280]{1,0:T(8,1...) custom-call(bf16[128,1280]{1,0:T(8,128)(2,1)} %bitcast.34, ...), custom_call_target="tpu_custom_call" | custom-call | tf_op jit(solution)/shard_map/front/pallas_call | solution.py:450
  100.3 8.0 %convolution_convert_fusion = bf16[3,1280,1280]{2,1,0:T(8,128)(2,1)} fusion(bf16[3,1280,128]{2,1,0:T(8,128)(2,1)} %bitcast.35, bf16[3,128,1280]{2,1,0:T(8,128)(2,1)} %get-tuple-element.35), kind=kOutput, calls=%fused_computation | convolution fusion | flops 1263206400 | bytes 11796480 | tf_op jit(solution)/shard_map/mat,mtd->mad/dot_general | solution.py:924
  108.3 147.3 %back.1 = (bf16[4,3,40,1280]{3,2,1,0:T(8,128)(2,1)}, bf16[4,8,40,480]{3,2,1,0:T(8,128)(2,1)}, f32[128,1280]{1,0:T(8,128)}, f32[8,384]{1,0:T(8,128)}) custom-call(bf16[3,8,4,40,1280]{4,3,2,1,0:T(8,128)(2,1)} %bitcast.32, bf16[1280,128]{1,0:T(8,128)(2,1)} %get-tuple-element.36.dctx_ref, bf16[480,1024]{1,0:T(8,128)(2,1)} %get-tuple-element.37.qkv_ref, ...), custom_call_target="tpu_custom_call" | custom-call | tf_op jit(solution)/shard_map/back/pallas_call | solution.py:854
  255.7 0.0 copy-start.5
  255.7 0.0 copy-start.1
  255.7 0.9 slice_reduce_fusion
  256.6 0.0 copy-done
  256.6 1.3 fusion
  257.9 0.0 copy-done.3
  257.9 2.2 fusion.3
  260.1 0.0 copy-done.5
  260.1 0.6 fusion.7
  260.7 0.0 copy-done.1
  260.7 4.7 %reshape.86 = f32[4,8,40,3,160]{4,3,2,1,0:T(4,128)} reshape(bf16[4,8,40,480]{3,2,1,0:T(8,128)(2,1)S(1)} %copy-done.1) | data formatting | bytes 3686400 | tf_op jit(solution)/shard_map/convert_element_type | solution.py:931
  265.4 6.7 %copy.31 = f32[4,40,3,8,160]{4,3,2,1,0:T(8,128)} copy(f32[4,40,3,8,160]{4,2,1,3,0:T(4,128)} %bitcast.33) | data formatting | bytes 4915200 | tf_op jit(solution)/shard_map/convert_element_type | solution.py:931
  272.1 5.1 %reshape.85 = f32[160,3840]{1,0:T(8,128)} reshape(f32[4,40,3,8,160]{4,3,2,1,0:T(8,128)} %copy.31) | data formatting | bytes 4915200 | tf_op jit(solution)/shard_map/convert_element_type | solution.py:931
  277.2 0.5 slice_bitcast_fusion
  277.7 0.0 copy-done.2
  277.7 0.2 convert_bitcast_fusion
  277.9 0.0 copy-start.4
  277.9 1.5 fusion.6
  279.4 0.7 copy.33
  (5 shorter events, 0.0 us)
Async XLA Ops:
  108.3 148.3 %copy-start = (bf16[1,128,1280]{2,1,0:T(8,128)(2,1)S(1)}, bf16[1,128,1280]{2,1,0:T(8,128)(2,1)}, u32[]{:S(2)}) copy-start(bf16[1,128,1280]{2,1,0:T(8,128)(2,1)} %param.16) | copy-start | bytes 983044
  108.3 149.6 %copy-start.3 = (f32[128,1280]{1,0:T(8,128)S(1)}, f32[128,1280]{1,0:T(8,128)}, u32[]{:S(2)}) copy-start(f32[128,1280]{1,0:T(8,128)} %get-tuple-element.32) | copy-start | bytes 1966084
  255.7 4.5 %copy-start.5 = (f32[8,384]{1,0:T(8,128)S(1)}, f32[8,384]{1,0:T(8,128)}, u32[]{:S(2)}) copy-start(f32[8,384]{1,0:T(8,128)} %get-tuple-element.45) | copy-start | bytes 36868
  255.7 5.0 %copy-start.1 = (bf16[4,8,40,480]{3,2,1,0:T(8,128)(2,1)S(1)}, bf16[4,8,40,480]{3,2,1,0:T(8,128)(2,1)}, u32[]{:S(2)}) copy-start(bf16[4,8,40,480]{3,2,1,0:T(8,128)(2,1)} %get-tuple-element.46) | copy-start | bytes 3686404
  272.1 5.6 %copy-start.2 = (bf16[4,3,40,1280]{3,2,1,0:T(8,128)(2,1)S(1)}, bf16[4,3,40,1280]{3,2,1,0:T(8,128)(2,1)}, u32[]{:S(2)}) copy-start(bf16[4,3,40,1280]{3,2,1,0:T(8,128)(2,1)} %get-tuple-element.47) | copy-start | bytes 3686404
  277.9 1.5 copy-start.4

commit v3 on v2

--- a/solution.py
+++ b/solution.py
@@ -489,24 +489,17 @@
     return total
 
 
-def masks_of(parts):
-    return {4: (2, 1), 2: (1,), 1: ()}[parts]
-
-
-def others(at):
-    return at.peers()
-
-
 def back_kernel(
     shards, replicas, parts, qblock,
-    g_ref, dctx_ref, qkv_ref, query_ref, log_ref, start_ref, normed_ref, wcols_ref, vec_ref, row_ref,
-    fin_ref, gw_ref, gn_ref, small_ref,
+    x_ref, gmixed_ref, xt_ref, dy_ref, dctx_ref, qkv_ref, query_ref, log_ref, start_ref, normed_ref, wcols_ref,
+    vec_ref, row_ref,
+    fin_ref, gw_ref, gin_ref, small_ref,
     dctx, grads, turned, proj,
-    own, from_core, from_y, from_x, from_z, extra,
+    left, right, stash, sums, from_x, from_z, extra,
     part_gn, gn_x, gn_z,
     gw, gw_core, gw_y, gw_sum, gw_land, gw_extra,
     windows, small_land, small_got,
-    d_send, d_recv, o_sem, c_send, c_recv, y_send, y_recv, x_send, x_recv, z_send, z_recv,
+    d_send, d_recv, y_send, y_recv, c_send, c_recv, x_send, x_recv, z_send, z_recv,
     r_send, r_recv, e_send, e_recv,
     nx_send, nx_recv, nz_send, nz_recv,
     wc_send, wc_recv, wy_send, wy_recv, wa_send, wa_recv, wr_send, wr_recv, we_send, we_recv,
@@ -519,11 +512,12 @@
     local = slab // HEAD
     block = length // shards
     width = normed_ref.shape[1]
-    peers = others(at)
-    halves = max(parts // 2, 1)
+    cols = width // 2
+    peers = at.peers()
     core = lax.rem(at.rep, 2)
     mine = lax.rem(at.rep, parts)
-    km = mine // 2 if parts > 1 else 0
+    i_part = lax.rem(mine, 2) if parts == 4 else 0
+    j_part = mine // 2 if parts == 4 else mine
     every = []
     mask = 1
     while mask < replicas:
@@ -533,89 +527,101 @@
     at.greet(tuple(every))
     mats = (2, 1, 0)
 
+    def lane(n, size):
+        return pl.ds(pl.multiple_of(n * size, 128), size)
+
     for i, (da, db) in enumerate(peers):
         dest = at.at(da, db)
         at.send(
-            dctx_ref.at[pl.ds(pl.multiple_of(dest * slab, slab), slab), :],
-            dctx.at[:, pl.ds(pl.multiple_of(me * block, block), block)],
-            d_send.at[i], d_recv.at[me], shard=dest,
+            dctx_ref.at[pl.ds(pl.multiple_of(dest * slab, 16), slab), :],
+            dctx.at[:, lane(me, block)], d_send.at[i], d_recv.at[me], shard=dest,
         )
-    locals_ = {}
+    def slot(n):
+        return slice(n * block, (n + 1) * block)
+
     for m in mats:
-        for k in range(halves):
-            if parts > 1:
-                at.send(
-                    g_ref.at[m, :, (1 - core) + 2 * k], from_core.at[m, k],
-                    c_send.at[m, k], c_recv.at[m, k], rep=at.flip(1),
-                )
-            copy = pltpu.make_async_copy(
-                g_ref.at[m, :, core + 2 * k if parts > 1 else 0], own.at[m, k], o_sem.at[m, k]
-            )
-            copy.start()
-            locals_[m, k] = copy
-    dctx[:, pl.ds(pl.multiple_of(me * block, block), block)] = dctx_ref[
-        pl.ds(pl.multiple_of(me * slab, slab), slab), :
-    ]
-
-    def after_core(m):
-        for k in range(halves):
-            locals_[m, k].wait()
-            if parts > 1:
-                at.arrived(from_core.at[m, k], c_recv.at[m, k])
-        if parts > 1:
-            def add(j, carry):
-                for k in range(halves):
-                    own[m, k, j] = own[m, k, j] + from_core[m, k, j]
-                return carry
-            lax.fori_loop(0, shards, add, 0)
         if parts == 4:
-            at.send(own.at[m, 1 - km], from_y.at[m], y_send.at[m], y_recv.at[m], rep=at.flip(2))
-
-    def after_y(m):
+            far = at.flip(2)
+            at.send(xt_ref.at[m, :, i_part], left.at[m, :, :, slot(1)], y_send.at[m, 0], y_recv.at[m, 0], rep=far)
+            at.send(
+                dy_ref.at[m, :, lane(1 - j_part, cols)], right.at[m, slot(1), :],
+                y_send.at[m, 1], y_recv.at[m, 1], rep=far,
+            )
+            at.send(xt_ref.at[m, :, 1 - i_part], stash.at[m], y_send.at[m, 2], y_recv.at[m, 2], rep=far)
+            near = 2
+            at.send(
+                xt_ref.at[m, :, 1 - i_part], left.at[m, :, :, slot(near)], c_send.at[m, 0], c_recv.at[m, 0],
+                rep=at.flip(1),
+            )
+            at.send(
+                dy_ref.at[m, :, lane(j_part, cols)], right.at[m, slot(near), :],
+                c_send.at[m, 1], c_recv.at[m, 1], rep=at.flip(1),
+            )
+        else:
+            near = 1
+            at.send(
+                xt_ref.at[m, :, 0], left.at[m, :, :, slot(near)], c_send.at[m, 0], c_recv.at[m, 0], rep=at.flip(1)
+            )
+            at.send(
+                dy_ref.at[m, :, lane(1 - j_part, cols)], right.at[m, slot(near), :],
+                c_send.at[m, 1], c_recv.at[m, 1], rep=at.flip(1),
+            )
+        left[m, :, :, slot(0)] = xt_ref[m, :, i_part]
+        right[m, slot(0), :] = dy_ref[m, :, lane(j_part, cols)]
+    dctx[:, lane(me, block)] = dctx_ref[pl.ds(pl.multiple_of(me * slab, 16), slab), :]
+
+    def relay(m):
         if parts == 4:
-            at.arrived(from_y.at[m], y_recv.at[m])
-            def add(j, carry):
-                own[m, km, j] = own[m, km, j] + from_y[m, j]
-                return carry
-            lax.fori_loop(0, shards, add, 0)
+            at.arrived(left.at[m, :, :, slot(1)], y_recv.at[m, 0])
+            at.arrived(right.at[m, slot(1), :], y_recv.at[m, 1])
+            at.arrived(stash.at[m], y_recv.at[m, 2])
+            at.send(stash.at[m], left.at[m, :, :, slot(3)], c_send.at[m, 2], c_recv.at[m, 2], rep=at.flip(1))
+            at.send(
+                right.at[m, slot(1), :], right.at[m, slot(3), :], c_send.at[m, 3], c_recv.at[m, 3], rep=at.flip(1)
+            )
+
+    def weight(m):
+        near = 2 if parts == 4 else 1
+        at.arrived(left.at[m, :, :, slot(near)], c_recv.at[m, 0])
+        at.arrived(right.at[m, slot(near), :], c_recv.at[m, 1])
+        if parts == 4:
+            at.arrived(left.at[m, :, :, slot(3)], c_recv.at[m, 2])
+            at.arrived(right.at[m, slot(3), :], c_recv.at[m, 3])
+        rows = left.shape[1] * left.shape[2]
+        out = dot(left[m].reshape(rows, parts * block), right[m])
+        sums[m] = out.reshape(sums.shape[1:]).astype(BF16)
         for db in range(1, minor):
-            for da in range(MAJOR):
-                at.send(
-                    own.at[m, km, at.at(da, db)], from_x.at[m, db - 1, at.at(da, db) // minor],
-                    x_send.at[m, db - 1, da], x_recv.at[m, db - 1, at.at(da, db) // minor],
-                    shard=at.at(0, db),
-                )
+            at.send(
+                sums.at[m, :, lax.rem(at.b + db, minor)], from_x.at[m, db - 1],
+                x_send.at[m, db - 1], x_recv.at[m, db - 1], shard=at.at(0, db),
+            )
 
     def after_x(m):
+        for db in range(1, minor):
+            at.arrived(from_x.at[m, db - 1], x_recv.at[m, db - 1])
         for da in range(1, MAJOR + 1):
-            to = at.at(da, 0)
-            ta = to // minor
-            total = own[m, km, to].astype(F32)
+            ta = lax.rem(at.a + da, MAJOR)
+            total = sums[m, ta, at.b].astype(F32)
             for db in range(1, minor):
-                at.arrived(from_x.at[m, db - 1, ta], x_recv.at[m, db - 1, ta])
                 total = total + from_x[m, db - 1, ta].astype(F32)
-            own[m, km, to] = total.astype(BF16)
+            sums[m, ta, at.b] = total.astype(BF16)
             if da < MAJOR:
                 at.send(
-                    own.at[m, km, to], from_z.at[m, da - 1], z_send.at[m, da - 1], z_recv.at[m, da - 1],
-                    shard=to,
+                    sums.at[m, ta, at.b], from_z.at[m, da - 1], z_send.at[m, da - 1], z_recv.at[m, da - 1],
+                    shard=at.at(da, 0),
                 )
 
+    def fin_slot(part, m=None):
+        row, rows, col, wide = part_box(part, parts, slab, width)
+        box = (pl.ds(pl.multiple_of(row, 16), rows), pl.ds(pl.multiple_of(col, 128), wide))
+        return fin_ref.at[(slice(None) if m is None else m,) + box]
+
     def after_z(m):
-        total = own[m, km, me].astype(F32)
+        total = sums[m, at.a, at.b].astype(F32)
         for da in range(1, MAJOR):
             at.arrived(from_z.at[m, da - 1], z_recv.at[m, da - 1])
             total = total + from_z[m, da - 1].astype(F32)
-        fin_ref[mine, m] = total.astype(BF16)
-
-    for m in mats:
-        after_core(m)
-
-    for da, db in peers:
-        origin = at.at(-da, -db)
-        at.arrived(
-            dctx.at[:, pl.ds(pl.multiple_of(origin * block, block), block)], d_recv.at[origin]
-        )
+        fin_slot(mine, m)[...] = total.astype(BF16)
 
     scales = vec_ref[5:6, :128]
     column = jnp.broadcast_to(scales, (128, 128)).T[:HEAD, 0:1]
@@ -623,6 +629,9 @@
     soft = jnp.maximum(column, 0.0) + jnp.log(1.0 + jnp.exp(-jnp.abs(column)))
     factor = base * soft
     grads[...] = jnp.zeros_like(grads)
+    for da, db in peers:
+        origin = at.at(-da, -db)
+        at.arrived(dctx.at[:, lane(origin, block)], d_recv.at[origin])
 
     def attend(i):
         reach = (i + 1) * qblock
@@ -636,27 +645,24 @@
             keys = qkv_ref[slab + h * HEAD : slab + (h + 1) * HEAD, :reach]
             values = qkv_ref[2 * slab + h * HEAD : 2 * slab + (h + 1) * HEAD, :reach]
             gctx = dctx[h * HEAD : (h + 1) * HEAD, span]
-            turn = (((0,), (0,)), ((), ()))
-            both = (((1,), (1,)), ((), ()))
-            scores = lax.dot_general(keys, queries, turn, preferred_element_type=F32)
+            scores = dot(keys, queries, TN)
             probs = jnp.where(allowed, jnp.exp(scores - log_ref[h : h + 1, span]), 0.0)
-            gprobs = lax.dot_general(values, gctx, turn, preferred_element_type=F32)
+            gprobs = dot(values, gctx, TN)
             delta = jnp.sum(probs * gprobs, axis=0, keepdims=True)
             gscores = (probs * (gprobs - delta)).astype(BF16)
             low = probs.astype(BF16)
-            grads[h * HEAD : (h + 1) * HEAD, span] = jnp.dot(
-                keys, gscores, preferred_element_type=F32
-            )
+            grads[h * HEAD : (h + 1) * HEAD, span] = dot(keys, gscores)
             kv = slice(slab + h * HEAD, slab + (h + 1) * HEAD)
-            grads[kv, :reach] += lax.dot_general(queries, gscores, both, preferred_element_type=F32)
+            grads[kv, :reach] += dot(queries, gscores, NT)
             kv = slice(2 * slab + h * HEAD, 2 * slab + (h + 1) * HEAD)
-            grads[kv, :reach] += lax.dot_general(gctx, low, both, preferred_element_type=F32)
+            grads[kv, :reach] += dot(gctx, low, NT)
 
     steps = length // qblock
     for i in range(steps):
         attend(i)
-        if i == steps - 2:
-            after_y(mats[0])
+        if i == steps - 3:
+            relay(mats[0])
+    relay(mats[1])
 
     gscale = jnp.zeros((HEAD, 1), F32)
     for h in range(local):
@@ -671,32 +677,50 @@
     proj[...] = turned[...].T[:, :slab3]
 
     wcols = wcols_ref[...].reshape(width, slab3)
-    gain_rows = jnp.zeros((8, width), F32)
 
     def partial(origin, acc):
-        tokens = pl.ds(pl.multiple_of(origin * block, block), block)
-        out = lax.dot_general(
-            proj[tokens, :], wcols, (((1,), (1,)), ((), ())), preferred_element_type=F32
-        )
+        tokens = lane(origin, block)
+        out = dot(proj[tokens, :], wcols, NT)
         part_gn[origin] = out.astype(BF16)
         weighted = out * normed_ref[tokens, :].astype(F32)
         return acc + jnp.sum(weighted.reshape(block // 8, 8, width), axis=0)
 
-    def away(i, acc):
+    def away_copy(i):
         db = 1 + i // MAJOR
         to = at.at(lax.rem(i + 1, MAJOR), db)
-        acc = partial(to, acc)
-        pltpu.make_async_remote_copy(
+        return to, pltpu.make_async_remote_copy(
             src_ref=part_gn.at[to], dst_ref=gn_x.at[db - 1, to // minor],
             send_sem=nx_send.at[db - 1, to // minor], recv_sem=nx_recv.at[db - 1, to // minor],
             device_id=(at.at(0, db), at.rep), device_id_type=MESH,
-        ).start()
+        )
+
+    def away(i, acc):
+        to, copy = away_copy(i)
+        acc = partial(to, acc)
+        copy.start()
         return acc
 
+    gain_rows = jnp.zeros((8, width), F32)
     gain_rows = lax.fori_loop(0, shards - MAJOR, away, gain_rows)
+
+    rp = width // (shards * parts)
+    halves = parts // 2
+    whole = dot(normed_ref[...], proj[...], TN)
+    gw[...] = whole.reshape(shards, parts, rp, slab3).astype(BF16)
+    for k in range(halves):
+        at.send(gw.at[:, (1 - core) + 2 * k], gw_core.at[k], wc_send.at[k], wc_recv.at[k], rep=at.flip(1))
+    weight(mats[0])
     gain_rows = lax.fori_loop(0, MAJOR, lambda i, acc: partial(at.at(i, 0), acc), gain_rows)
+    for k in range(halves):
+        at.arrived(gw_core.at[k], wc_recv.at[k])
+        gw_core[k] = gw[:, core + 2 * k] + gw_core[k]
+    km = mine // 2 if parts == 4 else 0
+    if parts == 4:
+        at.send(gw_core.at[1 - km], gw_y, wy_send.at[0], wy_recv.at[0], rep=at.flip(2))
+    weight(mats[1])
+    relay(mats[2])
+
     gain_row = jnp.sum(gain_rows, axis=0, keepdims=True) / vec_ref[0:1, :]
-
     rows = row_ref[...]
     place = lax.broadcasted_iota(jnp.int32, (8, width), 0)
     rows = jnp.where(place == 0, jnp.broadcast_to(gain_row, (8, width)), rows)
@@ -717,25 +741,16 @@
         at.send(windows.at[dest], small_land.at[me], v_send.at[i], v_recv.at[me], shard=dest)
     small_land[me] = windows[me]
 
-    rp = width // (shards * parts)
-    whole = lax.dot_general(
-        normed_ref[...], proj[...], (((0,), (0,)), ((), ())), preferred_element_type=F32
-    )
-    gw[...] = whole.reshape(shards, parts, rp, slab3).astype(BF16)
-    for k in range(halves):
-        if parts > 1:
-            at.send(
-                gw.at[:, (1 - core) + 2 * k], gw_core.at[k], wc_send.at[k], wc_recv.at[k], rep=at.flip(1)
-            )
-    for m in mats[1:]:
-        after_y(m)
-    for k in range(halves):
-        if parts > 1:
-            at.arrived(gw_core.at[k], wc_recv.at[k])
-            part = core + 2 * k
-            gw_core[k] = gw[:, part] + gw_core[k]
     if parts == 4:
-        at.send(gw_core.at[1 - km], gw_y, wy_send.at[0], wy_recv.at[0], rep=at.flip(2))
+        at.arrived(gw_y, wy_recv.at[0])
+        gw_sum[...] = gw_core[km] + gw_y[...]
+    else:
+        gw_sum[...] = gw_core[0]
+    for i, (da, db) in enumerate(peers):
+        dest = at.at(da, db)
+        at.send(gw_sum.at[dest], gw_land.at[me], wa_send.at[i], wa_recv.at[me], shard=dest)
+    gw_land[me] = gw_sum[me]
+    weight(mats[2])
 
     for da in range(1, MAJOR + 1):
         to = at.at(da, 0)
@@ -748,35 +763,17 @@
             part_gn[to] = total.astype(BF16)
             at.send(part_gn.at[to], gn_z.at[da - 1], nz_send.at[da - 1], nz_recv.at[da - 1], shard=to)
         else:
-            gn_ref[...] = total
-    for m in mats:
-        after_x(m)
-
-    if parts == 4:
-        at.arrived(gw_y, wy_recv.at[0])
-        gw_sum[...] = gw_core[km] + gw_y[...]
-    elif parts > 1:
-        gw_sum[...] = gw_core[0]
-    else:
-        gw_sum[...] = gw[:, 0]
-    for i, (da, db) in enumerate(peers):
-        dest = at.at(da, db)
-        at.send(gw_sum.at[dest], gw_land.at[me], wa_send.at[i], wa_recv.at[me], shard=dest)
-    gw_land[me] = gw_sum[me]
+            gin_ref[...] = total
+    after_x(mats[0])
+    after_x(mats[1])
 
     for da, db in peers:
         origin = at.at(-da, -db)
         at.arrived(small_land.at[origin], v_recv.at[origin])
     small = jnp.sum(small_land[...], axis=0)
+    lanes = lax.broadcasted_iota(jnp.int32, (slab, 128), 1)
     sides = jnp.concatenate(
-        [
-            jnp.where(
-                lax.broadcasted_iota(jnp.int32, (slab, 128), 1) == 6,
-                bias_q,
-                jnp.where(lax.broadcasted_iota(jnp.int32, (slab, 128), 1) == 7, bias_v, 0.0),
-            ),
-            jnp.zeros((256 - slab, 128), F32),
-        ],
+        [jnp.where(lanes == 6, bias_q, jnp.where(lanes == 7, bias_v, 0.0)), jnp.zeros((256 - slab, 128), F32)],
         axis=0,
     )
     sides = jnp.concatenate([sides[:128].T[:8], sides[128:].T[:8]], axis=1)
@@ -786,92 +783,140 @@
     small_got[0, :, :256] = jnp.where(tall < 5, window[:, :256], sides)
     unit = HEAD // shards
     small_got[0, :, 256:] = pltpu.roll(small[:, 384:], lax.rem(128 - me * unit, 128), 1)
-    for n, mask in enumerate(every):
-        at.send(small_got.at[2 * n], small_got.at[2 * n + 1], b_send.at[n], b_recv.at[n], rep=at.flip(mask))
+
+    def small_round(n):
+        at.send(
+            small_got.at[2 * n], small_got.at[2 * n + 1], b_send.at[n], b_recv.at[n], rep=at.flip(every[n])
+        )
+
+    def small_add(n):
         at.arrived(small_got.at[2 * n + 1], b_recv.at[n])
         small_got[2 * n + 2] = small_got[2 * n] + small_got[2 * n + 1]
-    small_ref[...] = small_got[2 * len(every)]
+
+    small_round(0)
+    for da, db in peers:
+        origin = at.at(-da, -db)
+        at.arrived(gw_land.at[origin], wa_recv.at[origin])
+    for n, mask in enumerate(extras):
+        if n == 0:
+            gw_extra[0] = gw_land[...]
+        at.send(gw_extra.at[2 * n], gw_extra.at[2 * n + 1], we_send.at[n], we_recv.at[n], rep=at.flip(mask))
+        at.arrived(gw_extra.at[2 * n + 1], we_recv.at[n])
+        gw_extra[2 * n + 2] = gw_extra[2 * n] + gw_extra[2 * n + 1]
+    land = gw_extra.at[2 * len(extras)] if extras else gw_land
+    for j in range(shards):
+        for t in range(3):
+            first = t * width + j * slab
+            gw_ref[mine, :, first : first + slab] = land[j, :, t * slab : (t + 1) * slab]
+
+    def hand_round(ref_slot, send_sem, recv_sem):
+        have, rounds, k = [mine], [], 0
+        for mask in ((2, 1) if parts == 4 else (1,)):
+            sends = []
+            for part in have:
+                sends.append((part, mask, k))
+                k += 1
+            fresh = [flipped(part, mask) for part in have]
+            rounds.append((sends, fresh))
+            have = have + fresh
+
+        def go(n):
+            for part, mask, k in rounds[n][0]:
+                at.send(ref_slot(part), ref_slot(part), send_sem.at[k], recv_sem.at[part], rep=at.flip(mask))
+
+        def take(n):
+            for part in rounds[n][1]:
+                at.arrived(ref_slot(part), recv_sem.at[part])
+
+        return go, take, len(rounds)
+
+    gw_go, gw_take, count = hand_round(lambda part: gw_ref.at[part], wr_send, wr_recv)
+    fin_go, fin_take, _ = hand_round(fin_slot, r_send, r_recv)
+    gw_go(0)
+    small_add(0)
+    small_round(1)
+    after_x(mats[2])
+
+    total = gin_ref[...]
+    for da in range(1, MAJOR):
+        at.arrived(gn_z.at[da - 1], nz_recv.at[da - 1])
+        total = total + gn_z[da - 1].astype(F32)
+    x = x_ref[...].astype(F32)
+    r = lax.rsqrt(jnp.mean(x * x, axis=-1, keepdims=True) + EPS)
+    weighted = vec_ref[0:1, :] * total
+    gin_ref[...] = gmixed_ref[...] + r * weighted - x * (r * r * r) * jnp.mean(x * weighted, axis=-1, keepdims=True)
 
     for m in mats:
         after_z(m)
     for n, mask in enumerate(extras):
-        at.send(fin_ref.at[mine], extra.at[n], e_send.at[n], e_recv.at[n], rep=at.flip(mask))
-        at.arrived(extra.at[n], e_recv.at[n])
-        at.started[-1][1].wait_send()
-        at.started.pop()
-        fin_ref[mine] = fin_ref[mine] + extra[n]
-    for da, db in peers:
-        origin = at.at(-da, -db)
-        at.arrived(gw_land.at[origin], wa_recv.at[origin])
-    gw_ref[mine] = gw_land[...]
-    for n, mask in enumerate(extras):
-        at.send(gw_ref.at[mine], gw_extra.at[n], we_send.at[n], we_recv.at[n], rep=at.flip(mask))
-        at.arrived(gw_extra.at[n], we_recv.at[n])
-        at.started[-1][1].wait_send()
-        at.started.pop()
-        gw_ref[mine] = gw_ref[mine] + gw_extra[n]
-    have = [mine]
-    rk = 0
-    for mask in masks_of(parts):
-        for part in have:
-            at.send(fin_ref.at[part], fin_ref.at[part], r_send.at[rk], r_recv.at[part], rep=at.flip(mask))
-            at.send(gw_ref.at[part], gw_ref.at[part], wr_send.at[rk], wr_recv.at[part], rep=at.flip(mask))
-            rk += 1
-        fresh = [flipped(part, mask) for part in have]
-        for part in fresh:
-            at.arrived(fin_ref.at[part], r_recv.at[part])
-            at.arrived(gw_ref.at[part], wr_recv.at[part])
-        have = have + fresh
-
-    total = gn_ref[...]
-    for da in range(1, MAJOR):
-        at.arrived(gn_z.at[da - 1], nz_recv.at[da - 1])
-        total = total + gn_z[da - 1].astype(F32)
-    gn_ref[...] = total
-    for db in range(1, minor):
-        for i in range(MAJOR):
-            pltpu.make_async_remote_copy(
-                src_ref=part_gn.at[me], dst_ref=part_gn.at[me],
-                send_sem=nx_send.at[db - 1, i], recv_sem=nx_recv.at[db - 1, i],
-                device_id=(at.at(0, db), at.rep), device_id_type=MESH,
-            ).wait_send()
+        if n == 0:
+            extra[0] = fin_slot(mine)[...]
+        at.send(extra.at[2 * n], extra.at[2 * n + 1], e_send.at[n], e_recv.at[n], rep=at.flip(mask))
+        at.arrived(extra.at[2 * n + 1], e_recv.at[n])
+        extra[2 * n + 2] = extra[2 * n] + extra[2 * n + 1]
+    if extras:
+        fin_slot(mine)[...] = extra[2 * len(extras)]
+    fin_go(0)
+    for n in range(count):
+        gw_take(n)
+        if n + 1 < count:
+            gw_go(n + 1)
+        fin_take(n)
+        if n + 1 < count:
+            fin_go(n + 1)
+    for n in range(1, len(every)):
+        small_add(n)
+        if n + 1 < len(every):
+            small_round(n + 1)
+    small_ref[...] = small_got[2 * len(every)]
+
+    def away_wait(i, carry):
+        away_copy(i)[1].wait_send()
+        return carry
+
+    lax.fori_loop(0, shards - MAJOR, away_wait, 0)
     at.settle()
 
 
-def back(shards, replicas, grads, dctx, qkv, query, log, start, normed, wcols, vec, rows):
-    parts, rp, width = grads.shape[2:]
+def back(shards, replicas, x, g_mixed, xt, dy, dctx, qkv, query, log, start, normed, wcols, vec, rows):
     slab3, length = qkv.shape
     slab = slab3 // 3
-    block = length // shards
+    block, width = x.shape
+    parts = parts_of(slab)
+    rp = slab // parts
+    rows_part = slab // 2 if parts == 4 else slab
+    cols = width // 2
     minor = shards // MAJOR
-    halves = max(parts // 2, 1)
+    halves = parts // 2
     peers = shards - 1
     dma = pltpu.SemaphoreType.DMA
     bits = (replicas - 1).bit_length()
-    more = max(bits - (parts - 1).bit_length(), 1)
+    more = bits - (parts - 1).bit_length()
     vm = pltpu.VMEM
     turned_rows = -(-slab3 // 128) * 128
+    shape = jax.ShapeDtypeStruct
     return pl.pallas_call(
         functools.partial(back_kernel, shards, replicas, parts, 2 * block),
         out_shape=(
-            jax.ShapeDtypeStruct((parts, 3, rp, width), BF16),
-            jax.ShapeDtypeStruct((parts, shards, rp, slab3), BF16),
-            jax.ShapeDtypeStruct((block, width), F32),
-            jax.ShapeDtypeStruct((8, 384), F32),
+            shape((3, slab, width), BF16),
+            shape((parts, rp, 3 * width), BF16),
+            shape((block, width), F32),
+            shape((8, 384), F32),
         ),
-        in_specs=[ANY] + [VMEM] * 9,
+        in_specs=[VMEM] * 13,
         out_specs=[VMEM] * 4,
         scratch_shapes=[
             vm((slab, length), BF16),
             vm((slab3, length), F32),
             vm((turned_rows, length), BF16),
             vm((length, slab3), BF16),
-            vm((3, halves, shards, rp, width), BF16),
-            vm((3, halves, shards, rp, width), BF16),
-            vm((3, shards, rp, width), BF16),
-            vm((3, minor - 1, MAJOR, rp, width), BF16),
-            vm((3, MAJOR - 1, rp, width), BF16),
-            vm((more, 3, rp, width), BF16),
+            vm((3, shards, rows_part, parts * block), BF16),
+            vm((3, parts * block, cols), BF16),
+            vm((3, shards, rows_part, block), BF16),
+            vm((3, MAJOR, minor, rows_part, cols), BF16),
+            vm((3, minor - 1, MAJOR, rows_part, cols), BF16),
+            vm((3, MAJOR - 1, rows_part, cols), BF16),
+            vm((2 * more + 1, 3, rows_part, cols), BF16),
             vm((shards, block, width), BF16),
             vm((minor - 1, MAJOR, block, width), BF16),
             vm((MAJOR - 1, block, width), BF16),
@@ -880,24 +925,24 @@
             vm((shards, rp, slab3), BF16),
             vm((shards, rp, slab3), BF16),
             vm((shards, rp, slab3), BF16),
-            vm((more, shards, rp, slab3), BF16),
+            vm((2 * more + 1, shards, rp, slab3), BF16),
             vm((shards, 8, 512), F32),
             vm((shards, 8, 512), F32),
             vm((2 * bits + 1, 8, 384), F32),
             dma((peers,)), dma((shards,)),
-            dma((3, halves)), dma((3, halves)), dma((3, halves)),
-            dma((3,)), dma((3,)),
-            dma((3, minor - 1, MAJOR)), dma((3, minor - 1, MAJOR)),
+            dma((3, 3)), dma((3, 3)),
+            dma((3, 4)), dma((3, 4)),
+            dma((3, minor - 1)), dma((3, minor - 1)),
             dma((3, MAJOR - 1)), dma((3, MAJOR - 1)),
-            dma((max(parts - 1, 1),)), dma((parts,)),
-            dma((more,)), dma((more,)),
+            dma((parts,)), dma((parts,)),
+            dma((max(more, 1),)), dma((max(more, 1),)),
             dma((minor - 1, MAJOR)), dma((minor - 1, MAJOR)),
             dma((MAJOR - 1,)), dma((MAJOR - 1,)),
             dma((halves,)), dma((halves,)),
             dma((1,)), dma((1,)),
             dma((peers,)), dma((shards,)),
-            dma((max(parts - 1, 1),)), dma((parts,)),
-            dma((more,)), dma((more,)),
+            dma((parts,)), dma((parts,)),
+            dma((max(more, 1),)), dma((max(more, 1),)),
             dma((peers,)), dma((shards,)),
             dma((bits,)), dma((bits,)),
         ],
@@ -905,7 +950,7 @@
             collective_id=1, has_side_effects=True, vmem_limit_bytes=58 << 20
         ),
         name="back",
-    )(grads, dctx, qkv, query, log, start, normed, wcols, vec, rows)
+    )(x, g_mixed, xt, dy, dctx, qkv, query, log, start, normed, wcols, vec, rows)
 
 
 def on_device(
@@ -921,18 +966,11 @@
     normed, qkv, query, log, vec, start, wcols, output, g_mixed, xt, dy, dctx, rows = front(
         shards, x, small, w_qkv, w_out, w_up, w_down, cotangent.reshape(block, width)
     )
-    grads = jnp.einsum("mat,mtd->mad", xt.reshape(3, width, block), dy, preferred_element_type=F32).astype(BF16)
-    parts = 4 if (width // shards) % 32 == 0 else 2
-    fin, gw, gn, small = back(
-        shards, replicas, grads.reshape(3, shards, parts, slab // parts, width), dctx, qkv, query, log, start, normed, wcols, vec, rows
+    fin, gw, input_grad, small = back(
+        shards, replicas, x, g_mixed, xt, dy, dctx, qkv, query, log, start, normed, wcols, vec, rows
     )
-    parts, rp = fin.shape[0], fin.shape[2]
-    fin = fin.transpose(1, 0, 2, 3).reshape(3, slab, width).astype(F32)
-    gw = gw.reshape(parts, shards, rp, 3, slab).transpose(0, 2, 3, 1, 4).reshape(slab, 3 * width).astype(F32)
-    xf = x.astype(F32)
-    r = lax.rsqrt(jnp.mean(xf * xf, axis=-1, keepdims=True) + EPS)
-    gain = vec[0]
-    input_grad = g_mixed + r * gain * gn - xf * (r * r * r) * jnp.mean(xf * gain * gn, axis=-1, keepdims=True)
+    gw = gw.reshape(slab, 3 * width).astype(F32)
+    fin = fin.astype(F32)
     unit = HEAD // shards
     return (
         output[None], input_grad[None], small[0, :slab], gw, small[6, :slab], small[7, :slab],

time: 282 us -> 231 us (0.82)
  Pallas kernels: 240 us -> 212 us
  local copies, waits for them, and re-layouts: 25.3 us -> 10.5 us
  matrix products: 7.99 us -> 0 us
    pallas_call x1, Pallas kernels: 147 us -> 120 us  [back(): pl.pallas_call(functools.partial(back_kernel, shards, replicas, parts, 2...]
    convert_element_type x3 -> x0, local copies, waits for them, and re-layouts: 16.5 us -> none  [on_device(): gw.reshape(parts, shards, rp, 3, slab).transpose(0, 2, 3, 1, 4)]
    dot_general x1 -> x0, matrix products: 7.99 us -> none  [on_device(): jnp.einsum('mat,mtd->mad', xt.reshape(3, width, block), dy, preferred_ele...]
    convert_element_type x1 -> x2, other arithmetic: 0.16 us -> 3.07 us  [the longest x1 2.88 us: on_device(): gw = gw.reshape(slab, 3 * width).astype(F32)]
where the time goes in v3:
time: 231 us; the launch traced here: 229 us
  Pallas kernels  212 us (92%)
  local copies, waits for them, and re-layouts  10.5 us (5%)
  other arithmetic  5.68 us (2%)
    pallas_call x1, Pallas kernels, back(): pl.pallas_call(functools.partial(back_kernel, shards, replicas, parts, 2...  120 us
    pallas_call x1, Pallas kernels, front(): pl.pallas_call(functools.partial(front_kernel, shards, wparts, fparts, 2...  92.4 us

profile of v3, /device:TPU:0, one launch (start us, length us, event | category | flops | bytes accessed | tf_op | source)
XLA Modules:
  0.0 229.2 jit_solution(7052203120884020953)
XLA Ops:
  0.6 0.7 subtract_convert_fusion
  1.3 0.7 broadcast_compare_fusion
  2.0 0.7 broadcast_in_dim.40
  2.6 0.7 broadcast_in_dim.46
  3.3 0.7 broadcast_in_dim.47
  3.9 0.7 broadcast_in_dim.41
  4.6 0.7 broadcast_in_dim.42
  5.3 0.7 broadcast_in_dim.43
  5.9 0.7 broadcast_in_dim.44
  6.6 1.3 convert_add_fusion.small_ref
  7.9 92.4 %front.1 = (bf16[1024,1280]{1,0:T(8,128)(2,1)}, bf16[480,1024]{1,0:T(8,128)(2,1)}, f32[160,1024]{1,0:T(8,128)}, f32[8,1024]{1,0:T(8,128)}, f32[8,1280]{1,0:T(8,1...) custom-call(bf16[128,1280]{1,0:T(8,128)(2,1)} %bitcast.23, ...), custom_call_target="tpu_custom_call" | custom-call | tf_op jit(solution)/shard_map/front/pallas_call | solution.py:450
  100.2 120.0 %back.1 = (bf16[3,160,1280]{2,1,0:T(8,128)(2,1)}, bf16[4,40,3840]{2,1,0:T(8,128)(2,1)}, f32[128,1280]{1,0:T(8,128)}, f32[8,384]{1,0:T(8,128)}) custom-call(bf16[128,1280]{1,0:T(8,128)(2,1)} %bitcast.24, f32[128,1280]{1,0:T(8,128)} %get-tuple-element.32.gmixed_ref, bf16[3,8,2,80,128]{4,3,2,1,0:T(8,128)(2,1)} %get-tuple-element.33.xt_ref, ...), custom_call_target="tpu_custom_call" | custom-call | tf_op jit(solution)/shard_map/back/pallas_call | solution.py:898
  220.2 0.0 copy-start
  220.2 1.3 slice_bitcast_fusion.3
  221.5 1.5 fusion
  223.0 2.9 %bitcast_convert_fusion = f32[160,3840]{1,0:T(8,128)} fusion(bf16[4,40,3840]{2,1,0:T(8,128)(2,1)} %get-tuple-element.46), kind=kLoop, calls=%fused_computation | loop fusion | flops 614400 | bytes 3686400 | tf_op jit(solution)/shard_map/convert_element_type | solution.py:972
  225.9 0.0 copy-done
  225.9 0.2 convert_element_type.46
  226.1 0.0 copy-start.2
  226.1 0.0 copy-start.1
  226.2 1.5 slice_bitcast_fusion
  227.6 0.0 copy-done.2
  227.6 0.7 copy.32
  228.4 0.0 copy-done.1
  228.4 0.8 copy.33
Async XLA Ops:
  220.2 5.7 %copy-start = (bf16[3,160,1280]{2,1,0:T(8,128)(2,1)S(1)}, bf16[3,160,1280]{2,1,0:T(8,128)(2,1)}, u32[]{:S(2)}) copy-start(bf16[3,160,1280]{2,1,0:T(8,128)(2,1)} %get-tuple-element.47) | copy-start | bytes 3686404
  226.1 1.5 copy-start.2
  226.1 2.2 copy-start.1

commit v4 on v3

v4 whole, which is shorter than its diff:
```python
import functools
import math

import jax
import jax.numpy as jnp
from jax import lax
from jax.experimental import pallas as pl
from jax.experimental.pallas import tpu as pltpu
from jax.sharding import PartitionSpec as P

HEADS = 16
HEAD = 80
EPS = 1e-06
QUERY_BASE = 1.442695041
MASKED = -1000000000.0
MESH = pl.DeviceIdType.MESH
MAJOR = 4
VMEM = pl.BlockSpec(memory_space=pltpu.VMEM)
ANY = pl.BlockSpec(memory_space=pl.ANY)
F32 = jnp.float32
BF16 = jnp.bfloat16
NN = (((1,), (0,)), ((), ()))
NT = (((1,), (1,)), ((), ()))
TN = (((0,), (0,)), ((), ()))


def dot(lhs, rhs, dims=NN):
    return lax.dot_general(lhs, rhs, dims, preferred_element_type=F32)


class Place:
    def __init__(self, shards):
        self.shards = shards
        self.minor = shards // MAJOR
        self.me = lax.axis_index("shard")
        self.rep = lax.axis_index("replica")
        self.a = self.me // self.minor
        self.b = lax.rem(self.me, self.minor)
        self.started = []

    def at(self, da, db):
        a = lax.rem(self.a + da + MAJOR, MAJOR)
        b = lax.rem(self.b + db + self.minor, self.minor)
        return a * self.minor + b

    def peers(self):
        return [(da, db) for da in range(MAJOR) for db in range(self.minor) if da or db]

    def flip(self, mask):
        bit = lax.rem(self.rep // mask, 2)
        return self.rep + mask - 2 * mask * bit

    def greet(self, masks):
        barrier = pltpu.get_barrier_semaphore()
        for da, db in self.peers():
            pl.semaphore_signal(
                barrier, inc=1, device_id=(self.at(da, db), self.rep), device_id_type=MESH
            )
        for mask in masks:
            pl.semaphore_signal(
                barrier, inc=1, device_id=(self.me, self.flip(mask)), device_id_type=MESH
            )
        pl.semaphore_wait(barrier, len(self.peers()) + len(masks))

    def send(self, src, dst, ssem, rsem, shard=None, rep=None, when=None):
        copy = pltpu.make_async_remote_copy(
            src_ref=src,
            dst_ref=dst,
            send_sem=ssem,
            recv_sem=rsem,
            device_id=(self.me if shard is None else shard, self.rep if rep is None else rep),
            device_id_type=MESH,
        )
        if when is None:
            copy.start()
        else:
            @pl.when(when)
            def _():
                copy.start()
        self.started.append((when, copy))

    def arrived(self, dst, rsem):
        pltpu.make_async_remote_copy(
            src_ref=dst,
            dst_ref=dst,
            send_sem=rsem,
            recv_sem=rsem,
            device_id=(self.me, self.rep),
            device_id_type=MESH,
        ).wait_recv()

    def exchange(self, src, dst, ssem, rsem, rep):
        self.send(src, dst, ssem, rsem, rep=rep)
        self.arrived(dst, rsem)
        self.started.pop()[1].wait_send()

    def settle(self):
        for when, copy in self.started:
            if when is None:
                copy.wait_send()
            else:
                @pl.when(when)
                def _():
                    copy.wait_send()
        self.started = []


class Line:
    def __init__(self, at, slot, major_send, minor_send, recv):
        self.at, self.slot = at, slot
        self.major_send, self.minor_send, self.recv = major_send, minor_send, recv

    def onward(self, origin, up, down, d):
        at = self.at
        if up is not None:
            at.send(
                self.slot(origin), self.slot(origin), self.major_send.at[0, d], self.recv(origin),
                shard=lax.min(at.a + 1, MAJOR - 1) * at.minor + at.b, when=up,
            )
        if down is not None:
            at.send(
                self.slot(origin), self.slot(origin), self.major_send.at[1, d], self.recv(origin),
                shard=lax.max(at.a - 1, 0) * at.minor + at.b, when=down,
            )

    def across(self, origin, when=None):
        at = self.at
        for db in range(1, at.minor):
            at.send(
                self.slot(origin), self.slot(origin), self.minor_send.at[origin // at.minor, db - 1],
                self.recv(origin), shard=at.at(0, db), when=when,
            )

    def begin(self):
        at = self.at
        self.onward(at.me, at.a + 1 < MAJOR, at.a > 0, 0)
        self.across(at.me)

    def sides(self, d):
        at = self.at
        for side in (-1, 1):
            ok = (at.a - d >= 0) if side < 0 else (at.a + d < MAJOR)
            origin = lax.max(at.a - d, 0) if side < 0 else lax.min(at.a + d, MAJOR - 1)
            yield side, ok, origin * at.minor + at.b

    def take(self, d, then=None):
        for side, ok, origin in self.sides(d):
            @pl.when(ok)
            def _():
                self.at.arrived(self.slot(origin), self.recv(origin))

            if then is not None:
                then(origin, ok)

    def along(self, d):
        at = self.at
        if d + 1 < MAJOR:
            for side, ok, origin in self.sides(d):
                if side < 0:
                    self.onward(origin, ok & (at.a + 1 < MAJOR), None, d)
                else:
                    self.onward(origin, None, ok & (at.a > 0), d)

    def aside(self, d):
        for side, ok, origin in self.sides(d):
            self.across(origin, when=ok)

    def step(self, d, then=None):
        self.take(d, then)
        self.along(d)
        self.aside(d)


def parts_of(rows):
    return 4 if rows % 32 == 0 else 2


def part_box(part, parts, rows, cols):
    if parts == 4:
        i, j, rows = lax.rem(part, 2), part // 2, rows // 2
    else:
        i, j = 0, part
    return i * rows, rows, j * (cols // 2), cols // 2


def flipped(part, mask):
    bit = lax.rem(part // mask, 2)
    return part + mask - 2 * mask * bit


def layer_kernel(
    shards, replicas, wparts, parts, qblock,
    x_ref, small_ref, w_ref, wout_ref, wup_ref, wdown_ref, cot_ref,
    out_ref, fin_ref, gw_ref, gin_ref, small_out_ref,
    normed_ref, qkv_ref, query_ref, log_ref, vec_ref, start_ref, wcols_ref,
    xt_ref, dy_ref, dctx_ref, row_ref, gmixed_ref,
    xg, packets, pieces, turned, context, att, weights,
    dctx, grads, proj, left, right, stash, sums, from_x, from_z, extra,
    gw, gw_core, gw_y, gw_sum, gw_land, gw_extra,
    windows, small_land, small_got,
    xm_send, xn_send, x_recv, p_send, p_recv, w_send, w_recv, wc_send,
    fm_send, fn_send, f_recv, fy_send, fc_send, local_sem, a_send, a_recv,
    d_send, d_recv, gy_send, gy_recv, gc_send, gc_recv, gx_send, gx_recv, gz_send, gz_recv,
    r_send, r_recv, e_send, e_recv, nx_send, nx_recv, nz_send, nz_recv,
    vc_send, vc_recv, vy_send, vy_recv, va_send, va_recv, vr_send, vr_recv, ve_send, ve_recv,
    s_send, s_recv, b_send, b_recv,
):
    at = Place(shards)
    me, minor = at.me, at.minor
    block, width = x_ref.shape
    length = shards * block
    slab = width // shards
    slab3 = 3 * slab
    local = slab // HEAD
    peers = at.peers()
    masks = (2, 1) if parts == 4 else (1,)
    every = []
    bit = 1
    while bit < replicas:
        every.append(bit)
        bit *= 2
    extras = [m for m in every if m >= parts]
    mine = lax.rem(at.rep, parts)
    wpart = lax.rem(at.rep, wparts)

    loads = []
    for m, ref in enumerate((wout_ref, wup_ref, wdown_ref)):
        copy = pltpu.make_async_copy(
            ref, weights.at[m, pl.ds(pl.multiple_of(me * slab, 16), slab), :], local_sem.at[m]
        )
        copy.start()
        loads.append(copy)
    xg[me] = x_ref[...]
    packets[me] = small_ref[:8]
    at.greet(tuple(every))

    def wslot(origin, part):
        row, rows, col, cols = part_box(part, parts, slab, width)
        return weights.at[
            :,
            pl.ds(pl.multiple_of(origin * slab + row, 16), rows),
            pl.ds(pl.multiple_of(col, 128), cols),
        ]

    rows_line = Line(at, lambda o: xg.at[o], xm_send, xn_send, lambda o: x_recv.at[o])
    ffn_line = Line(
        at, lambda o: wslot(o, mine), fm_send, fn_send, lambda o: f_recv.at[o, mine]
    )

    def to_replicas(origin, when=None):
        slot = wslot(origin, mine)
        for mask in masks:
            sem = fy_send.at[origin] if mask == 2 else fc_send.at[origin, 0]
            at.send(slot, slot, sem, f_recv.at[origin, mine], rep=at.flip(mask), when=when)

    rows_line.begin()
    for i, (da, db) in enumerate(peers):
        at.send(packets.at[me], packets.at[me], p_send.at[i], p_recv.at[me], shard=at.at(da, db))
    for copy in loads:
        copy.wait()
    ffn_line.begin()

    cut = slab // wparts
    for j in range(shards):
        for t in range(3):
            first = t * width + j * slab
            pieces[j, :, :, t * slab : (t + 1) * slab] = w_ref[:, first : first + slab].reshape(
                wparts, cut, slab
            )
    for i, (da, db) in enumerate(peers):
        dest = at.at(da, db)
        at.send(
            pieces.at[dest, wpart], wcols_ref.at[me, wpart], w_send.at[i], w_recv.at[me, wpart], shard=dest
        )
    wcols_ref[me] = pieces[me]

    rows_line.step(1)
    ffn_line.step(1, to_replicas)

    def ffn_minor(distance):
        for db in range(1, minor):
            sides = ((-1, 1) if distance else (0,))
            for side in sides:
                a = at.a + side * distance
                ok = None
                if distance:
                    ok = (a >= 0) & (a < MAJOR)
                origin = lax.max(lax.min(a, MAJOR - 1), 0) * minor + lax.rem(at.b + db, minor)
                slot = wslot(origin, mine)
                if ok is None:
                    at.arrived(slot, f_recv.at[origin, mine])
                else:
                    @pl.when(ok)
                    def _():
                        at.arrived(slot, f_recv.at[origin, mine])
                to_replicas(origin, ok)

    ffn_minor(0)

    if wparts == 2:
        for i, (da, db) in enumerate(peers):
            origin = at.at(-da, -db)
            slot = wcols_ref.at[origin, wpart]
            at.arrived(slot, w_recv.at[origin, wpart])
            at.send(slot, slot, wc_send.at[i], w_recv.at[origin, wpart], rep=at.flip(1))

    for da, db in peers:
        origin = at.at(-da, -db)
        at.arrived(packets.at[origin], p_recv.at[origin])
    vectors = jnp.zeros((8, width), F32)
    scales = jnp.zeros((1, 128), F32)
    lanes = lax.broadcasted_iota(jnp.int32, (8, width), 1)
    unit = HEAD // shards
    for j in range(shards):
        piece = packets[j]
        wide = jnp.concatenate([piece, jnp.zeros((8, width - piece.shape[1]), F32)], axis=1)
        wide = jnp.where(lanes < slab, wide, 0.0)
        vectors = vectors + (pltpu.roll(wide, j * slab, 1) if j else wide)
        scale = jnp.where(lanes[0:1, :128] < unit, piece[5:6, :128], 0.0)
        scales = scales + (pltpu.roll(scale, j * unit, 1) if j else scale)
        start_ref[:, j * block : (j + 1) * block] = jnp.broadcast_to(piece[6:7, :block], (8, block))
    rows = lax.broadcasted_iota(jnp.int32, (8, width), 0)
    vec_ref[...] = jnp.where(rows < 5, vectors, 0.0)
    vec_ref[5:6, :128] = scales
    gain = vec_ref[0:1, :]
    column = jnp.broadcast_to(scales, (128, 128)).T[:HEAD, 0:1]
    soft = jnp.maximum(column, 0.0) + jnp.log(1.0 + jnp.exp(-jnp.abs(column)))
    factor = jnp.concatenate([QUERY_BASE / math.sqrt(HEAD) * soft] * local, axis=0)
    own = small_ref[8:16, :]
    tall = jnp.concatenate([own, jnp.zeros((120, 256), F32)], axis=0)
    tall = jnp.concatenate([tall[:, :128].T, tall[:, 128:].T], axis=0)
    bias_query = tall[:slab, 0:1]
    bias_value = tall[:slab, 1:2]

    rows_line.step(2)
    ffn_line.step(2, to_replicas)
    ffn_minor(1)
    for da, db in peers:
        origin = at.at(-da, -db)
        last = wparts - 1 - wpart
        at.arrived(wcols_ref.at[origin, last], w_recv.at[origin, last])
    turned[...] = wcols_ref[...].reshape(width, slab3).T

    def project(origin):
        rows_in = xg[origin].astype(F32)
        scale = lax.rsqrt(jnp.mean(rows_in * rows_in, axis=-1, keepdims=True) + EPS)
        normed = (rows_in * scale * gain).astype(BF16)
        tokens = pl.ds(pl.multiple_of(origin * block, block), block)
        normed_ref[tokens, :] = normed
        out = dot(turned[...], normed, NT)
        query = out[:slab] + bias_query
        query_ref[:, tokens] = query
        qkv_ref[:slab, tokens] = (query * factor).astype(BF16)
        qkv_ref[slab : 2 * slab, tokens] = out[slab : 2 * slab].astype(BF16)
        qkv_ref[2 * slab :, tokens] = (out[2 * slab :] + bias_value).astype(BF16)

    rows_line.step(3)
    ffn_line.step(3, to_replicas)

    def project_major(i, carry):
        project(at.at(i, 0))
        return carry

    def project_minor(i, carry):
        origin = at.at(lax.rem(i, MAJOR), 1 + i // MAJOR)
        at.arrived(xg.at[origin], x_recv.at[origin])
        project(origin)
        return carry

    lax.fori_loop(0, MAJOR, project_major, 0)
    ffn_minor(2)
    lax.fori_loop(0, shards - MAJOR, project_minor, 0)
    ffn_minor(3)

    log_ref[...] = jnp.zeros_like(log_ref)
    for i in range(length // qblock):
        reach = (i + 1) * qblock
        span = slice(i * qblock, reach)
        starts = start_ref[0:1, span]
        key_place = lax.broadcasted_iota(jnp.int32, (reach, qblock), 0).astype(F32)
        query_place = (i * qblock + lax.broadcasted_iota(jnp.int32, (1, qblock), 1)).astype(F32)
        allowed = (key_place >= starts) & (key_place <= query_place)
        for h in range(local):
            head = slice(h * HEAD, (h + 1) * HEAD)
            queries = qkv_ref[h * HEAD : (h + 1) * HEAD, span]
            keys = qkv_ref[slab + h * HEAD : slab + (h + 1) * HEAD, :reach]
            values = qkv_ref[2 * slab + h * HEAD : 2 * slab + (h + 1) * HEAD, :reach]
            scores = jnp.where(allowed, dot(keys, queries, TN), MASKED)
            top = jnp.max(scores, axis=0, keepdims=True)
            powers = jnp.exp(scores - top)
            total = jnp.sum(powers, axis=0, keepdims=True)
            probs = (powers * (1.0 / total)).astype(BF16)
            log_ref[h : h + 1, span] = top + jnp.log(total)
            context[head, span] = dot(values, probs).astype(BF16)
        heads = pl.ds(pl.multiple_of(me * slab, 16), slab)
        for j in range(i * qblock // block, reach // block):
            piece = slice(j * block, (j + 1) * block)
            at.send(context.at[:, piece], att.at[heads, :], a_send.at[j], a_recv.at[me], shard=j, when=me != j)

            @pl.when(me == j)
            def _():
                att[heads, :] = context[:, piece]

    order = [(0, db) for db in range(1, minor)]
    order += [(da, db) for da in range(1, MAJOR) for db in range(minor)]
    if parts == 4:
        for da, db in order:
            origin = at.at(da, db)
            part = flipped(mine, 2)
            slot = wslot(origin, part)
            at.arrived(slot, f_recv.at[origin, part])
            at.send(slot, slot, fc_send.at[origin, 1], f_recv.at[origin, part], rep=at.flip(1))
    for da, db in peers:
        origin = at.at(-da, -db)
        at.arrived(att.at[pl.ds(pl.multiple_of(origin * slab, 16), slab), :], a_recv.at[origin])
    others = [flipped(mine, 1)] + ([flipped(flipped(mine, 1), 2)] if parts == 4 else [])
    for da, db in order:
        origin = at.at(da, db)
        for part in others:
            at.arrived(wslot(origin, part), f_recv.at[origin, part])

    slab3 = 3 * slab
    cols = width // 2
    core = lax.rem(at.rep, 2)
    i_part = lax.rem(mine, 2) if parts == 4 else 0
    j_part = mine // 2 if parts == 4 else mine
    mats = (2, 1, 0)

    def lane(n, size):
        return pl.ds(pl.multiple_of(n * size, 128), size)

    def slot(n):
        return slice(n * block, (n + 1) * block)

    def meet_near(m):
        near = parts // 2
        at.send(
            xt_ref.at[m, :, 1 - i_part if parts == 4 else 0], left.at[m, :, :, slot(near)],
            gc_send.at[m, 0], gc_recv.at[m, 0], rep=at.flip(1),
        )
        at.send(
            dy_ref.at[m, :, lane(j_part if parts == 4 else 1 - j_part, cols)], right.at[m, slot(near), :],
            gc_send.at[m, 1], gc_recv.at[m, 1], rep=at.flip(1),
        )
        left[m, :, :, slot(0)] = xt_ref[m, :, i_part]
        right[m, slot(0), :] = dy_ref[m, :, lane(j_part, cols)]

    def meet_far(m):
        if parts == 4:
            far = at.flip(2)
            at.send(
                xt_ref.at[m, :, i_part], left.at[m, :, :, slot(1)], gy_send.at[m, 0], gy_recv.at[m, 0], rep=far
            )
            at.send(
                dy_ref.at[m, :, lane(1 - j_part, cols)], right.at[m, slot(1), :],
                gy_send.at[m, 1], gy_recv.at[m, 1], rep=far,
            )
            at.send(xt_ref.at[m, :, 1 - i_part], stash.at[m], gy_send.at[m, 2], gy_recv.at[m, 2], rep=far)

    def relay(m):
        if parts == 4:
            at.arrived(left.at[m, :, :, slot(1)], gy_recv.at[m, 0])
            at.arrived(right.at[m, slot(1), :], gy_recv.at[m, 1])
            at.arrived(stash.at[m], gy_recv.at[m, 2])
            at.send(stash.at[m], left.at[m, :, :, slot(3)], gc_send.at[m, 2], gc_recv.at[m, 2], rep=at.flip(1))
            at.send(
                right.at[m, slot(1), :], right.at[m, slot(3), :], gc_send.at[m, 3], gc_recv.at[m, 3], rep=at.flip(1)
            )

    def weight(m):
        near = 2 if parts == 4 else 1
        at.arrived(left.at[m, :, :, slot(near)], gc_recv.at[m, 0])
        at.arrived(right.at[m, slot(near), :], gc_recv.at[m, 1])
        if parts == 4:
            at.arrived(left.at[m, :, :, slot(3)], gc_recv.at[m, 2])
            at.arrived(right.at[m, slot(3), :], gc_recv.at[m, 3])
        rows = left.shape[1] * left.shape[2]
        out = dot(left[m].reshape(rows, parts * block), right[m])
        sums[m] = out.reshape(sums.shape[1:]).astype(BF16)

    def weight_across(m):
        for db in range(1, minor):
            at.send(
                sums.at[m, :, lax.rem(at.b + db, minor)], from_x.at[m, db - 1],
                gx_send.at[m, db - 1], gx_recv.at[m, db - 1], shard=at.at(0, db),
            )

    ahead = jnp.where(at.a < MAJOR // 2, 1, -1)
    middle = (at.a > 0) & (at.a < MAJOR - 1)

    def turn(n):
        return jnp.where(at.a < MAJOR // 2, MAJOR - 1 - n, n)

    class Chain:
        def __init__(self, own, land, ssem, rsem):
            self.own, self.land, self.ssem, self.rsem = own, land, ssem, rsem

        def go(self, n, when=None):
            t = turn(n)
            way = -ahead if n == 3 else ahead
            to = lax.max(lax.min(at.a + way, MAJOR - 1), 0) * minor + at.b
            dst = jnp.where(middle, MAJOR, t) if n == 1 else t
            at.send(self.own(t), self.land(dst), self.ssem.at[n], self.rsem.at[dst], shard=to, when=when)

        def summed(self, n):
            if n < 3:
                self.go(n, jnp.logical_not(middle))

        def joined(self, n):
            t = turn(n)

            @pl.when(middle)
            def _():
                at.arrived(self.land(t), self.rsem.at[t])
                self.own(t)[...] = self.own(t)[...] + self.land(t)[...]

            self.go(n, middle)

        def result(self):
            at.arrived(self.land(at.a), self.rsem.at[at.a])
            total = self.own(at.a)[...].astype(F32) + self.land(at.a)[...].astype(F32)
            self.own(at.a)[...] = total.astype(BF16)

            @pl.when(middle)
            def _():
                at.arrived(self.land(MAJOR), self.rsem.at[MAJOR])
                self.own(at.a)[...] = (total + self.land(MAJOR)[...].astype(F32)).astype(BF16)

            return self.own(at.a)[...]

    ffn_sums = {
        m: Chain(
            lambda t, m=m: sums.at[m, t, at.b], lambda n, m=m: from_z.at[m, n], gz_send.at[m], gz_recv.at[m]
        )
        for m in mats
    }

    def land_x(db, t):
        return weights.at[db - 1, pl.ds(pl.multiple_of(t * block, block), block), :]

    def land_z(n):
        return weights.at[0, pl.ds(pl.multiple_of((MAJOR + n) * block, block), block), :]

    row_sums = Chain(lambda t: xg.at[t * minor + at.b], land_z, nz_send, nz_recv)

    def rows_across(n):
        t = turn(n)
        for db in range(1, minor):
            to = t * minor + lax.rem(at.b + db, minor)
            at.send(
                xg.at[to], land_x(db, t), nx_send.at[db - 1, n], nx_recv.at[db - 1, t], shard=at.at(0, db)
            )

    def rows_summed(n):
        t = turn(n)
        own = row_sums.own(t)
        total = own[...].astype(F32)
        for db in range(1, minor):
            at.arrived(land_x(db, t), nx_recv.at[db - 1, t])
            total = total + land_x(db, t)[...].astype(F32)
        own[...] = total.astype(BF16)
        row_sums.summed(n)

    def weight_summed(m):
        for db in range(1, minor):
            at.arrived(from_x.at[m, db - 1], gx_recv.at[m, db - 1])
        for n in range(MAJOR):
            t = turn(n)
            total = sums[m, t, at.b].astype(F32)
            for db in range(1, minor):
                total = total + from_x[m, db - 1, t].astype(F32)
            sums[m, t, at.b] = total.astype(BF16)
            ffn_sums[m].summed(n)

    def weight_joined(m, n):
        ffn_sums[m].joined(n)

    def fin_slot(part, m=None):
        row, rows, col, wide = part_box(part, parts, slab, width)
        box = (pl.ds(pl.multiple_of(row, 16), rows), pl.ds(pl.multiple_of(col, 128), wide))
        return fin_ref.at[(slice(None) if m is None else m,) + box]

    def weight_done(m):
        fin_slot(mine, m)[...] = ffn_sums[m].result()

    forward, at.started = at.started, []
    keep_row = small_ref[10:11, :block]
    b_out, gain_two, b_up, b_down = (vec_ref[i : i + 1, :] for i in range(1, 5))
    halves = xt_ref.shape[2]

    def split_rows(value):
        return value.reshape(shards, halves, slab // halves, block)

    att_t = (att[...].astype(F32) * keep_row).astype(BF16)
    dy_ref[2] = cot_ref[...]
    mixed = x_ref[...].astype(F32) + dot(att_t.T, weights[0]) + b_out
    r = lax.rsqrt(jnp.mean(mixed * mixed, axis=-1, keepdims=True) + EPS)
    normed_two = (mixed * r * gain_two).astype(BF16)
    hidden = dot(normed_two, weights[1]) + b_up
    s = 1.0 / (1.0 + jnp.exp(-hidden))
    act = (hidden * s).astype(BF16)
    xt_ref[2] = split_rows(act.T)
    meet_far(2)
    meet_near(2)
    cot = cot_ref[...].astype(F32)
    g_hidden = dot(cot_ref[...], weights[2], NT) * (s + hidden * s * (1.0 - s))
    low = g_hidden.astype(BF16)
    g_normed = dot(low, weights[1], NT)
    weighted = gain_two * g_normed
    g_mixed = cot + r * weighted - mixed * (r * r * r) * jnp.mean(mixed * weighted, axis=-1, keepdims=True)
    g_low = g_mixed.astype(BF16)
    out_ref[...] = (mixed + dot(act, weights[2]) + b_down).astype(BF16)
    dctx_ref[...] = (dot(weights[0], g_low, NT).astype(BF16).astype(F32) * keep_row).astype(BF16)
    backward, at.started = at.started, forward
    at.settle()
    at.started = backward
    for i, (da, db) in enumerate(peers):
        dest = at.at(da, db)
        at.send(
            dctx_ref.at[pl.ds(pl.multiple_of(dest * slab, 16), slab), :],
            dctx.at[:, lane(me, block)], d_send.at[i], d_recv.at[me], shard=dest,
        )
    dctx[:, lane(me, block)] = dctx_ref[pl.ds(pl.multiple_of(me * slab, 16), slab), :]
    dy_ref[1] = low
    xt_ref[1] = split_rows(normed_two.T)
    meet_near(1)
    gmixed_ref[...] = g_mixed
    dy_ref[0] = g_low
    xt_ref[0] = split_rows(att_t)
    meet_near(0)
    row_ref[...] = jnp.zeros_like(row_ref)
    row_ref[1:2, :] = jnp.sum(g_mixed, axis=0, keepdims=True)
    row_ref[2:3, :] = jnp.sum(g_normed * mixed * r, axis=0, keepdims=True)
    row_ref[3:4, :] = jnp.sum(g_hidden, axis=0, keepdims=True)
    row_ref[4:5, :] = jnp.sum(cot, axis=0, keepdims=True)

    base = QUERY_BASE / math.sqrt(HEAD)
    factor = base * soft
    grads[...] = jnp.zeros_like(grads)
    for da, db in peers:
        origin = at.at(-da, -db)
        at.arrived(dctx.at[:, lane(origin, block)], d_recv.at[origin])

    def attend(i):
        reach = (i + 1) * qblock
        span = slice(i * qblock, reach)
        starts = start_ref[0:1, span]
        key_place = lax.broadcasted_iota(jnp.int32, (reach, qblock), 0).astype(F32)
        query_place = (i * qblock + lax.broadcasted_iota(jnp.int32, (1, qblock), 1)).astype(F32)
        allowed = (key_place >= starts) & (key_place <= query_place)
        for h in range(local):
            queries = qkv_ref[h * HEAD : (h + 1) * HEAD, span]
            keys = qkv_ref[slab + h * HEAD : slab + (h + 1) * HEAD, :reach]
            values = qkv_ref[2 * slab + h * HEAD : 2 * slab + (h + 1) * HEAD, :reach]
            gctx = dctx[h * HEAD : (h + 1) * HEAD, span]
            scores = dot(keys, queries, TN)
            probs = jnp.where(allowed, jnp.exp(scores - log_ref[h : h + 1, span]), 0.0)
            gprobs = dot(values, gctx, TN)
            delta = jnp.sum(probs * gprobs, axis=0, keepdims=True)
            gscores = (probs * (gprobs - delta)).astype(BF16)
            low = probs.astype(BF16)
            grads[h * HEAD : (h + 1) * HEAD, span] = dot(keys, gscores)
            kv = slice(slab + h * HEAD, slab + (h + 1) * HEAD)
            grads[kv, :reach] += dot(queries, gscores, NT)
            kv = slice(2 * slab + h * HEAD, 2 * slab + (h + 1) * HEAD)
            grads[kv, :reach] += dot(gctx, low, NT)

    steps = length // qblock
    for i in range(steps):
        attend(i)
        if i == 1:
            relay(2)
            meet_far(1)
        if i == 2:
            weight(2)
            weight_across(2)

    gscale = jnp.zeros((HEAD, 1), F32)
    for h in range(local):
        rows = slice(h * HEAD, (h + 1) * HEAD)
        scaled = grads[rows, :]
        gscale = gscale + jnp.sum(scaled * query_ref[rows, :], axis=1, keepdims=True)
        grads[rows, :] = scaled * factor
    gscale = gscale * (base / (1.0 + jnp.exp(-column)))
    bias_q = jnp.sum(grads[:slab, :], axis=1, keepdims=True)
    bias_v = jnp.sum(grads[2 * slab :, :], axis=1, keepdims=True)
    tall_rows = grads.shape[0]
    low_t = grads[...].astype(BF16)
    if tall_rows % 128:
        low_t = jnp.concatenate([low_t, jnp.zeros((-tall_rows % 128, length), BF16)], axis=0)
    proj[...] = low_t.T[:, :slab3]

    wcols = wcols_ref[...].reshape(width, slab3)

    def partial(origin, acc):
        tokens = lane(origin, block)
        out = dot(proj[tokens, :], wcols, NT)
        xg[origin] = out.astype(BF16)
        weighted = out * normed_ref[tokens, :].astype(F32)
        return acc + jnp.sum(weighted.reshape(block // 8, 8, width), axis=0)

    rp = width // (shards * parts)
    halves = parts // 2
    whole = dot(normed_ref[...], proj[...], TN)
    gw[...] = whole.reshape(shards, parts, rp, slab3).astype(BF16)
    for k in range(halves):
        at.send(gw.at[:, (1 - core) + 2 * k], gw_core.at[k], vc_send.at[k], vc_recv.at[k], rep=at.flip(1))

    def away(i, acc):
        return partial(at.at(lax.rem(i, MAJOR), 1 + i // MAJOR), acc)

    gain_rows = jnp.zeros((8, width), F32)
    gain_rows = lax.fori_loop(0, shards - MAJOR, away, gain_rows)
    rows_across(0)
    rows_across(1)
    relay(1)
    meet_far(0)
    gain_rows = lax.fori_loop(0, MAJOR, lambda i, acc: partial(at.at(i, 0), acc), gain_rows)
    weight(1)
    weight_across(1)
    rows_across(2)
    weight_summed(2)
    for k in range(halves):
        at.arrived(gw_core.at[k], vc_recv.at[k])
        gw_core[k] = gw[:, core + 2 * k] + gw_core[k]
    km = mine // 2 if parts == 4 else 0
    rows_summed(0)
    weight_joined(2, 0)
    weight_joined(2, 1)
    weight_joined(2, 3)
    relay(0)
    if parts == 4:
        at.send(gw_core.at[1 - km], gw_y, vy_send.at[0], vy_recv.at[0], rep=at.flip(2))
    weight(0)
    weight_across(0)
    rows_across(3)

    gain_row = jnp.sum(gain_rows, axis=0, keepdims=True) / vec_ref[0:1, :]
    rows = row_ref[...]
    place = lax.broadcasted_iota(jnp.int32, (8, width), 0)
    rows = jnp.where(place == 0, jnp.broadcast_to(gain_row, (8, width)), rows)
    turn_in = jnp.concatenate(
        [jnp.broadcast_to(gscale, (HEAD, 128)), jnp.zeros((128 - HEAD, 128), F32)], axis=0
    )
    scale_row = jnp.broadcast_to(turn_in.T[0:1, :], (8, 128))
    scale_tile = jnp.where(lax.broadcasted_iota(jnp.int32, (8, 128), 0) == 5, scale_row, 0.0)
    for j in range(shards):
        first = min(j * slab // 128 * 128, width - 256)
        windows[j, :, :256] = rows[:, first : first + 256]
        windows[j, :, 256:] = scale_tile
    for i, (da, db) in enumerate(peers):
        dest = at.at(da, db)
        at.send(windows.at[dest], small_land.at[me], s_send.at[i], s_recv.at[me], shard=dest)
    small_land[me] = windows[me]

    if parts == 4:
        at.arrived(gw_y, vy_recv.at[0])
        gw_sum[...] = gw_core[km] + gw_y[...]
    else:
        gw_sum[...] = gw_core[0]
    for i, (da, db) in enumerate(peers):
        dest = at.at(da, db)
        at.send(gw_sum.at[dest], gw_land.at[me], va_send.at[i], va_recv.at[me], shard=dest)
    gw_land[me] = gw_sum[me]
    rows_summed(1)
    row_sums.joined(0)
    weight_summed(1)
    rows_summed(2)
    row_sums.joined(1)
    weight_joined(1, 0)
    weight_joined(1, 1)
    weight_joined(1, 3)
    weight_summed(0)
    rows_summed(3)
    weight_joined(0, 0)
    weight_joined(0, 1)
    weight_joined(0, 3)
    row_sums.joined(3)

    for da, db in peers:
        origin = at.at(-da, -db)
        at.arrived(small_land.at[origin], s_recv.at[origin])
    small = jnp.sum(small_land[...], axis=0)
    lanes = lax.broadcasted_iota(jnp.int32, (slab, 128), 1)
    sides = jnp.concatenate(
        [jnp.where(lanes == 6, bias_q, jnp.where(lanes == 7, bias_v, 0.0)), jnp.zeros((256 - slab, 128), F32)],
        axis=0,
    )
    sides = jnp.concatenate([sides[:128].T[:8], sides[128:].T[:8]], axis=1)
    shift = me * slab - lax.min(me * slab // 128 * 128, width - 256)
    window = pltpu.roll(small[:, :256], lax.rem(256 - shift, 256), 1)
    tall = lax.broadcasted_iota(jnp.int32, (8, 256), 0)
    small_got[0, :, :256] = jnp.where(tall < 5, window, sides)
    small_got[0, :, 256:] = pltpu.roll(small[:, 256:], lax.rem(128 - me * unit, 128), 1)

    def small_round(n):
        at.send(
            small_got.at[2 * n], small_got.at[2 * n + 1], b_send.at[n], b_recv.at[n], rep=at.flip(every[n])
        )

    def small_add(n):
        at.arrived(small_got.at[2 * n + 1], b_recv.at[n])
        small_got[2 * n + 2] = small_got[2 * n] + small_got[2 * n + 1]

    small_round(0)
    for da, db in peers:
        origin = at.at(-da, -db)
        at.arrived(gw_land.at[origin], va_recv.at[origin])
    for n, mask in enumerate(extras):
        at.exchange(gw_land, gw_extra.at[n], ve_send.at[n], ve_recv.at[n], at.flip(mask))
        gw_land[...] = gw_land[...] + gw_extra[n]
    for j in range(shards):
        for t in range(3):
            first = t * width + j * slab
            gw_ref[mine, :, first : first + slab] = gw_land[j, :, t * slab : (t + 1) * slab]

    def hand_round(ref_slot, send_sem, recv_sem):
        have, rounds, k = [mine], [], 0
        for mask in ((2, 1) if parts == 4 else (1,)):
            sends = []
            for part in have:
                sends.append((part, mask, k))
                k += 1
            fresh = [flipped(part, mask) for part in have]
            rounds.append((sends, fresh))
            have = have + fresh

        def go(n):
            for part, mask, k in rounds[n][0]:
                at.send(ref_slot(part), ref_slot(part), send_sem.at[k], recv_sem.at[part], rep=at.flip(mask))

        def take(n):
            for part in rounds[n][1]:
                at.arrived(ref_slot(part), recv_sem.at[part])

        return go, take, len(rounds)

    gw_go, gw_take, count = hand_round(lambda part: gw_ref.at[part], vr_send, vr_recv)
    fin_go, fin_take, _ = hand_round(fin_slot, r_send, r_recv)
    gw_go(0)
    small_add(0)
    small_round(1)

    for m in mats:
        weight_done(m)
    for n, mask in enumerate(extras):
        at.exchange(fin_slot(mine), extra.at[n], e_send.at[n], e_recv.at[n], at.flip(mask))
        fin_slot(mine)[...] = fin_slot(mine)[...] + extra[n]
    fin_go(0)
    total = row_sums.result().astype(F32)
    x = x_ref[...].astype(F32)
    r = lax.rsqrt(jnp.mean(x * x, axis=-1, keepdims=True) + EPS)
    weighted = vec_ref[0:1, :] * total
    gin_ref[...] = gmixed_ref[...] + r * weighted - x * (r * r * r) * jnp.mean(x * weighted, axis=-1, keepdims=True)

    for n in range(count):
        gw_take(n)
        if n + 1 < count:
            gw_go(n + 1)
        fin_take(n)
        if n + 1 < count:
            fin_go(n + 1)
    for n in range(1, len(every)):
        small_add(n)
        if n + 1 < len(every):
            small_round(n + 1)
    small_out_ref[...] = small_got[2 * len(every)]

    at.settle()


def layer(shards, replicas, inputs, small, w_qkv, w_out, w_up, w_down, cotangent):
    block, width = inputs.shape
    slab = width // shards
    slab3 = 3 * slab
    length = shards * block
    wparts = 2 if slab % 32 == 0 else 1
    parts = parts_of(slab)
    halves = parts // 2
    rp = slab // parts
    rows_part = slab // 2 if parts == 4 else slab
    cols = width // 2
    minor = shards // MAJOR
    peers = shards - 1
    bits = (replicas - 1).bit_length()
    more = bits - (parts - 1).bit_length()
    shape = jax.ShapeDtypeStruct
    dma = pltpu.SemaphoreType.DMA
    vm = pltpu.VMEM
    return pl.pallas_call(
        functools.partial(layer_kernel, shards, replicas, wparts, parts, 2 * block),
        out_shape=(
            shape((block, width), BF16),
            shape((3, slab, width), BF16),
            shape((parts, rp, 3 * width), BF16),
            shape((block, width), F32),
            shape((8, 384), F32),
        ),
        in_specs=[VMEM] * 3 + [ANY] * 3 + [VMEM],
        out_specs=[VMEM] * 5,
        scratch_shapes=[
            vm((length, width), BF16),
            vm((slab3, length), BF16),
            vm((slab, length), F32),
            vm((8, length), F32),
            vm((8, width), F32),
            vm((8, length), F32),
            vm((shards, wparts, slab // wparts, slab3), BF16),
            vm((3, shards, halves, slab // halves, block), BF16),
            vm((3, block, width), BF16),
            vm((width, block), BF16),
            vm((8, width), F32),
            vm((block, width), F32),
            vm((shards, block, width), BF16),
            vm((shards, 8, 256), F32),
            vm((shards, wparts, slab // wparts, slab3), BF16),
            vm((slab3, width), BF16),
            vm((slab, length), BF16),
            vm((width, block), BF16),
            vm((3, width, width), BF16),
            vm((slab, length), BF16),
            vm((slab3, length), F32),
            vm((length, slab3), BF16),
            vm((3, shards, rows_part, parts * block), BF16),
            vm((3, parts * block, cols), BF16),
            vm((3, shards, rows_part, block) if parts == 4 else (1, 1, 16, block), BF16),
            vm((3, MAJOR, minor, rows_part, cols), BF16),
            vm((3, minor - 1, MAJOR, rows_part, cols), BF16),
            vm((3, MAJOR + 1, rows_part, cols), BF16),
            vm((max(more, 1), 3, rows_part, cols), BF16),
            vm((shards, parts, rp, slab3), BF16),
            vm((halves, shards, rp, slab3), BF16),
            vm((shards, rp, slab3) if parts == 4 else (1, 16, 128), BF16),
            vm((shards, rp, slab3), BF16),
            vm((shards, rp, slab3), BF16),
            vm((max(more, 1), shards, rp, slab3), BF16),
            vm((shards, 8, 384), F32),
            vm((shards, 8, 384), F32),
            vm((2 * bits + 1, 8, 384), F32),
            dma((2, MAJOR)), dma((MAJOR, minor - 1)), dma((shards,)),
            dma((peers,)), dma((shards,)),
            dma((peers,)), dma((shards, wparts)), dma((peers,)),
            dma((2, MAJOR)), dma((MAJOR, minor - 1)), dma((shards, parts)),
            dma((shards,)), dma((shards, 2)),
            dma((3,)), dma((shards,)), dma((shards,)),
            dma((peers,)), dma((shards,)),
            dma((3, 3)), dma((3, 3)),
            dma((3, 4)), dma((3, 4)),
            dma((3, minor - 1)), dma((3, minor - 1)),
            dma((3, MAJOR)), dma((3, MAJOR + 1)),
            dma((parts,)), dma((parts,)),
            dma((max(more, 1),)), dma((max(more, 1),)),
            dma((minor - 1, MAJOR)), dma((minor - 1, MAJOR)),
            dma((MAJOR,)), dma((MAJOR + 1,)),
            dma((halves,)), dma((halves,)),
            dma((1,)), dma((1,)),
            dma((peers,)), dma((shards,)),
            dma((parts,)), dma((parts,)),
            dma((max(more, 1),)), dma((max(more, 1),)),
            dma((peers,)), dma((shards,)),
            dma((bits,)), dma((bits,)),
        ],
        compiler_params=pltpu.CompilerParams(
            collective_id=0, has_side_effects=True, vmem_limit_bytes=62 << 20
        ),
        name="layer",
    )(inputs, small, w_qkv, w_out, w_up, w_down, cotangent)


def pack(positions, segment_ids, gain_one, b_query, b_value, query_scale, b_out, gain_two, b_up, b_down):
    block = positions.shape[-1]
    me = lax.axis_index("shard")
    starts = (me * block + lax.iota(jnp.int32, block) - positions.reshape(block)).astype(F32)
    keep = (segment_ids.reshape(block) != 0).astype(F32)
    table = {
        0: gain_one, 1: b_out, 2: gain_two, 3: b_up, 4: b_down, 5: query_scale, 6: starts,
        8: b_query, 9: b_value, 10: keep,
    }
    total = jnp.zeros((16, 256), F32)
    for row, vector in table.items():
        total = total + jnp.pad(vector.astype(F32)[None], ((row, 15 - row), (0, 256 - vector.shape[0])))
    return total


def on_device(
    inputs, segment_ids, positions, gain_one, w_qkv, b_query, b_value, query_scale, w_out, b_out,
    gain_two, w_up, b_up, w_down, b_down, cotangent,
):
    shards = lax.axis_size("shard")
    replicas = lax.axis_size("replica")
    block, width = inputs.shape[1:]
    slab = width // shards
    x = inputs.reshape(block, width)
    small = pack(positions, segment_ids, gain_one, b_query, b_value, query_scale, b_out, gain_two, b_up, b_down)
    output, fin, gw, input_grad, small = layer(
        shards, replicas, x, small, w_qkv, w_out, w_up, w_down, cotangent.reshape(block, width)
    )
    gw = gw.reshape(slab, 3 * width).astype(F32)
    fin = fin.astype(F32)
    unit = HEAD // shards
    return (
        output[None], input_grad[None], small[0, :slab], gw, small[6, :slab], small[7, :slab],
        small[5, 256 : 256 + unit], fin[0], small[1, :slab], small[2, :slab], fin[1], small[3, :slab],
        fin[2], small[4, :slab],
    )


def solution(mesh):
    rows = P("replica", "shard", None)
    ids = P("replica", "shard")
    vector = P("shard")
    matrix = P("shard", None)
    in_specs = (
        rows, ids, ids, vector, matrix, vector, vector, vector, matrix, vector, vector, matrix, vector,
        matrix, vector, rows,
    )
    out_specs = (
        rows, rows, vector, matrix, vector, vector, vector, matrix, vector, vector, matrix, vector, matrix,
        vector,
    )
    return jax.shard_map(on_device, mesh=mesh, in_specs=in_specs, out_specs=out_specs, check_vma=False)
```

time: 231 us -> 203 us (0.88)
  Pallas kernels: 212 us -> 185 us
    pallas_call x2 -> x1, Pallas kernels: 212 us -> 185 us  [layer(): pl.pallas_call(functools.partial(layer_kernel, shards, replicas, wparts,...]
where the time goes in v4:
time: 203 us; the launch traced here: 201 us
  Pallas kernels  185 us (91%)
  local copies, waits for them, and re-layouts  10.5 us (5%)
  other arithmetic  5.75 us (3%)
    pallas_call x1, Pallas kernels, layer(): pl.pallas_call(functools.partial(layer_kernel, shards, replicas, wparts,...  185 us
    broadcast_in_dim x7, local copies, waits for them, and re-layouts, pack(): vector.astype(F32)[None]  4.61 us

profile of v4, /device:TPU:0, one launch (start us, length us, event | category | flops | bytes accessed | tf_op | source)
XLA Modules:
  0.0 201.5 jit_solution(17535118815508448507)
XLA Ops:
  0.6 0.7 subtract_convert_fusion
  1.3 0.7 broadcast_in_dim.40
  2.0 0.7 broadcast_in_dim.41
  2.6 0.7 broadcast_in_dim.42
  3.3 0.7 broadcast_in_dim.43
  3.9 0.7 broadcast_in_dim.44
  4.6 0.7 broadcast_in_dim.46
  5.3 0.7 broadcast_in_dim.47
  5.9 0.7 broadcast_compare_fusion
  6.6 1.3 convert_add_fusion.small_ref
  7.9 184.6 %layer.1 = (bf16[128,1280]{1,0:T(8,128)(2,1)}, bf16[3,160,1280]{2,1,0:T(8,128)(2,1)}, bf16[4,40,3840]{2,1,0:T(8,128)(2,1)}, f32[128,1280]{1,0:T(8,128)}, f32[8,384]{1,0:T(8,128)}) custom-call(bf16[128,1280]{1,0:T(8,128)(2,1)} %bitcast.24, f32[16,256]{1,0:T(8,128)} %convert_add_fusion.small_ref, bf16[160,3840]{1,0:T(8,128)(2,1)} %w_ref.1, ...), custom_call_target="tpu_custom_call" | custom-call | tf_op jit(solution)/shard_map/layer/pallas_call | solution.py:890
  192.4 1.5 fusion
  194.0 1.5 convert_element_type.46
  195.5 0.0 copy-start
  195.5 1.5 slice_bitcast_fusion
  197.0 0.0 copy-start.2
  197.0 0.0 copy-start.1
  197.0 1.3 slice_bitcast_fusion.3
  198.2 0.0 copy-done
  198.2 1.7 bitcast_convert_fusion
  199.9 0.0 copy-done.2
  199.9 0.7 copy.32
  200.6 0.0 copy-done.1
  200.7 0.8 copy.33
Async XLA Ops:
  195.5 2.8 %copy-start = (bf16[4,40,3840]{2,1,0:T(8,128)(2,1)S(1)}, bf16[4,40,3840]{2,1,0:T(8,128)(2,1)}, u32[]{:S(2)}) copy-start(bf16[4,40,3840]{2,1,0:T(8,128)(2,1)} %get-tuple-element.22) | copy-start | bytes 3686404
  197.0 3.0 %copy-start.2 = (bf16[128,1280]{1,0:T(8,128)(2,1)S(1)}, bf16[128,1280]{1,0:T(8,128)(2,1)}, u32[]{:S(2)}) copy-start(bf16[128,1280]{1,0:T(8,128)(2,1)} %get-tuple-element.19) | copy-start | bytes 983044
  197.0 3.7 %copy-start.1 = (f32[128,1280]{1,0:T(8,128)S(1)}, f32[128,1280]{1,0:T(8,128)}, u32[]{:S(2)}) copy-start(f32[128,1280]{1,0:T(8,128)} %get-tuple-element.20) | copy-start | bytes 1966084

commit v5 on v4

--- a/solution.py
+++ b/solution.py
@@ -131,10 +131,9 @@
                 self.recv(origin), shard=at.at(0, db), when=when,
             )
 
-    def begin(self):
+    def along_own(self):
         at = self.at
         self.onward(at.me, at.a + 1 < MAJOR, at.a > 0, 0)
-        self.across(at.me)
 
     def sides(self, d):
         at = self.at
@@ -190,16 +189,18 @@
 
 def layer_kernel(
     shards, replicas, wparts, parts, qblock,
-    x_ref, small_ref, w_ref, wout_ref, wup_ref, wdown_ref, cot_ref,
-    out_ref, fin_ref, gw_ref, gin_ref, small_out_ref,
+    x_ref, segment_ref, position_ref, gain_one_ref, b_query_ref, b_value_ref, scale_ref,
+    b_out_ref, gain_two_ref, b_up_ref, b_down_ref, w_hbm, wout_ref, wup_ref, wdown_ref, cot_hbm,
+    out_hbm, fin_hbm, gw_hbm, gin_hbm, small_out_ref,
+    out_ref, fin_ref, gw_ref, gin_ref, w_ref, cot_ref, small_ref,
     normed_ref, qkv_ref, query_ref, log_ref, vec_ref, start_ref, wcols_ref,
     xt_ref, dy_ref, dctx_ref, row_ref, gmixed_ref,
     xg, packets, pieces, turned, context, att, weights,
     dctx, grads, proj, left, right, stash, sums, from_x, from_z, extra,
     gw, gw_core, gw_y, gw_sum, gw_land, gw_extra,
     windows, small_land, small_got,
-    xm_send, xn_send, x_recv, p_send, p_recv, w_send, w_recv, wc_send,
-    fm_send, fn_send, f_recv, fy_send, fc_send, local_sem, a_send, a_recv,
+    xm_send, xn_send, x_recv, p_send, p_recv, w_send, w_recv, wc_send, wy_send,
+    fm_send, fn_send, f_recv, fy_send, fc_send, local_sem, a_send, a_recv, done_sem,
     d_send, d_recv, gy_send, gy_recv, gc_send, gc_recv, gx_send, gx_recv, gz_send, gz_recv,
     r_send, r_recv, e_send, e_recv, nx_send, nx_recv, nz_send, nz_recv,
     vc_send, vc_recv, vy_send, vy_recv, va_send, va_recv, vr_send, vr_recv, ve_send, ve_recv,
@@ -230,7 +231,22 @@
         )
         copy.start()
         loads.append(copy)
+    w_load = pltpu.make_async_copy(w_hbm, w_ref, local_sem.at[3])
+    w_load.start()
+    cot_load = pltpu.make_async_copy(cot_hbm, cot_ref, local_sem.at[4])
+    cot_load.start()
     xg[me] = x_ref[...]
+    small_ref[...] = jnp.zeros_like(small_ref)
+    table = {
+        0: gain_one_ref, 1: b_out_ref, 2: gain_two_ref, 3: b_up_ref, 4: b_down_ref, 5: scale_ref,
+        8: b_query_ref, 9: b_value_ref,
+    }
+    for row, ref in table.items():
+        size = ref.shape[0]
+        small_ref[row : row + 1, :size] = ref[...].astype(F32).reshape(1, size)
+    place = me * block + lax.broadcasted_iota(jnp.int32, (1, block), 1)
+    small_ref[6:7, :block] = (place - position_ref[...]).astype(F32)
+    small_ref[10:11, :block] = (segment_ref[...] != 0).astype(F32)
     packets[me] = small_ref[:8]
     at.greet(tuple(every))
 
@@ -253,13 +269,14 @@
             sem = fy_send.at[origin] if mask == 2 else fc_send.at[origin, 0]
             at.send(slot, slot, sem, f_recv.at[origin, mine], rep=at.flip(mask), when=when)
 
-    rows_line.begin()
     for i, (da, db) in enumerate(peers):
         at.send(packets.at[me], packets.at[me], p_send.at[i], p_recv.at[me], shard=at.at(da, db))
+    rows_line.along_own()
     for copy in loads:
         copy.wait()
-    ffn_line.begin()
-
+    ffn_line.across(me)
+    rows_line.across(me)
+    w_load.wait()
     cut = slab // wparts
     for j in range(shards):
         for t in range(3):
@@ -267,15 +284,16 @@
             pieces[j, :, :, t * slab : (t + 1) * slab] = w_ref[:, first : first + slab].reshape(
                 wparts, cut, slab
             )
+    parity = lax.rem(at.a + mine // 2, 2)
+    chosen = parity == 0 if parts == 4 else None
     for i, (da, db) in enumerate(peers):
         dest = at.at(da, db)
         at.send(
-            pieces.at[dest, wpart], wcols_ref.at[me, wpart], w_send.at[i], w_recv.at[me, wpart], shard=dest
+            pieces.at[dest, wpart], wcols_ref.at[me, wpart], w_send.at[i], w_recv.at[me, wpart], shard=dest,
+            when=chosen,
         )
     wcols_ref[me] = pieces[me]
-
-    rows_line.step(1)
-    ffn_line.step(1, to_replicas)
+    ffn_line.along_own()
 
     def ffn_minor(distance):
         for db in range(1, minor):
@@ -295,14 +313,32 @@
                         at.arrived(slot, f_recv.at[origin, mine])
                 to_replicas(origin, ok)
 
+    def columns(phase):
+        for q in range(2):
+            for db in range(minor):
+                da = lax.rem(parity + phase, 2) + 2 * q
+                origin = at.at(-da, -db)
+                slot = wcols_ref.at[origin, wpart]
+                real = origin != me
+
+                @pl.when(real)
+                def _():
+                    at.arrived(slot, w_recv.at[origin, wpart])
+
+                if parts == 4 and phase == 0:
+                    at.send(
+                        slot, slot, wy_send.at[origin], w_recv.at[origin, wpart], rep=at.flip(2), when=real
+                    )
+                if wparts == 2:
+                    at.send(
+                        slot, slot, wc_send.at[origin], w_recv.at[origin, wpart], rep=at.flip(1), when=real
+                    )
+
     ffn_minor(0)
-
-    if wparts == 2:
-        for i, (da, db) in enumerate(peers):
-            origin = at.at(-da, -db)
-            slot = wcols_ref.at[origin, wpart]
-            at.arrived(slot, w_recv.at[origin, wpart])
-            at.send(slot, slot, wc_send.at[i], w_recv.at[origin, wpart], rep=at.flip(1))
+    rows_line.step(1)
+    ffn_line.step(1, to_replicas)
+    rows_line.step(2)
+    columns(0)
 
     for da, db in peers:
         origin = at.at(-da, -db)
@@ -332,13 +368,15 @@
     bias_query = tall[:slab, 0:1]
     bias_value = tall[:slab, 1:2]
 
-    rows_line.step(2)
     ffn_line.step(2, to_replicas)
     ffn_minor(1)
-    for da, db in peers:
-        origin = at.at(-da, -db)
-        last = wparts - 1 - wpart
-        at.arrived(wcols_ref.at[origin, last], w_recv.at[origin, last])
+    rows_line.step(3)
+    columns(1)
+    if wparts == 2:
+        for da, db in peers:
+            origin = at.at(-da, -db)
+            last = wparts - 1 - wpart
+            at.arrived(wcols_ref.at[origin, last], w_recv.at[origin, last])
     turned[...] = wcols_ref[...].reshape(width, slab3).T
 
     def project(origin):
@@ -354,7 +392,6 @@
         qkv_ref[slab : 2 * slab, tokens] = out[slab : 2 * slab].astype(BF16)
         qkv_ref[2 * slab :, tokens] = (out[2 * slab :] + bias_value).astype(BF16)
 
-    rows_line.step(3)
     ffn_line.step(3, to_replicas)
 
     def project_major(i, carry):
@@ -536,10 +573,11 @@
     }
 
     def land_x(db, t):
-        return weights.at[db - 1, pl.ds(pl.multiple_of(t * block, block), block), :]
+        first = (db - 1) // 2 * MAJOR + t
+        return weights.at[(db - 1) % 2, pl.ds(pl.multiple_of(first * block, block), block), :]
 
     def land_z(n):
-        return weights.at[0, pl.ds(pl.multiple_of((MAJOR + n) * block, block), block), :]
+        return weights.at[1, pl.ds(pl.multiple_of((MAJOR + n) * block, block), block), :]
 
     row_sums = Chain(lambda t: xg.at[t * minor + at.b], land_z, nz_send, nz_recv)
 
@@ -592,6 +630,7 @@
         return value.reshape(shards, halves, slab // halves, block)
 
     att_t = (att[...].astype(F32) * keep_row).astype(BF16)
+    cot_load.wait()
     dy_ref[2] = cot_ref[...]
     mixed = x_ref[...].astype(F32) + dot(att_t.T, weights[0]) + b_out
     r = lax.rsqrt(jnp.mean(mixed * mixed, axis=-1, keepdims=True) + EPS)
@@ -609,7 +648,6 @@
     weighted = gain_two * g_normed
     g_mixed = cot + r * weighted - mixed * (r * r * r) * jnp.mean(mixed * weighted, axis=-1, keepdims=True)
     g_low = g_mixed.astype(BF16)
-    out_ref[...] = (mixed + dot(act, weights[2]) + b_down).astype(BF16)
     dctx_ref[...] = (dot(weights[0], g_low, NT).astype(BF16).astype(F32) * keep_row).astype(BF16)
     backward, at.started = at.started, forward
     at.settle()
@@ -623,11 +661,16 @@
     dctx[:, lane(me, block)] = dctx_ref[pl.ds(pl.multiple_of(me * slab, 16), slab), :]
     dy_ref[1] = low
     xt_ref[1] = split_rows(normed_two.T)
+    meet_far(1)
     meet_near(1)
     gmixed_ref[...] = g_mixed
     dy_ref[0] = g_low
     xt_ref[0] = split_rows(att_t)
+    meet_far(0)
     meet_near(0)
+    out_ref[...] = (mixed + dot(act, weights[2]) + b_down).astype(BF16)
+    written = [pltpu.make_async_copy(out_ref, out_hbm, done_sem.at[0])]
+    written[0].start()
     row_ref[...] = jnp.zeros_like(row_ref)
     row_ref[1:2, :] = jnp.sum(g_mixed, axis=0, keepdims=True)
     row_ref[2:3, :] = jnp.sum(g_normed * mixed * r, axis=0, keepdims=True)
@@ -670,7 +713,6 @@
         attend(i)
         if i == 1:
             relay(2)
-            meet_far(1)
         if i == 2:
             weight(2)
             weight_across(2)
@@ -699,6 +741,18 @@
         weighted = out * normed_ref[tokens, :].astype(F32)
         return acc + jnp.sum(weighted.reshape(block // 8, 8, width), axis=0)
 
+    def away(i, acc):
+        return partial(turn(1 + lax.rem(i, 3)) * minor + lax.rem(at.b + 1 + i // 3, minor), acc)
+
+    gain_rows = jnp.zeros((8, width), F32)
+    for db in range(1, minor):
+        gain_rows = partial(turn(0) * minor + lax.rem(at.b + db, minor), gain_rows)
+    rows_across(0)
+    relay(1)
+    gain_rows = lax.fori_loop(0, 3 * (minor - 1), away, gain_rows)
+    weight(1)
+    weight_across(1)
+
     rp = width // (shards * parts)
     halves = parts // 2
     whole = dot(normed_ref[...], proj[...], TN)
@@ -706,34 +760,7 @@
     for k in range(halves):
         at.send(gw.at[:, (1 - core) + 2 * k], gw_core.at[k], vc_send.at[k], vc_recv.at[k], rep=at.flip(1))
 
-    def away(i, acc):
-        return partial(at.at(lax.rem(i, MAJOR), 1 + i // MAJOR), acc)
-
-    gain_rows = jnp.zeros((8, width), F32)
-    gain_rows = lax.fori_loop(0, shards - MAJOR, away, gain_rows)
-    rows_across(0)
-    rows_across(1)
-    relay(1)
-    meet_far(0)
     gain_rows = lax.fori_loop(0, MAJOR, lambda i, acc: partial(at.at(i, 0), acc), gain_rows)
-    weight(1)
-    weight_across(1)
-    rows_across(2)
-    weight_summed(2)
-    for k in range(halves):
-        at.arrived(gw_core.at[k], vc_recv.at[k])
-        gw_core[k] = gw[:, core + 2 * k] + gw_core[k]
-    km = mine // 2 if parts == 4 else 0
-    rows_summed(0)
-    weight_joined(2, 0)
-    weight_joined(2, 1)
-    weight_joined(2, 3)
-    relay(0)
-    if parts == 4:
-        at.send(gw_core.at[1 - km], gw_y, vy_send.at[0], vy_recv.at[0], rep=at.flip(2))
-    weight(0)
-    weight_across(0)
-    rows_across(3)
 
     gain_row = jnp.sum(gain_rows, axis=0, keepdims=True) / vec_ref[0:1, :]
     rows = row_ref[...]
@@ -753,6 +780,24 @@
         at.send(windows.at[dest], small_land.at[me], s_send.at[i], s_recv.at[me], shard=dest)
     small_land[me] = windows[me]
 
+    weight_summed(2)
+    relay(0)
+    weight(0)
+    weight_across(0)
+    rows_across(1)
+    rows_across(2)
+    for k in range(halves):
+        at.arrived(gw_core.at[k], vc_recv.at[k])
+        gw_core[k] = gw[:, core + 2 * k] + gw_core[k]
+    km = mine // 2 if parts == 4 else 0
+    if parts == 4:
+        at.send(gw_core.at[1 - km], gw_y, vy_send.at[0], vy_recv.at[0], rep=at.flip(2))
+    rows_summed(0)
+    weight_joined(2, 0)
+    weight_joined(2, 1)
+    weight_joined(2, 3)
+    weight_summed(1)
+    row_sums.joined(0)
     if parts == 4:
         at.arrived(gw_y, vy_recv.at[0])
         gw_sum[...] = gw_core[km] + gw_y[...]
@@ -762,21 +807,51 @@
         dest = at.at(da, db)
         at.send(gw_sum.at[dest], gw_land.at[me], va_send.at[i], va_recv.at[me], shard=dest)
     gw_land[me] = gw_sum[me]
-    rows_summed(1)
-    row_sums.joined(0)
-    weight_summed(1)
-    rows_summed(2)
-    row_sums.joined(1)
+    rows_across(3)
     weight_joined(1, 0)
     weight_joined(1, 1)
     weight_joined(1, 3)
     weight_summed(0)
-    rows_summed(3)
     weight_joined(0, 0)
     weight_joined(0, 1)
     weight_joined(0, 3)
-    row_sums.joined(3)
-
+    rows_summed(1)
+    row_sums.joined(1)
+
+    def hand_round(ref_slot, send_sem, recv_sem):
+        have, rounds, k = [mine], [], 0
+        for mask in ((2, 1) if parts == 4 else (1,)):
+            sends = []
+            for part in have:
+                sends.append((part, mask, k))
+                k += 1
+            fresh = [flipped(part, mask) for part in have]
+            rounds.append((sends, fresh))
+            have = have + fresh
+
+        def go(n):
+            for part, mask, k in rounds[n][0]:
+                at.send(ref_slot(part), ref_slot(part), send_sem.at[k], recv_sem.at[part], rep=at.flip(mask))
+
+        def take(n):
+            for part in rounds[n][1]:
+                at.arrived(ref_slot(part), recv_sem.at[part])
+
+        return go, take, len(rounds)
+
+    gw_go, gw_take, count = hand_round(lambda part: gw_ref.at[part], vr_send, vr_recv)
+    fin_go, fin_take, _ = hand_round(fin_slot, r_send, r_recv)
+    for m in mats:
+        weight_done(m)
+    for n, mask in enumerate(extras):
+        at.exchange(fin_slot(mine), extra.at[n], e_send.at[n], e_recv.at[n], at.flip(mask))
+        fin_slot(mine)[...] = fin_slot(mine)[...] + extra[n]
+    def write(src, dst, n):
+        copy = pltpu.make_async_copy(src, dst, done_sem.at[n])
+        copy.start()
+        written.append(copy)
+
+    fin_go(0)
     for da, db in peers:
         origin = at.at(-da, -db)
         at.arrived(small_land.at[origin], s_recv.at[origin])
@@ -803,6 +878,7 @@
         small_got[2 * n + 2] = small_got[2 * n] + small_got[2 * n + 1]
 
     small_round(0)
+    rows_summed(2)
     for da, db in peers:
         origin = at.at(-da, -db)
         at.arrived(gw_land.at[origin], va_recv.at[origin])
@@ -814,62 +890,40 @@
             first = t * width + j * slab
             gw_ref[mine, :, first : first + slab] = gw_land[j, :, t * slab : (t + 1) * slab]
 
-    def hand_round(ref_slot, send_sem, recv_sem):
-        have, rounds, k = [mine], [], 0
-        for mask in ((2, 1) if parts == 4 else (1,)):
-            sends = []
-            for part in have:
-                sends.append((part, mask, k))
-                k += 1
-            fresh = [flipped(part, mask) for part in have]
-            rounds.append((sends, fresh))
-            have = have + fresh
-
-        def go(n):
-            for part, mask, k in rounds[n][0]:
-                at.send(ref_slot(part), ref_slot(part), send_sem.at[k], recv_sem.at[part], rep=at.flip(mask))
-
-        def take(n):
-            for part in rounds[n][1]:
-                at.arrived(ref_slot(part), recv_sem.at[part])
-
-        return go, take, len(rounds)
-
-    gw_go, gw_take, count = hand_round(lambda part: gw_ref.at[part], vr_send, vr_recv)
-    fin_go, fin_take, _ = hand_round(fin_slot, r_send, r_recv)
     gw_go(0)
     small_add(0)
     small_round(1)
-
-    for m in mats:
-        weight_done(m)
-    for n, mask in enumerate(extras):
-        at.exchange(fin_slot(mine), extra.at[n], e_send.at[n], e_recv.at[n], at.flip(mask))
-        fin_slot(mine)[...] = fin_slot(mine)[...] + extra[n]
-    fin_go(0)
+    rows_summed(3)
+    row_sums.joined(3)
+    for n in range(count - 1):
+        fin_take(n)
+        fin_go(n + 1)
+        gw_take(n)
+        gw_go(n + 1)
+    for n in range(1, len(every)):
+        small_add(n)
+        if n + 1 < len(every):
+            small_round(n + 1)
+    small_out_ref[...] = small_got[2 * len(every)]
+
     total = row_sums.result().astype(F32)
     x = x_ref[...].astype(F32)
     r = lax.rsqrt(jnp.mean(x * x, axis=-1, keepdims=True) + EPS)
     weighted = vec_ref[0:1, :] * total
     gin_ref[...] = gmixed_ref[...] + r * weighted - x * (r * r * r) * jnp.mean(x * weighted, axis=-1, keepdims=True)
 
-    for n in range(count):
-        gw_take(n)
-        if n + 1 < count:
-            gw_go(n + 1)
-        fin_take(n)
-        if n + 1 < count:
-            fin_go(n + 1)
-    for n in range(1, len(every)):
-        small_add(n)
-        if n + 1 < len(every):
-            small_round(n + 1)
-    small_out_ref[...] = small_got[2 * len(every)]
-
+
+    write(gin_ref, gin_hbm, 3)
+    fin_take(count - 1)
+    write(fin_ref, fin_hbm, 1)
+    gw_take(count - 1)
+    write(gw_ref, gw_hbm, 2)
     at.settle()
-
-
-def layer(shards, replicas, inputs, small, w_qkv, w_out, w_up, w_down, cotangent):
+    for copy in written:
+        copy.wait()
+
+
+def layer(shards, replicas, inputs, segment_ids, positions, vectors, w_qkv, w_out, w_up, w_down, cotangent):
     block, width = inputs.shape
     slab = width // shards
     slab3 = 3 * slab
@@ -896,9 +950,16 @@
             shape((block, width), F32),
             shape((8, 384), F32),
         ),
-        in_specs=[VMEM] * 3 + [ANY] * 3 + [VMEM],
-        out_specs=[VMEM] * 5,
+        in_specs=[VMEM] * 11 + [ANY] * 5,
+        out_specs=[ANY] * 4 + [VMEM],
         scratch_shapes=[
+            vm((block, width), BF16),
+            vm((3, slab, width), BF16),
+            vm((parts, rp, 3 * width), BF16),
+            vm((block, width), F32),
+            vm(w_qkv.shape, BF16),
+            vm((block, width), BF16),
+            vm((16, 256), F32),
             vm((length, width), BF16),
             vm((slab3, length), BF16),
             vm((slab, length), F32),
@@ -939,10 +1000,10 @@
             vm((2 * bits + 1, 8, 384), F32),
             dma((2, MAJOR)), dma((MAJOR, minor - 1)), dma((shards,)),
             dma((peers,)), dma((shards,)),
-            dma((peers,)), dma((shards, wparts)), dma((peers,)),
+            dma((peers,)), dma((shards, wparts)), dma((shards,)), dma((shards,)),
             dma((2, MAJOR)), dma((MAJOR, minor - 1)), dma((shards, parts)),
             dma((shards,)), dma((shards, 2)),
-            dma((3,)), dma((shards,)), dma((shards,)),
+            dma((5,)), dma((shards,)), dma((shards,)), dma((4,)),
             dma((peers,)), dma((shards,)),
             dma((3, 3)), dma((3, 3)),
             dma((3, 4)), dma((3, 4)),
@@ -964,22 +1025,64 @@
             collective_id=0, has_side_effects=True, vmem_limit_bytes=62 << 20
         ),
         name="layer",
-    )(inputs, small, w_qkv, w_out, w_up, w_down, cotangent)
-
-
-def pack(positions, segment_ids, gain_one, b_query, b_value, query_scale, b_out, gain_two, b_up, b_down):
-    block = positions.shape[-1]
-    me = lax.axis_index("shard")
-    starts = (me * block + lax.iota(jnp.int32, block) - positions.reshape(block)).astype(F32)
-    keep = (segment_ids.reshape(block) != 0).astype(F32)
-    table = {
-        0: gain_one, 1: b_out, 2: gain_two, 3: b_up, 4: b_down, 5: query_scale, 6: starts,
-        8: b_query, 9: b_value, 10: keep,
-    }
-    total = jnp.zeros((16, 256), F32)
-    for row, vector in table.items():
-        total = total + jnp.pad(vector.astype(F32)[None], ((row, 15 - row), (0, 256 - vector.shape[0])))
-    return total
+    )(inputs, segment_ids, positions, *vectors, w_qkv, w_out, w_up, w_down, cotangent)
+
+
+def finish_kernel(
+    slab, unit, fin_ref, gw_ref, small_ref, gin_ref, out_ref,
+    w_out_ref, w_up_ref, w_down_ref, w_qkv_ref, input_ref, output_ref,
+    gain_one_ref, b_query_ref, b_value_ref, scale_ref, b_out_ref, gain_two_ref, b_up_ref, b_down_ref,
+):
+    w_out_ref[...] = fin_ref[0].astype(F32)
+    w_up_ref[...] = fin_ref[1].astype(F32)
+    w_down_ref[...] = fin_ref[2].astype(F32)
+    w_qkv_ref[...] = gw_ref[...].astype(F32)
+    input_ref[...] = gin_ref[...]
+    output_ref[...] = out_ref[...]
+
+    @pl.when(pl.program_id(0) == 0)
+    def _():
+        table = {
+            0: gain_one_ref, 1: b_out_ref, 2: gain_two_ref, 3: b_up_ref, 4: b_down_ref,
+            6: b_query_ref, 7: b_value_ref,
+        }
+        for row, ref in table.items():
+            ref[...] = small_ref[row : row + 1, :slab].reshape(slab)
+        scale_ref[...] = small_ref[5:6, 256 : 256 + unit].reshape(unit)
+
+
+def finish(fin, gw, small, gin, out):
+    slab, width = fin.shape[1:]
+    block = gin.shape[0]
+    steps = 4 if slab % 32 == 0 else 2
+    unit = HEAD * slab // width
+    part, tokens = slab // steps, block // steps
+    shape = jax.ShapeDtypeStruct
+
+    def rows(size, columns):
+        return pl.BlockSpec((size, columns), lambda i: (i, 0))
+
+    whole = pl.BlockSpec((8, 384), lambda i: (0, 0))
+    vector = pl.BlockSpec((slab,), lambda i: (0,))
+    return pl.pallas_call(
+        functools.partial(finish_kernel, slab, unit),
+        grid=(steps,),
+        out_shape=[shape((slab, width), F32)] * 3
+        + [shape((slab, 3 * width), F32), shape((block, width), F32), shape((block, width), BF16)]
+        + [shape((slab,), F32)] * 3
+        + [shape((unit,), F32)]
+        + [shape((slab,), F32)] * 4,
+        in_specs=[
+            pl.BlockSpec((3, part, width), lambda i: (0, i, 0)), rows(part, 3 * width), whole,
+            rows(tokens, width), rows(tokens, width),
+        ],
+        out_specs=[rows(part, width)] * 3
+        + [rows(part, 3 * width), rows(tokens, width), rows(tokens, width)]
+        + [vector] * 3
+        + [pl.BlockSpec((unit,), lambda i: (0,))]
+        + [vector] * 4,
+        name="finish",
+    )(fin, gw, small, gin, out)
 
 
 def on_device(
@@ -990,18 +1093,18 @@
     replicas = lax.axis_size("replica")
     block, width = inputs.shape[1:]
     slab = width // shards
-    x = inputs.reshape(block, width)
-    small = pack(positions, segment_ids, gain_one, b_query, b_value, query_scale, b_out, gain_two, b_up, b_down)
     output, fin, gw, input_grad, small = layer(
-        shards, replicas, x, small, w_qkv, w_out, w_up, w_down, cotangent.reshape(block, width)
+        shards, replicas, inputs.reshape(block, width), segment_ids, positions,
+        (gain_one, b_query, b_value, query_scale, b_out, gain_two, b_up, b_down),
+        w_qkv, w_out, w_up, w_down, cotangent.reshape(block, width),
     )
-    gw = gw.reshape(slab, 3 * width).astype(F32)
-    fin = fin.astype(F32)
-    unit = HEAD // shards
+    (
+        g_out, g_up, g_down, g_qkv, input_grad, output, g_gain_one, g_b_query, g_b_value, g_scale, g_b_out,
+        g_gain_two, g_b_up, g_b_down,
+    ) = finish(fin, gw.reshape(slab, 3 * width), small, input_grad, output)
     return (
-        output[None], input_grad[None], small[0, :slab], gw, small[6, :slab], small[7, :slab],
-        small[5, 256 : 256 + unit], fin[0], small[1, :slab], small[2, :slab], fin[1], small[3, :slab],
-        fin[2], small[4, :slab],
+        output[None], input_grad[None], g_gain_one, g_qkv, g_b_query, g_b_value, g_scale, g_out, g_b_out,
+        g_gain_two, g_up, g_b_up, g_down, g_b_down,
     )
 
 

time: 203 us -> 181 us (0.89)
  local copies, waits for them, and re-layouts: 10.5 us -> 0 us
  other arithmetic: 5.75 us -> 0 us
  Pallas kernels: 185 us -> 180 us
    pallas_call x1, Pallas kernels: 185 us -> 175 us  [layer(): pl.pallas_call(functools.partial(layer_kernel, shards, replicas, wparts,...]
    pallas_call x0 -> x1, Pallas kernels: none -> 4.99 us  [finish(): pl.pallas_call(functools.partial(finish_kernel, slab, unit), grid=(steps,...]
    broadcast_in_dim x7 -> x0, local copies, waits for them, and re-layouts: 4.61 us -> none  [pack(): vector.astype(F32)[None]]
    convert_element_type x3 -> x0, other arithmetic: 3.81 us -> none  [the longest x1 1.68 us: on_device(): gw = gw.reshape(slab, 3 * width).astype(F32)]
    squeeze x2 -> x0, local copies, waits for them, and re-layouts: 2.76 us -> none  [the longest x1 1.48 us: on_device(): fin[2]]
where the time goes in v5:
time: 181 us
  Pallas kernels  180 us (99%)
    pallas_call x1, Pallas kernels, layer(): pl.pallas_call(functools.partial(layer_kernel, shards, replicas, wparts,...  175 us
    pallas_call x1, Pallas kernels, finish(): pl.pallas_call(functools.partial(finish_kernel, slab, unit), grid=(steps,...  4.99 us

profile of v5, /device:TPU:0, one launch (start us, length us, event | category | flops | bytes accessed | tf_op | source)
XLA Modules:
  0.0 181.2 jit_solution(7322110590681202786)
XLA Ops:
  0.7 175.4 %layer.1 = (bf16[128,1280]{1,0:T(8,128)(2,1)}, bf16[3,160,1280]{2,1,0:T(8,128)(2,1)}, bf16[4,40,3840]{2,1,0:T(8,128)(2,1)}, f32[128,1280]{1,0:T(8,128)}, f32[8,384]{1,0:T(8,128)}) custom-call(bf16[128,1280]{1,0:T(8,128)(2,1)} %bitcast.6, s32[1,128]{1,0:T(1,128)} %segment_ref.1, s32[1,128]{1,0:T(1,128)} %position_ref.1, bf16[160]{0:T(256)(128)(2,1)} %gain_one_ref.1, ...), custom_call_target="tpu_custom_call" | custom-call | tf_op jit(solution)/shard_map/layer/pallas_call | solution.py:944
  176.0 5.0 %finish.1 = (f32[160,1280]{1,0:T(8,128)}, f32[160,1280]{1,0:T(8,128)}, f32[160,1280]{1,0:T(8,128)}, f32[160,3840]{1,0:T(8,128)}, f32[128,1280]{1,0:T(8,128)}, /*...) custom-call(bf16[3,160,1280]{2,1,0:T(8,128)(2,1)} %get-tuple-element, ...), custom_call_target="tpu_custom_call" | custom-call | tf_op jit(solution)/shard_map/finish/pallas_call | solution.py:1067

commit v6 on v5

--- a/solution.py
+++ b/solution.py
@@ -269,6 +269,57 @@
             sem = fy_send.at[origin] if mask == 2 else fc_send.at[origin, 0]
             at.send(slot, slot, sem, f_recv.at[origin, mine], rep=at.flip(mask), when=when)
 
+    cols = width // 2
+    core = lax.rem(at.rep, 2)
+    i_part = lax.rem(mine, 2) if parts == 4 else 0
+    j_part = mine // 2 if parts == 4 else mine
+    mats = (2, 1, 0)
+
+    def lane(n, size):
+        return pl.ds(pl.multiple_of(n * size, 128), size)
+
+    def seat(n):
+        return slice(n * block, (n + 1) * block)
+
+    near = parts // 2
+
+    def meet_columns(m):
+        if parts == 4:
+            at.send(
+                dy_ref.at[m, :, lane(1 - j_part, cols)], right.at[m, seat(1), :],
+                gy_send.at[m, 1], gy_recv.at[m, 1], rep=at.flip(2),
+            )
+        at.send(
+            dy_ref.at[m, :, lane(j_part if parts == 4 else 1 - j_part, cols)], right.at[m, seat(near), :],
+            gc_send.at[m, 1], gc_recv.at[m, 1], rep=at.flip(1),
+        )
+        right[m, seat(0), :] = dy_ref[m, :, lane(j_part, cols)]
+
+    def meet_rows(m):
+        if parts == 4:
+            far = at.flip(2)
+            at.send(xt_ref.at[m, :, 1 - i_part], stash.at[m], gy_send.at[m, 2], gy_recv.at[m, 2], rep=far)
+            at.send(
+                xt_ref.at[m, :, i_part], left.at[m, :, :, seat(1)], gy_send.at[m, 0], gy_recv.at[m, 0], rep=far
+            )
+        at.send(
+            xt_ref.at[m, :, 1 - i_part if parts == 4 else 0], left.at[m, :, :, seat(near)],
+            gc_send.at[m, 0], gc_recv.at[m, 0], rep=at.flip(1),
+        )
+        left[m, :, :, seat(0)] = xt_ref[m, :, i_part]
+
+    def relay_columns(m):
+        if parts == 4:
+            at.arrived(right.at[m, seat(1), :], gy_recv.at[m, 1])
+            at.send(
+                right.at[m, seat(1), :], right.at[m, seat(3), :], gc_send.at[m, 3], gc_recv.at[m, 3], rep=at.flip(1)
+            )
+
+    def relay_rows(m):
+        if parts == 4:
+            at.arrived(stash.at[m], gy_recv.at[m, 2])
+            at.send(stash.at[m], left.at[m, :, :, seat(3)], gc_send.at[m, 2], gc_recv.at[m, 2], rep=at.flip(1))
+
     for i, (da, db) in enumerate(peers):
         at.send(packets.at[me], packets.at[me], p_send.at[i], p_recv.at[me], shard=at.at(da, db))
     rows_line.along_own()
@@ -276,6 +327,9 @@
         copy.wait()
     ffn_line.across(me)
     rows_line.across(me)
+    cot_load.wait()
+    dy_ref[2] = cot_ref[...]
+    meet_columns(2)
     w_load.wait()
     cut = slab // wparts
     for j in range(shards):
@@ -372,6 +426,7 @@
     ffn_minor(1)
     rows_line.step(3)
     columns(1)
+    relay_columns(2)
     if wparts == 2:
         for da, db in peers:
             origin = at.at(-da, -db)
@@ -456,61 +511,13 @@
         for part in others:
             at.arrived(wslot(origin, part), f_recv.at[origin, part])
 
-    slab3 = 3 * slab
-    cols = width // 2
-    core = lax.rem(at.rep, 2)
-    i_part = lax.rem(mine, 2) if parts == 4 else 0
-    j_part = mine // 2 if parts == 4 else mine
-    mats = (2, 1, 0)
-
-    def lane(n, size):
-        return pl.ds(pl.multiple_of(n * size, 128), size)
-
-    def slot(n):
-        return slice(n * block, (n + 1) * block)
-
-    def meet_near(m):
-        near = parts // 2
-        at.send(
-            xt_ref.at[m, :, 1 - i_part if parts == 4 else 0], left.at[m, :, :, slot(near)],
-            gc_send.at[m, 0], gc_recv.at[m, 0], rep=at.flip(1),
-        )
-        at.send(
-            dy_ref.at[m, :, lane(j_part if parts == 4 else 1 - j_part, cols)], right.at[m, slot(near), :],
-            gc_send.at[m, 1], gc_recv.at[m, 1], rep=at.flip(1),
-        )
-        left[m, :, :, slot(0)] = xt_ref[m, :, i_part]
-        right[m, slot(0), :] = dy_ref[m, :, lane(j_part, cols)]
-
-    def meet_far(m):
+    def weight(m):
+        at.arrived(left.at[m, :, :, seat(near)], gc_recv.at[m, 0])
+        at.arrived(right.at[m, seat(near), :], gc_recv.at[m, 1])
         if parts == 4:
-            far = at.flip(2)
-            at.send(
-                xt_ref.at[m, :, i_part], left.at[m, :, :, slot(1)], gy_send.at[m, 0], gy_recv.at[m, 0], rep=far
-            )
-            at.send(
-                dy_ref.at[m, :, lane(1 - j_part, cols)], right.at[m, slot(1), :],
-                gy_send.at[m, 1], gy_recv.at[m, 1], rep=far,
-            )
-            at.send(xt_ref.at[m, :, 1 - i_part], stash.at[m], gy_send.at[m, 2], gy_recv.at[m, 2], rep=far)
-
-    def relay(m):
-        if parts == 4:
-            at.arrived(left.at[m, :, :, slot(1)], gy_recv.at[m, 0])
-            at.arrived(right.at[m, slot(1), :], gy_recv.at[m, 1])
-            at.arrived(stash.at[m], gy_recv.at[m, 2])
-            at.send(stash.at[m], left.at[m, :, :, slot(3)], gc_send.at[m, 2], gc_recv.at[m, 2], rep=at.flip(1))
-            at.send(
-                right.at[m, slot(1), :], right.at[m, slot(3), :], gc_send.at[m, 3], gc_recv.at[m, 3], rep=at.flip(1)
-            )
-
-    def weight(m):
-        near = 2 if parts == 4 else 1
-        at.arrived(left.at[m, :, :, slot(near)], gc_recv.at[m, 0])
-        at.arrived(right.at[m, slot(near), :], gc_recv.at[m, 1])
-        if parts == 4:
-            at.arrived(left.at[m, :, :, slot(3)], gc_recv.at[m, 2])
-            at.arrived(right.at[m, slot(3), :], gc_recv.at[m, 3])
+            at.arrived(left.at[m, :, :, seat(1)], gy_recv.at[m, 0])
+            at.arrived(left.at[m, :, :, seat(3)], gc_recv.at[m, 2])
+            at.arrived(right.at[m, seat(3), :], gc_recv.at[m, 3])
         rows = left.shape[1] * left.shape[2]
         out = dot(left[m].reshape(rows, parts * block), right[m])
         sums[m] = out.reshape(sums.shape[1:]).astype(BF16)
@@ -613,6 +620,60 @@
     def weight_joined(m, n):
         ffn_sums[m].joined(n)
 
+    def rows_last_across():
+        t = turn(3)
+        for n in range(2):
+            half = pl.ds(n * cols, cols)
+            for db in range(1, minor):
+                to = t * minor + lax.rem(at.b + db, minor)
+                at.send(
+                    xg.at[to, :, half], land_x(db, t).at[:, half], nx_send.at[db - 1, 3 + n],
+                    nx_recv.at[db - 1, MAJOR if n else t], shard=at.at(0, db),
+                )
+
+    def rows_last():
+        t = turn(3)
+        own = row_sums.own(t)
+        to = lax.max(lax.min(at.a - ahead, MAJOR - 1), 0) * minor + at.b
+        for n in range(2):
+            half = pl.ds(n * cols, cols)
+            total = own[:, half].astype(F32)
+            for db in range(1, minor):
+                piece = land_x(db, t).at[:, half]
+                at.arrived(piece, nx_recv.at[db - 1, MAJOR if n else t])
+                total = total + piece[...].astype(F32)
+            own[:, half] = total.astype(BF16)
+
+            @pl.when(middle)
+            def _():
+                if n == 0:
+                    at.arrived(land_z(t), nz_recv.at[t])
+                own[:, half] = own[:, half] + land_z(t)[:, half]
+
+            at.send(
+                own.at[:, half], land_z(t).at[:, half], nz_send.at[3 + n],
+                nz_recv.at[MAJOR + 1 if n else t], shard=to, when=middle,
+            )
+
+    def rows_result():
+        own = row_sums.own(at.a)
+        mine_z = land_z(at.a)
+
+        @pl.when(middle)
+        def _():
+            at.arrived(mine_z, nz_recv.at[at.a])
+            at.arrived(land_z(MAJOR), nz_recv.at[MAJOR])
+            first = own[...].astype(F32) + mine_z[...].astype(F32)
+            gin_ref[...] = first + land_z(MAJOR)[...].astype(F32)
+
+        @pl.when(jnp.logical_not(middle))
+        def _():
+            at.arrived(mine_z.at[:, :cols], nz_recv.at[at.a])
+            at.arrived(mine_z.at[:, cols:], nz_recv.at[MAJOR + 1])
+            gin_ref[...] = own[...].astype(F32) + mine_z[...].astype(F32)
+
+        return gin_ref[...]
+
     def fin_slot(part, m=None):
         row, rows, col, wide = part_box(part, parts, slab, width)
         box = (pl.ds(pl.multiple_of(row, 16), rows), pl.ds(pl.multiple_of(col, 128), wide))
@@ -630,8 +691,6 @@
         return value.reshape(shards, halves, slab // halves, block)
 
     att_t = (att[...].astype(F32) * keep_row).astype(BF16)
-    cot_load.wait()
-    dy_ref[2] = cot_ref[...]
     mixed = x_ref[...].astype(F32) + dot(att_t.T, weights[0]) + b_out
     r = lax.rsqrt(jnp.mean(mixed * mixed, axis=-1, keepdims=True) + EPS)
     normed_two = (mixed * r * gain_two).astype(BF16)
@@ -639,8 +698,7 @@
     s = 1.0 / (1.0 + jnp.exp(-hidden))
     act = (hidden * s).astype(BF16)
     xt_ref[2] = split_rows(act.T)
-    meet_far(2)
-    meet_near(2)
+    meet_rows(2)
     cot = cot_ref[...].astype(F32)
     g_hidden = dot(cot_ref[...], weights[2], NT) * (s + hidden * s * (1.0 - s))
     low = g_hidden.astype(BF16)
@@ -661,13 +719,13 @@
     dctx[:, lane(me, block)] = dctx_ref[pl.ds(pl.multiple_of(me * slab, 16), slab), :]
     dy_ref[1] = low
     xt_ref[1] = split_rows(normed_two.T)
-    meet_far(1)
-    meet_near(1)
+    meet_columns(1)
+    meet_rows(1)
     gmixed_ref[...] = g_mixed
     dy_ref[0] = g_low
     xt_ref[0] = split_rows(att_t)
-    meet_far(0)
-    meet_near(0)
+    meet_columns(0)
+    meet_rows(0)
     out_ref[...] = (mixed + dot(act, weights[2]) + b_down).astype(BF16)
     written = [pltpu.make_async_copy(out_ref, out_hbm, done_sem.at[0])]
     written[0].start()
@@ -676,6 +734,40 @@
     row_ref[2:3, :] = jnp.sum(g_normed * mixed * r, axis=0, keepdims=True)
     row_ref[3:4, :] = jnp.sum(g_hidden, axis=0, keepdims=True)
     row_ref[4:5, :] = jnp.sum(cot, axis=0, keepdims=True)
+
+    def hand_round(ref_slot, send_sem, recv_sem):
+        have, rounds, k = [mine], [], 0
+        for mask in ((2, 1) if parts == 4 else (1,)):
+            sends = []
+            for part in have:
+                sends.append((part, mask, k))
+                k += 1
+            fresh = [flipped(part, mask) for part in have]
+            rounds.append((sends, fresh))
+            have = have + fresh
+
+        def go(n):
+            for part, mask, k in rounds[n][0]:
+                at.send(ref_slot(part), ref_slot(part), send_sem.at[k], recv_sem.at[part], rep=at.flip(mask))
+
+        def take(n):
+            for part in rounds[n][1]:
+                at.arrived(ref_slot(part), recv_sem.at[part])
+
+        return go, take, len(rounds)
+
+    gw_go, gw_take, count = hand_round(lambda part: gw_ref.at[part], vr_send, vr_recv)
+    fin_hands = [
+        hand_round(lambda part, m=m: fin_slot(part, m), r_send.at[m], r_recv.at[m]) for m in range(3)
+    ]
+
+    def weight_last(m):
+        weight_done(m)
+        for n, mask in enumerate(extras):
+            here = fin_slot(mine, m)
+            at.exchange(here, extra.at[n, m], e_send.at[n, m], e_recv.at[n, m], at.flip(mask))
+            here[...] = here[...] + extra[n, m]
+        fin_hands[m][0](0)
 
     base = QUERY_BASE / math.sqrt(HEAD)
     factor = base * soft
@@ -708,14 +800,12 @@
             kv = slice(2 * slab + h * HEAD, 2 * slab + (h + 1) * HEAD)
             grads[kv, :reach] += dot(gctx, low, NT)
 
-    steps = length // qblock
-    for i in range(steps):
+    relay_rows(2)
+    attend(0)
+    weight(2)
+    weight_across(2)
+    for i in range(1, length // qblock):
         attend(i)
-        if i == 1:
-            relay(2)
-        if i == 2:
-            weight(2)
-            weight_across(2)
 
     gscale = jnp.zeros((HEAD, 1), F32)
     for h in range(local):
@@ -748,7 +838,8 @@
     for db in range(1, minor):
         gain_rows = partial(turn(0) * minor + lax.rem(at.b + db, minor), gain_rows)
     rows_across(0)
-    relay(1)
+    relay_columns(1)
+    relay_rows(1)
     gain_rows = lax.fori_loop(0, 3 * (minor - 1), away, gain_rows)
     weight(1)
     weight_across(1)
@@ -781,11 +872,10 @@
     small_land[me] = windows[me]
 
     weight_summed(2)
-    relay(0)
+    relay_columns(0)
+    relay_rows(0)
     weight(0)
     weight_across(0)
-    rows_across(1)
-    rows_across(2)
     for k in range(halves):
         at.arrived(gw_core.at[k], vc_recv.at[k])
         gw_core[k] = gw[:, core + 2 * k] + gw_core[k]
@@ -796,8 +886,6 @@
     weight_joined(2, 0)
     weight_joined(2, 1)
     weight_joined(2, 3)
-    weight_summed(1)
-    row_sums.joined(0)
     if parts == 4:
         at.arrived(gw_y, vy_recv.at[0])
         gw_sum[...] = gw_core[km] + gw_y[...]
@@ -807,7 +895,11 @@
         dest = at.at(da, db)
         at.send(gw_sum.at[dest], gw_land.at[me], va_send.at[i], va_recv.at[me], shard=dest)
     gw_land[me] = gw_sum[me]
-    rows_across(3)
+    rows_across(1)
+    rows_across(2)
+    rows_last_across()
+    weight_summed(1)
+    row_sums.joined(0)
     weight_joined(1, 0)
     weight_joined(1, 1)
     weight_joined(1, 3)
@@ -815,43 +907,33 @@
     weight_joined(0, 0)
     weight_joined(0, 1)
     weight_joined(0, 3)
+    for da, db in peers:
+        origin = at.at(-da, -db)
+        at.arrived(gw_land.at[origin], va_recv.at[origin])
+    for n, mask in enumerate(extras):
+        at.exchange(gw_land, gw_extra.at[n], ve_send.at[n], ve_recv.at[n], at.flip(mask))
+        gw_land[...] = gw_land[...] + gw_extra[n]
+    for j in range(shards):
+        for t in range(3):
+            first = t * width + j * slab
+            gw_ref[mine, :, first : first + slab] = gw_land[j, :, t * slab : (t + 1) * slab]
+
+    gw_go(0)
     rows_summed(1)
+    weight_last(2)
+    weight_last(1)
+    weight_last(0)
     row_sums.joined(1)
-
-    def hand_round(ref_slot, send_sem, recv_sem):
-        have, rounds, k = [mine], [], 0
-        for mask in ((2, 1) if parts == 4 else (1,)):
-            sends = []
-            for part in have:
-                sends.append((part, mask, k))
-                k += 1
-            fresh = [flipped(part, mask) for part in have]
-            rounds.append((sends, fresh))
-            have = have + fresh
-
-        def go(n):
-            for part, mask, k in rounds[n][0]:
-                at.send(ref_slot(part), ref_slot(part), send_sem.at[k], recv_sem.at[part], rep=at.flip(mask))
-
-        def take(n):
-            for part in rounds[n][1]:
-                at.arrived(ref_slot(part), recv_sem.at[part])
-
-        return go, take, len(rounds)
-
-    gw_go, gw_take, count = hand_round(lambda part: gw_ref.at[part], vr_send, vr_recv)
-    fin_go, fin_take, _ = hand_round(fin_slot, r_send, r_recv)
-    for m in mats:
-        weight_done(m)
-    for n, mask in enumerate(extras):
-        at.exchange(fin_slot(mine), extra.at[n], e_send.at[n], e_recv.at[n], at.flip(mask))
-        fin_slot(mine)[...] = fin_slot(mine)[...] + extra[n]
+    for n in range(count - 1):
+        gw_take(n)
+        gw_go(n + 1)
+
+
     def write(src, dst, n):
         copy = pltpu.make_async_copy(src, dst, done_sem.at[n])
         copy.start()
         written.append(copy)
 
-    fin_go(0)
     for da, db in peers:
         origin = at.at(-da, -db)
         at.arrived(small_land.at[origin], s_recv.at[origin])
@@ -879,34 +961,22 @@
 
     small_round(0)
     rows_summed(2)
-    for da, db in peers:
-        origin = at.at(-da, -db)
-        at.arrived(gw_land.at[origin], va_recv.at[origin])
-    for n, mask in enumerate(extras):
-        at.exchange(gw_land, gw_extra.at[n], ve_send.at[n], ve_recv.at[n], at.flip(mask))
-        gw_land[...] = gw_land[...] + gw_extra[n]
-    for j in range(shards):
-        for t in range(3):
-            first = t * width + j * slab
-            gw_ref[mine, :, first : first + slab] = gw_land[j, :, t * slab : (t + 1) * slab]
-
-    gw_go(0)
     small_add(0)
     small_round(1)
-    rows_summed(3)
-    row_sums.joined(3)
+    rows_last()
+    gw_take(count - 1)
+    write(gw_ref, gw_hbm, 2)
     for n in range(count - 1):
-        fin_take(n)
-        fin_go(n + 1)
-        gw_take(n)
-        gw_go(n + 1)
+        for m in mats:
+            fin_hands[m][1](n)
+            fin_hands[m][0](n + 1)
     for n in range(1, len(every)):
         small_add(n)
         if n + 1 < len(every):
             small_round(n + 1)
     small_out_ref[...] = small_got[2 * len(every)]
 
-    total = row_sums.result().astype(F32)
+    total = rows_result()
     x = x_ref[...].astype(F32)
     r = lax.rsqrt(jnp.mean(x * x, axis=-1, keepdims=True) + EPS)
     weighted = vec_ref[0:1, :] * total
@@ -914,10 +984,9 @@
 
 
     write(gin_ref, gin_hbm, 3)
-    fin_take(count - 1)
-    write(fin_ref, fin_hbm, 1)
-    gw_take(count - 1)
-    write(gw_ref, gw_hbm, 2)
+    for m in mats:
+        fin_hands[m][1](count - 1)
+        write(fin_ref.at[m], fin_hbm.at[m], 4 + m)
     at.settle()
     for copy in written:
         copy.wait()
@@ -1003,16 +1072,16 @@
             dma((peers,)), dma((shards, wparts)), dma((shards,)), dma((shards,)),
             dma((2, MAJOR)), dma((MAJOR, minor - 1)), dma((shards, parts)),
             dma((shards,)), dma((shards, 2)),
-            dma((5,)), dma((shards,)), dma((shards,)), dma((4,)),
+            dma((5,)), dma((shards,)), dma((shards,)), dma((7,)),
             dma((peers,)), dma((shards,)),
             dma((3, 3)), dma((3, 3)),
             dma((3, 4)), dma((3, 4)),
             dma((3, minor - 1)), dma((3, minor - 1)),
             dma((3, MAJOR)), dma((3, MAJOR + 1)),
-            dma((parts,)), dma((parts,)),
-            dma((max(more, 1),)), dma((max(more, 1),)),
-            dma((minor - 1, MAJOR)), dma((minor - 1, MAJOR)),
-            dma((MAJOR,)), dma((MAJOR + 1,)),
+            dma((3, parts)), dma((3, parts)),
+            dma((max(more, 1), 3)), dma((max(more, 1), 3)),
+            dma((minor - 1, MAJOR + 1)), dma((minor - 1, MAJOR + 1)),
+            dma((MAJOR + 1,)), dma((MAJOR + 2,)),
             dma((halves,)), dma((halves,)),
             dma((1,)), dma((1,)),
             dma((peers,)), dma((shards,)),

time: 181 us -> 176 us (0.972)
  Pallas kernels: 180 us -> 174 us
    pallas_call x1, Pallas kernels: 175 us -> 169 us  [layer(): pl.pallas_call(functools.partial(layer_kernel, shards, replicas, wparts,...]
where the time goes in v6:
time: 176 us; the launch traced here: 175 us
  Pallas kernels  174 us (99%)
    pallas_call x1, Pallas kernels, layer(): pl.pallas_call(functools.partial(layer_kernel, shards, replicas, wparts,...  169 us
    pallas_call x1, Pallas kernels, finish(): pl.pallas_call(functools.partial(finish_kernel, slab, unit), grid=(steps,...  4.99 us

profile of v6, /device:TPU:0, one launch (start us, length us, event | category | flops | bytes accessed | tf_op | source)
XLA Modules:
  0.0 175.0 jit_solution(17947386302775024924)
XLA Ops:
  0.7 169.2 %layer.1 = (bf16[128,1280]{1,0:T(8,128)(2,1)}, bf16[3,160,1280]{2,1,0:T(8,128)(2,1)}, bf16[4,40,3840]{2,1,0:T(8,128)(2,1)}, f32[128,1280]{1,0:T(8,128)}, f32[8,384]{1,0:T(8,128)}) custom-call(bf16[128,1280]{1,0:T(8,128)(2,1)} %bitcast.6, s32[1,128]{1,0:T(1,128)} %segment_ref.1, s32[1,128]{1,0:T(1,128)} %position_ref.1, bf16[160]{0:T(256)(128)(2,1)} %gain_one_ref.1, ...), custom_call_target="tpu_custom_call" | custom-call | tf_op jit(solution)/shard_map/layer/pallas_call | solution.py:1013
  169.8 5.0 %finish.1 = (f32[160,1280]{1,0:T(8,128)}, f32[160,1280]{1,0:T(8,128)}, f32[160,1280]{1,0:T(8,128)}, f32[160,3840]{1,0:T(8,128)}, f32[128,1280]{1,0:T(8,128)}, /*...) custom-call(bf16[3,160,1280]{2,1,0:T(8,128)(2,1)} %get-tuple-element, ...), custom_call_target="tpu_custom_call" | custom-call | tf_op jit(solution)/shard_map/finish/pallas_call | solution.py:1136

commit v7 on v6

--- a/solution.py
+++ b/solution.py
@@ -1123,7 +1123,7 @@
 def finish(fin, gw, small, gin, out):
     slab, width = fin.shape[1:]
     block = gin.shape[0]
-    steps = 4 if slab % 32 == 0 else 2
+    steps = 2
     unit = HEAD * slab // width
     part, tokens = slab // steps, block // steps
     shape = jax.ShapeDtypeStruct

time: 176 us -> 175 us (level)
  no operation moved by 1% of the time
where the time goes in v7:
time: 175 us; the launch traced here: 174 us
  Pallas kernels  173 us (99%)
    pallas_call x1, Pallas kernels, layer(): pl.pallas_call(functools.partial(layer_kernel, shards, replicas, wparts,...  169 us
    pallas_call x1, Pallas kernels, finish(): pl.pallas_call(functools.partial(finish_kernel, slab, unit), grid=(steps,...  4.16 us

profile of v7, /device:TPU:0, one launch (start us, length us, event | category | flops | bytes accessed | tf_op | source)
XLA Modules:
  0.0 174.2 jit_solution(1506428228903016479)
XLA Ops:
  0.7 169.2 %layer.1 = (bf16[128,1280]{1,0:T(8,128)(2,1)}, bf16[3,160,1280]{2,1,0:T(8,128)(2,1)}, bf16[4,40,3840]{2,1,0:T(8,128)(2,1)}, f32[128,1280]{1,0:T(8,128)}, f32[8,384]{1,0:T(8,128)}) custom-call(bf16[128,1280]{1,0:T(8,128)(2,1)} %bitcast.6, s32[1,128]{1,0:T(1,128)} %segment_ref.1, s32[1,128]{1,0:T(1,128)} %position_ref.1, bf16[160]{0:T(256)(128)(2,1)} %gain_one_ref.1, ...), custom_call_target="tpu_custom_call" | custom-call | tf_op jit(solution)/shard_map/layer/pallas_call | solution.py:1013
  169.8 4.2 %finish.1 = (f32[160,1280]{1,0:T(8,128)}, f32[160,1280]{1,0:T(8,128)}, f32[160,1280]{1,0:T(8,128)}, f32[160,3840]{1,0:T(8,128)}, f32[128,1280]{1,0:T(8,128)}, /*...) custom-call(bf16[3,160,1280]{2,1,0:T(8,128)(2,1)} %get-tuple-element, ...), custom_call_target="tpu_custom_call" | custom-call | tf_op jit(solution)/shard_map/finish/pallas_call | solution.py:1136

commit v8 on v7

--- a/solution.py
+++ b/solution.py
@@ -772,6 +772,7 @@
     base = QUERY_BASE / math.sqrt(HEAD)
     factor = base * soft
     grads[...] = jnp.zeros_like(grads)
+    relay_rows(2)
     for da, db in peers:
         origin = at.at(-da, -db)
         at.arrived(dctx.at[:, lane(origin, block)], d_recv.at[origin])
@@ -800,10 +801,9 @@
             kv = slice(2 * slab + h * HEAD, 2 * slab + (h + 1) * HEAD)
             grads[kv, :reach] += dot(gctx, low, NT)
 
-    relay_rows(2)
-    attend(0)
     weight(2)
     weight_across(2)
+    attend(0)
     for i in range(1, length // qblock):
         attend(i)
 

time: 175 us -> 174 us (level)
  no operation moved by 1% of the time
where the time goes in v8:
time: 174 us
  Pallas kernels  173 us (99%)
    pallas_call x1, Pallas kernels, layer(): pl.pallas_call(functools.partial(layer_kernel, shards, replicas, wparts,...  169 us
    pallas_call x1, Pallas kernels, finish(): pl.pallas_call(functools.partial(finish_kernel, slab, unit), grid=(steps,...  4.16 us

profile of v8, /device:TPU:0, one launch (start us, length us, event | category | flops | bytes accessed | tf_op | source)
XLA Modules:
  0.0 174.1 jit_solution(14596274050840703519)
XLA Ops:
  0.7 169.1 %layer.1 = (bf16[128,1280]{1,0:T(8,128)(2,1)}, bf16[3,160,1280]{2,1,0:T(8,128)(2,1)}, bf16[4,40,3840]{2,1,0:T(8,128)(2,1)}, f32[128,1280]{1,0:T(8,128)}, f32[8,384]{1,0:T(8,128)}) custom-call(bf16[128,1280]{1,0:T(8,128)(2,1)} %bitcast.6, s32[1,128]{1,0:T(1,128)} %segment_ref.1, s32[1,128]{1,0:T(1,128)} %position_ref.1, bf16[160]{0:T(256)(128)(2,1)} %gain_one_ref.1, ...), custom_call_target="tpu_custom_call" | custom-call | tf_op jit(solution)/shard_map/layer/pallas_call | solution.py:1013
  169.8 4.2 %finish.1 = (f32[160,1280]{1,0:T(8,128)}, f32[160,1280]{1,0:T(8,128)}, f32[160,1280]{1,0:T(8,128)}, f32[160,3840]{1,0:T(8,128)}, f32[128,1280]{1,0:T(8,128)}, /*...) custom-call(bf16[3,160,1280]{2,1,0:T(8,128)(2,1)} %get-tuple-element, ...), custom_call_target="tpu_custom_call" | custom-call | tf_op jit(solution)/shard_map/finish/pallas_call | solution.py:1136
